TPU v7x, 32 devices: a whole 2x2x4 slice. The times are simulated.
32 devices in a mesh: pos: 8 (over z, y), fr: 4 (over x, core).
Axes of the slice: x: 2, y: 2, z: 4, core: 2. Of those that a mesh axis runs over, the one named last changes fastest.
Arguments:
- inputs: bfloat16 [8, 2048, 1024], P('pos', 'fr'), may hold values from -6 to 6
- delays: int32 [32, 8], P('fr', 'pos'), may hold values from 0 to 2
- query_weight: bfloat16 [8, 1024, 1024], P('pos', 'fr'), may hold values from -0.1875 to 0.1875
- key_weight: bfloat16 [8, 1024, 1024], P('pos', 'fr'), may hold values from -0.1875 to 0.1875
- value_weight: bfloat16 [8, 1024, 1024], P('pos', 'fr'), may hold values from -0.1875 to 0.1875
- out_weight: bfloat16 [8, 1024, 1024], P('pos', 'fr'), may hold values from -0.375 to 0.375
- gate_weight: bfloat16 [8, 1024, 2816], P('pos', 'fr'), may hold values from -0.1875 to 0.1875
- up_weight: bfloat16 [8, 1024, 2816], P('pos', 'fr'), may hold values from -0.1875 to 0.1875
- down_weight: bfloat16 [8, 2816, 1024], P('pos', 'fr'), may hold values from -0.109375 to 0.109375
- attention_gain: bfloat16 [8, 1024], P('pos', 'fr'), may hold values from 0.099609375 to 1.8984375
- feed_gain: bfloat16 [8, 1024], P('pos', 'fr'), may hold values from 0.099609375 to 1.8984375
- cotangent: bfloat16 [8, 2048, 1024], P('pos', 'fr'), may hold values from -6 to 6
Outputs:
- output: bfloat16 [8, 2048, 1024], P('pos', 'fr')
- input_grad: bfloat16 [8, 2048, 1024], P('pos', 'fr')
- query_weight_grad: float32 [8, 1024, 1024], P('pos', 'fr')
- key_weight_grad: float32 [8, 1024, 1024], P('pos', 'fr')
- value_weight_grad: float32 [8, 1024, 1024], P('pos', 'fr')
- out_weight_grad: float32 [8, 1024, 1024], P('pos', 'fr')
- gate_weight_grad: float32 [8, 1024, 2816], P('pos', 'fr')
- up_weight_grad: float32 [8, 1024, 2816], P('pos', 'fr')
- down_weight_grad: float32 [8, 2816, 1024], P('pos', 'fr')
- attention_gain_grad: float32 [8, 1024], P('pos', 'fr')
- feed_gain_grad: float32 [8, 1024], P('pos', 'fr')
All inputs are finite; a program needn't handle non-finite values.
Results may differ from a plain program's by a relative error of at most 0.02.
Values may be sent and summed in bfloat16 or wider, within the bound.
A program may use at most 256 MiB of HBM per device.

v0:
```python
import jax
import jax.numpy as jnp
from jax import lax
from jax.sharding import PartitionSpec as P

HEAD = 64


EPSILON = 1e-06
NEGATIVE = -1e30


def shifted(x, axis, by):
    peers = lax.axis_size(axis)
    pairs = [(i, i + by) for i in range(peers) if 0 <= i + by < peers]
    return lax.ppermute(x, axis, pairs)


def rms_scaling(values):
    return lax.rsqrt(jnp.mean(values * values, -1, keepdims=True) + EPSILON)


def product(operand, weight):
    return jnp.dot(operand, weight, preferred_element_type=jnp.float32)


def outer_sum(operand, second):
    return lax.dot_general(
        operand, second, (((0,), (0,)), ((), ())), preferred_element_type=jnp.float32
    )


def back_product(grad_rows, weight):
    return lax.dot_general(
        grad_rows, weight, (((1,), (1,)), ((), ())), preferred_element_type=jnp.float32
    )


def norm_back(values, scaling, gain_row, grad_normed):
    weighted = gain_row * grad_normed
    return scaling * weighted - values * scaling**3 * jnp.mean(weighted * values, -1, keepdims=True)


def project_in(hidden, weights):
    scaling = rms_scaling(hidden)
    normed = (hidden * scaling * weights[7].astype(jnp.float32)).astype(jnp.bfloat16)
    queries = product(normed, weights[0]).astype(jnp.bfloat16)
    key_rows = product(normed, weights[1]).astype(jnp.bfloat16)
    value_rows = product(normed, weights[2]).astype(jnp.bfloat16)
    return (scaling, normed, queries, key_rows, value_rows)


def attend(queries, keys_all, values_all, position, logsum):
    frames = queries.shape[0]
    head_count = queries.shape[1] // HEAD
    positions = keys_all.shape[0]
    query_heads = queries.reshape(frames, head_count, HEAD)
    key_heads = keys_all.reshape(positions, frames, head_count, HEAD)
    value_heads = values_all.reshape(positions, frames, head_count, HEAD)
    scores = jnp.einsum(
        "fhe,jfhe->fhj", query_heads, key_heads, preferred_element_type=jnp.float32
    ) * HEAD ** (-0.5)
    allowed = jnp.arange(positions) <= position
    scores = jnp.where(allowed, scores, NEGATIVE)
    if logsum is None:
        highest = jnp.max(scores, -1, keepdims=True)
        logsum = highest + jnp.log(jnp.sum(jnp.exp(scores - highest), -1, keepdims=True))
    soft_weights = jnp.exp(scores - logsum)
    soft_low = soft_weights.astype(jnp.bfloat16)
    attended = jnp.einsum(
        "fhj,jfhe->fhe", soft_low, value_heads, preferred_element_type=jnp.float32
    )
    attended = attended.astype(jnp.bfloat16).reshape(frames, -1)
    return (attended, logsum, soft_weights, soft_low)


def finish(hidden, attended, weights):
    branch = hidden + product(attended, weights[3])
    scaling_two = rms_scaling(branch)
    normed_two = (branch * scaling_two * weights[8].astype(jnp.float32)).astype(jnp.bfloat16)
    gate_act = product(normed_two, weights[4])
    up_act = product(normed_two, weights[5])
    inner_act = (jax.nn.silu(gate_act) * up_act).astype(jnp.bfloat16)
    return (branch, scaling_two, normed_two, gate_act, up_act, inner_act)


def on_device(
    inputs,
    delays,
    query_weight,
    key_weight,
    value_weight,
    out_weight,
    gate_weight,
    up_weight,
    down_weight,
    attention_gain,
    feed_gain,
    cotangent,
):
    position = lax.axis_index("pos")
    own_rows = inputs[0]
    frames = own_rows.shape[0]
    rim_rows = shifted(own_rows[frames - 2 :], "fr", 1)
    extended = jnp.concatenate([rim_rows, own_rows], 0)
    lag_rows = jnp.repeat(delays[:, 0], frames // delays.shape[0])[:, None]
    hidden = jnp.where(
        lag_rows == 0,
        extended[2:],
        jnp.where(lag_rows == 1, extended[1 : frames + 1], extended[:frames]),
    )
    hidden = hidden.astype(jnp.float32)
    gathered = (
        lax.all_gather(query_weight, "fr", axis=1, tiled=True),
        lax.all_gather(key_weight, "fr", axis=1, tiled=True),
        lax.all_gather(value_weight, "fr", axis=1, tiled=True),
        lax.all_gather(out_weight, "fr", axis=1, tiled=True),
        lax.all_gather(gate_weight, "fr", axis=1, tiled=True),
        lax.all_gather(up_weight, "fr", axis=1, tiled=True),
        lax.all_gather(down_weight, "fr", axis=1, tiled=True),
        lax.all_gather(attention_gain, "fr", axis=1, tiled=True),
        lax.all_gather(feed_gain, "fr", axis=1, tiled=True),
    )
    forward_weights = tuple((shard_piece[0] for shard_piece in gathered))
    scaling, normed, queries, key_rows, value_rows = project_in(hidden, forward_weights)
    keys_all, values_all = (
        lax.all_gather(key_rows[None], "pos", axis=0, tiled=True),
        lax.all_gather(value_rows[None], "pos", axis=0, tiled=True),
    )
    attended, logsum, soft_weights, soft_low = attend(queries, keys_all, values_all, position, None)
    branch, scaling_two, normed_two, gate_act, up_act, inner_act = finish(
        hidden, attended, forward_weights
    )
    output = (branch + product(inner_act, forward_weights[6])).astype(jnp.bfloat16)
    regathered = (
        lax.all_gather(query_weight, "fr", axis=1, tiled=True),
        lax.all_gather(key_weight, "fr", axis=1, tiled=True),
        lax.all_gather(value_weight, "fr", axis=1, tiled=True),
        lax.all_gather(out_weight, "fr", axis=1, tiled=True),
        lax.all_gather(gate_weight, "fr", axis=1, tiled=True),
        lax.all_gather(up_weight, "fr", axis=1, tiled=True),
        lax.all_gather(down_weight, "fr", axis=1, tiled=True),
        lax.all_gather(attention_gain, "fr", axis=1, tiled=True),
        lax.all_gather(feed_gain, "fr", axis=1, tiled=True),
    )
    backward_weights = tuple((shard_piece[0] for shard_piece in regathered))
    scaling, normed, queries, key_rows, value_rows = project_in(hidden, backward_weights)
    keys_all, values_all = (
        lax.all_gather(key_rows[None], "pos", axis=0, tiled=True),
        lax.all_gather(value_rows[None], "pos", axis=0, tiled=True),
    )
    attended, logsum, soft_weights, soft_low = attend(
        queries, keys_all, values_all, position, logsum
    )
    branch, scaling_two, normed_two, gate_act, up_act, inner_act = finish(
        hidden, attended, backward_weights
    )
    (
        query_full,
        key_full,
        value_full,
        out_full,
        gate_full,
        up_full,
        down_full,
        gain_one,
        gain_two,
    ) = backward_weights
    grad_out = cotangent[0]
    grad_inner = back_product(grad_out, down_full)
    sigmoid_gate = jax.nn.sigmoid(gate_act)
    grad_gate = (
        grad_inner * up_act * sigmoid_gate * (1.0 + gate_act * (1.0 - sigmoid_gate))
    ).astype(jnp.bfloat16)
    grad_up = (grad_inner * jax.nn.silu(gate_act)).astype(jnp.bfloat16)
    down_grad = outer_sum(inner_act, grad_out)
    gate_grad = outer_sum(normed_two, grad_gate)
    up_grad = outer_sum(normed_two, grad_up)
    grad_normed_two = back_product(grad_gate, gate_full) + back_product(grad_up, up_full)
    feed_gain_grad = jnp.sum(grad_normed_two * branch * scaling_two, 0)
    grad_branch = grad_out.astype(jnp.float32) + norm_back(
        branch, scaling_two, gain_two.astype(jnp.float32), grad_normed_two
    )
    grad_branch_low = grad_branch.astype(jnp.bfloat16)
    out_grad = outer_sum(attended, grad_branch_low)
    grad_attended = back_product(grad_branch_low, out_full).astype(jnp.bfloat16)
    head_count = queries.shape[1] // HEAD
    positions = keys_all.shape[0]
    grad_heads = grad_attended.reshape(frames, head_count, HEAD)
    query_heads = queries.reshape(frames, head_count, HEAD)
    key_heads = keys_all.reshape(positions, frames, head_count, HEAD)
    value_heads = values_all.reshape(positions, frames, head_count, HEAD)
    grad_soft = jnp.einsum(
        "fhe,jfhe->fhj", grad_heads, value_heads, preferred_element_type=jnp.float32
    )
    centre = jnp.sum(grad_soft * soft_weights, -1, keepdims=True)
    grad_scores = (soft_weights * (grad_soft - centre)).astype(jnp.bfloat16)
    grad_queries = jnp.einsum(
        "fhj,jfhe->fhe", grad_scores, key_heads, preferred_element_type=jnp.float32
    ) * HEAD ** (-0.5)
    grad_queries = grad_queries.astype(jnp.bfloat16).reshape(frames, -1)
    key_terms = jnp.einsum(
        "fhj,fhe->jfhe", grad_scores, query_heads, preferred_element_type=jnp.float32
    ) * HEAD ** (-0.5)
    value_terms = jnp.einsum(
        "fhj,fhe->jfhe", soft_low, grad_heads, preferred_element_type=jnp.float32
    )
    key_sum, value_sum = (
        lax.psum_scatter(
            key_terms.reshape(positions, frames, -1).astype(jnp.bfloat16),
            "pos",
            scatter_dimension=0,
            tiled=True,
        ).astype(jnp.float32),
        lax.psum_scatter(
            value_terms.reshape(positions, frames, -1).astype(jnp.bfloat16),
            "pos",
            scatter_dimension=0,
            tiled=True,
        ).astype(jnp.float32),
    )
    grad_keys = key_sum[0].astype(jnp.bfloat16)
    grad_values = value_sum[0].astype(jnp.bfloat16)
    query_grad = outer_sum(normed, grad_queries)
    key_grad = outer_sum(normed, grad_keys)
    value_grad = outer_sum(normed, grad_values)
    grad_normed = (
        back_product(grad_queries, query_full)
        + back_product(grad_keys, key_full)
        + back_product(grad_values, value_full)
    )
    attention_gain_grad = jnp.sum(grad_normed * hidden * scaling, 0)
    grad_hidden = grad_branch + norm_back(
        hidden, scaling, gain_one.astype(jnp.float32), grad_normed
    )
    grad_extended = jnp.pad(jnp.where(lag_rows == 0, grad_hidden, 0.0), ((2, 0), (0, 0)))
    grad_extended = grad_extended + jnp.pad(
        jnp.where(lag_rows == 1, grad_hidden, 0.0), ((1, 1), (0, 0))
    )
    grad_extended = grad_extended + jnp.pad(
        jnp.where(lag_rows == 2, grad_hidden, 0.0), ((0, 2), (0, 0))
    )
    rim_back = shifted(grad_extended[:2], "fr", -1)
    input_grad = (grad_extended[2:] + jnp.pad(rim_back, ((frames - 2, 0), (0, 0)))).astype(
        jnp.bfloat16
    )
    reduced = (
        lax.psum_scatter(
            query_grad[None].astype(jnp.bfloat16), "fr", scatter_dimension=1, tiled=True
        ).astype(jnp.float32),
        lax.psum_scatter(
            key_grad[None].astype(jnp.bfloat16), "fr", scatter_dimension=1, tiled=True
        ).astype(jnp.float32),
        lax.psum_scatter(
            value_grad[None].astype(jnp.bfloat16), "fr", scatter_dimension=1, tiled=True
        ).astype(jnp.float32),
        lax.psum_scatter(
            out_grad[None].astype(jnp.bfloat16), "fr", scatter_dimension=1, tiled=True
        ).astype(jnp.float32),
        lax.psum_scatter(
            gate_grad[None].astype(jnp.bfloat16), "fr", scatter_dimension=1, tiled=True
        ).astype(jnp.float32),
        lax.psum_scatter(
            up_grad[None].astype(jnp.bfloat16), "fr", scatter_dimension=1, tiled=True
        ).astype(jnp.float32),
        lax.psum_scatter(
            down_grad[None].astype(jnp.bfloat16), "fr", scatter_dimension=1, tiled=True
        ).astype(jnp.float32),
        lax.psum_scatter(
            attention_gain_grad[None].astype(jnp.bfloat16), "fr", scatter_dimension=1, tiled=True
        ).astype(jnp.float32),
        lax.psum_scatter(
            feed_gain_grad[None].astype(jnp.bfloat16), "fr", scatter_dimension=1, tiled=True
        ).astype(jnp.float32),
    )
    return (
        output[None],
        input_grad[None],
        reduced[0],
        reduced[1],
        reduced[2],
        reduced[3],
        reduced[4],
        reduced[5],
        reduced[6],
        reduced[7],
        reduced[8],
    )


def solution(mesh):
    return jax.shard_map(
        on_device,
        mesh=mesh,
        in_specs=(
            P("pos", "fr", None),
            P("fr", "pos"),
            P("pos", "fr", None),
            P("pos", "fr", None),
            P("pos", "fr", None),
            P("pos", "fr", None),
            P("pos", "fr", None),
            P("pos", "fr", None),
            P("pos", "fr", None),
            P("pos", "fr"),
            P("pos", "fr"),
            P("pos", "fr", None),
        ),
        out_specs=(
            P("pos", "fr", None),
            P("pos", "fr", None),
            P("pos", "fr", None),
            P("pos", "fr", None),
            P("pos", "fr", None),
            P("pos", "fr", None),
            P("pos", "fr", None),
            P("pos", "fr", None),
            P("pos", "fr", None),
            P("pos", "fr"),
            P("pos", "fr"),
        ),
        check_vma=False,
    )
```

profile of v0, /device:TPU:0, one launch (start us, length us, event | category | flops | bytes accessed | tf_op | source)
XLA Modules:
  0.0 1196.5 jit_solution(10028611180217504459)
XLA Ops:
  21.0 13.9 %all-gather.14.cloned.1.call-done = bf16[1,1024,1024]{2,1,0:T(8,128)(2,1)} async-done(((bf16[1,256,1024]{2,1,0:T(8,128)(2,1)}), bf16[1,1024,1024]{2,1,0:T(8,128)(2,1)}) %all-gather.14.cloned.1.call-update) | async-done | bytes 2097168 | tf_op jit(solution)/shard_map/all_gather | solution.py:115
  38.8 20.2 %all-gather.16.cloned.1.call-done = bf16[1,1024,1024]{2,1,0:T(8,128)(2,1)} async-done(((bf16[1,256,1024]{2,1,0:T(8,128)(2,1)}), bf16[1,1024,1024]{2,1,0:T(8,128)(2,1)}) %all-gather.16.cloned.1.call-update) | async-done | bytes 2097168 | tf_op jit(solution)/shard_map/all_gather | solution.py:116
  70.5 12.7 %all-gather.12.cloned.1.call-done = bf16[1,1024,1024]{2,1,0:T(8,128)(2,1)} async-done(((bf16[1,256,1024]{2,1,0:T(8,128)(2,1)}), bf16[1,1024,1024]{2,1,0:T(8,128)(2,1)}) %all-gather.12.cloned.1.call-update) | async-done | bytes 2097168 | tf_op jit(solution)/shard_map/all_gather | solution.py:114
  88.9 39.1 %all-gather.24.cloned.1.call-done = bf16[1,2816,1024]{2,1,0:T(8,128)(2,1)} async-done(((bf16[1,704,1024]{2,1,0:T(8,128)(2,1)}), bf16[1,2816,1024]{2,1,0:T(8,128)(2,1)}) %all-gather.24.cloned.1.call-update) | async-done | bytes 5767184 | tf_op jit(solution)/shard_map/all_gather | solution.py:120
  136.7 118.4 %all-gather.26.cloned.1.call-done = bf16[4096,1024]{1,0:T(8,128)(2,1)} async-done(((bf16[512,1024]{1,0:T(8,128)(2,1)}), bf16[4096,1024]{1,0:T(8,128)(2,1)}) %all-gather.26.cloned.1.call-update) | async-done | bytes 8388624 | tf_op jit(solution)/shard_map/all_gather | solution.py:127
  255.1 11.3 copy.36
  266.4 12.2 %copy.73 = bf16[128,8,8,512]{3,2,1,0:T(8,128)(2,1)} copy(bf16[128,8,8,512]{3,1,2,0:T(8,128)(2,1)} %bitcast.166) | data formatting | bytes 16777216
  278.6 101.7 %all-gather.28.cloned.1.call-done = bf16[4096,1024]{1,0:T(8,128)(2,1)} async-done(((bf16[512,1024]{1,0:T(8,128)(2,1)}), bf16[4096,1024]{1,0:T(8,128)(2,1)}) %all-gather.28.cloned.1.call-update) | async-done | bytes 8388624 | tf_op jit(solution)/shard_map/all_gather | solution.py:128
  380.3 11.6 copy.37
  391.9 12.2 %copy.74 = bf16[128,8,8,512]{3,2,1,0:T(8,128)(2,1)} copy(bf16[128,8,8,512]{3,1,2,0:T(8,128)(2,1)} %bitcast.167) | data formatting | bytes 16777216
  410.8 11.5 multiply_reduce_fusion.2
  426.9 20.8 %all-gather.22.cloned.1.call-done = bf16[1,1024,2816]{2,1,0:T(8,128)(2,1)} async-done(((bf16[1,256,2816]{2,1,0:T(8,128)(2,1)}), bf16[1,1024,2816]{2,1,0:T(8,128)(2,1)}) %all-gather.22.cloned.1.call-update) | async-done | bytes 5767184 | tf_op jit(solution)/shard_map/all_gather | solution.py:119
  456.3 36.3 %all-gather.20.cloned.1.call-done = bf16[1,1024,2816]{2,1,0:T(8,128)(2,1)} async-done(((bf16[1,256,2816]{2,1,0:T(8,128)(2,1)}), bf16[1,1024,2816]{2,1,0:T(8,128)(2,1)}) %all-gather.20.cloned.1.call-update) | async-done | bytes 5767184 | tf_op jit(solution)/shard_map/all_gather | solution.py:118
  492.6 11.7 multiply_convert_fusion.3
  595.3 90.8 %reduce-scatter.16.cloned.1.call-done = bf16[1,512,1024]{1,2,0:T(8,128)(2,1)} async-done(((bf16[8,512,1024]{1,2,0:T(8,128)(2,1)}), bf16[1,512,1024]{1,2,0:T(8,128)(2,1)}) %reduce-scatter.16.cloned.1.call-update) | async-done | bytes 1048592 | tf_op jit(solution)/shard_map/reduce_scatter | solution.py:209
  690.6 145.7 %reduce-scatter.18.cloned.1.call-done = bf16[1,512,1024]{1,2,0:T(8,128)(2,1)} async-done(((bf16[8,512,1024]{1,2,0:T(8,128)(2,1)}), bf16[1,512,1024]{1,2,0:T(8,128)(2,1)}) %reduce-scatter.18.cloned.1.call-update) | async-done | bytes 1048592 | tf_op jit(solution)/shard_map/reduce_scatter | solution.py:215
  861.6 30.6 %reduce-scatter.26.cloned.1.call-done = bf16[1,256,1024]{2,1,0:T(8,128)(2,1)} async-done(((bf16[1,1024,1024]{2,1,0:T(8,128)(2,1)}), bf16[1,256,1024]{2,1,0:T(8,128)(2,1)}) %reduce-scatter.26.cloned.1.call-update) | async-done | bytes 524304 | tf_op jit(solution)/shard_map/reduce_scatter | solution.py:257
  894.3 31.4 %reduce-scatter.20.cloned.1.call-done = bf16[1,256,1024]{2,1,0:T(8,128)(2,1)} async-done(((bf16[1,1024,1024]{2,1,0:T(8,128)(2,1)}), bf16[1,256,1024]{2,1,0:T(8,128)(2,1)}) %reduce-scatter.20.cloned.1.call-update) | async-done | bytes 524304 | tf_op jit(solution)/shard_map/reduce_scatter | solution.py:248
  927.8 55.0 %reduce-scatter.32.cloned.1.call-done = bf16[1,704,1024]{2,1,0:T(8,128)(2,1)} async-done(((bf16[1,2816,1024]{2,1,0:T(8,128)(2,1)}), bf16[1,704,1024]{2,1,0:T(8,128)(2,1)}) %reduce-scatter.32.cloned.1.call-update) | async-done | bytes 1441808 | tf_op jit(solution)/shard_map/reduce_scatter | solution.py:266
  986.2 53.8 %reduce-scatter.28.cloned.1.call-done = bf16[1,256,2816]{2,1,0:T(8,128)(2,1)} async-done(((bf16[1,1024,2816]{2,1,0:T(8,128)(2,1)}), bf16[1,256,2816]{2,1,0:T(8,128)(2,1)}) %reduce-scatter.28.cloned.1.call-update) | async-done | bytes 1441808 | tf_op jit(solution)/shard_map/reduce_scatter | solution.py:260
  1043.1 54.0 %reduce-scatter.30.cloned.1.call-done = bf16[1,256,2816]{2,1,0:T(8,128)(2,1)} async-done(((bf16[1,1024,2816]{2,1,0:T(8,128)(2,1)}), bf16[1,256,2816]{2,1,0:T(8,128)(2,1)}) %reduce-scatter.30.cloned.1.call-update) | async-done | bytes 1441808 | tf_op jit(solution)/shard_map/reduce_scatter | solution.py:263
  1103.8 16.4 %reduce-scatter.34.cloned.1.call-done = bf16[256,1]{1,0:T(8,128)(2,1)} async-done(((bf16[1024,1]{1,0:T(8,128)(2,1)}), bf16[256,1]{1,0:T(8,128)(2,1)}) %reduce-scatter.34.cloned.1.call-update) | async-done | bytes 528
  1122.9 31.0 %reduce-scatter.22.cloned.1.call-done = bf16[1,256,1024]{2,1,0:T(8,128)(2,1)} async-done(((bf16[1,1024,1024]{2,1,0:T(8,128)(2,1)}), bf16[1,256,1024]{2,1,0:T(8,128)(2,1)}) %reduce-scatter.22.cloned.1.call-update) | async-done | bytes 524304 | tf_op jit(solution)/shard_map/reduce_scatter | solution.py:251
  1156.0 31.4 %reduce-scatter.24.cloned.1.call-done = bf16[1,256,1024]{2,1,0:T(8,128)(2,1)} async-done(((bf16[1,1024,1024]{2,1,0:T(8,128)(2,1)}), bf16[1,256,1024]{2,1,0:T(8,128)(2,1)}) %reduce-scatter.24.cloned.1.call-update) | async-done | bytes 524304 | tf_op jit(solution)/shard_map/reduce_scatter | solution.py:254
  (176 shorter events, 207.7 us)
Async XLA Ops:
  7.2 27.7 %all-gather.14.cloned.1.call-start = ((), (), s32[]{:S(2)}) async-start(), calls=%async_computation.12 | async-start | bytes 2621440 | tf_op jit(solution)/shard_map/all_gather | solution.py:115
  7.9 51.1 %all-gather.16.cloned.1.call-start = ((), (), s32[]{:S(2)}) async-start(), calls=%async_computation.13 | async-start | bytes 2621440 | tf_op jit(solution)/shard_map/all_gather | solution.py:116
  8.7 74.5 %all-gather.12.cloned.1.call-start = ((), (), s32[]{:S(2)}) async-start(), calls=%async_computation.11 | async-start | bytes 2621440 | tf_op jit(solution)/shard_map/all_gather | solution.py:114
  9.4 118.6 %all-gather.24.cloned.1.call-start = ((), (), s32[]{:S(2)}) async-start(), calls=%async_computation.17 | async-start | bytes 7208960 | tf_op jit(solution)/shard_map/all_gather | solution.py:120
  10.0 245.1 %all-gather.26.cloned.1.call-start = ((), (), s32[]{:S(2)}) async-start(), calls=%async_computation.27 | async-start | bytes 9437184 | tf_op jit(solution)/shard_map/all_gather | solution.py:127
  10.1 9.1 collective-permute-start
  38.8 341.6 %all-gather.28.cloned.1.call-start = ((), (), s32[]{:S(2)}) async-start(), calls=%async_computation.28 | async-start | bytes 9437184 | tf_op jit(solution)/shard_map/all_gather | solution.py:128
  62.9 359.4 %all-gather.18.cloned.1.call-start = ((), (), s32[]{:S(2)}) async-start(), calls=%async_computation.14 | async-start | bytes 2621440 | tf_op jit(solution)/shard_map/all_gather | solution.py:117
  63.7 384.0 %all-gather.22.cloned.1.call-start = ((), (), s32[]{:S(2)}) async-start(), calls=%async_computation.16 | async-start | bytes 7208960 | tf_op jit(solution)/shard_map/all_gather | solution.py:119
  64.4 428.2 %all-gather.20.cloned.1.call-start = ((), (), s32[]{:S(2)}) async-start(), calls=%async_computation.15 | async-start | bytes 7208960 | tf_op jit(solution)/shard_map/all_gather | solution.py:118
  65.2 621.0 %reduce-scatter.16.cloned.1.call-start = ((), (), s32[]{:S(2)}) async-start(), calls=%async_computation.18 | async-start | bytes 9437184 | tf_op jit(solution)/shard_map/reduce_scatter | solution.py:209
  88.9 315.2 %copy-start = (f32[512,16,64]{0,2,1:T(8,128)}, f32[512,16,64]{0,2,1:T(8,128)S(1)}, u32[]{:S(2)}) copy-start(f32[512,16,64]{0,2,1:T(8,128)S(1)} %bitcast_convert_fusion.1) | copy-start | bytes 6291460
  538.5 297.9 %reduce-scatter.18.cloned.1.call-start = ((), (), s32[]{:S(2)}) async-start(), calls=%async_computation.19 | async-start | bytes 9437184 | tf_op jit(solution)/shard_map/reduce_scatter | solution.py:215
  547.8 312.3 %reduce-scatter.36.cloned.1.call-start = ((), (), s32[]{:S(2)}) async-start(), calls=%async_computation.30 | async-start | bytes 327680
  548.8 343.4 %reduce-scatter.26.cloned.1.call-start = ((), (), s32[]{:S(2)}) async-start(), calls=%async_computation.23 | async-start | bytes 2621440 | tf_op jit(solution)/shard_map/reduce_scatter | solution.py:257
  553.4 372.3 %reduce-scatter.20.cloned.1.call-start = ((), (), s32[]{:S(2)}) async-start(), calls=%async_computation.20 | async-start | bytes 2621440 | tf_op jit(solution)/shard_map/reduce_scatter | solution.py:248
  571.0 411.8 %reduce-scatter.32.cloned.1.call-start = ((), (), s32[]{:S(2)}) async-start(), calls=%async_computation.26 | async-start | bytes 7208960 | tf_op jit(solution)/shard_map/reduce_scatter | solution.py:266
  579.3 460.7 %reduce-scatter.28.cloned.1.call-start = ((), (), s32[]{:S(2)}) async-start(), calls=%async_computation.24 | async-start | bytes 7208960 | tf_op jit(solution)/shard_map/reduce_scatter | solution.py:260
  587.2 510.0 %reduce-scatter.30.cloned.1.call-start = ((), (), s32[]{:S(2)}) async-start(), calls=%async_computation.25 | async-start | bytes 7208960 | tf_op jit(solution)/shard_map/reduce_scatter | solution.py:263
  595.1 525.1 %reduce-scatter.34.cloned.1.call-start = ((), (), s32[]{:S(2)}) async-start(), calls=%async_computation.29 | async-start | bytes 327680
  843.9 309.9 %reduce-scatter.22.cloned.1.call-start = ((), (), s32[]{:S(2)}) async-start(), calls=%async_computation.21 | async-start | bytes 2621440 | tf_op jit(solution)/shard_map/reduce_scatter | solution.py:251
  848.1 339.3 %reduce-scatter.24.cloned.1.call-start = ((), (), s32[]{:S(2)}) async-start(), calls=%async_computation.22 | async-start | bytes 2621440 | tf_op jit(solution)/shard_map/reduce_scatter | solution.py:254
  1043.1 57.3 %copy-start.17 = (pred[512]{0:T(512)(128)(4,1)S(1)}, pred[512]{0:T(512)(128)(4,1)}, u32[]{:S(2)}) copy-start(pred[512]{0:T(512)(128)(4,1)} %copy-done.16) | copy-start | bytes 1540
  1101.5 20.1 %collective-permute-start.1 = (f32[2,1024]{1,0:T(2,128)S(1)}, f32[2,1024]{1,0:T(2,128)S(1)}, u32[]{:S(2)}, u32[]{:S(2)}) collective-permute-start(f32[2,1024]{1,0:T(2,128)S(1)} %pad_add_fusion.1), channel_id=1, source_target_pairs={{1,0},{2,1},{3,2},{5,4},{6,5},{7,6},{9,8},{10,9},{11,10},{13,12},{... | collective-permute-start | bytes 24584 | tf_op jit(solution)/shard_map/ppermute | solution.py:16
  (25 other events, 237.6 us)
Sparse Core Ops, SparseCore 0:
  9.6 25.2 all-gather.13
  36.4 22.5 all-gather.15
  60.6 22.5 all-gather.11
  84.6 43.3 all-gather.23
  130.6 124.4 all-gather.25
  257.6 122.6 all-gather.27
  381.9 20.7 all-gather.17
  404.2 43.3 all-gather.21
  449.2 43.3 all-gather.19
  538.6 147.4 reduce-scatter.15
  689.7 146.5 reduce-scatter.17
  839.2 19.1 reduce-scatter.35
  861.0 31.1 reduce-scatter.25
  894.5 31.1 reduce-scatter.19
  928.1 54.7 reduce-scatter.31
  985.2 54.7 reduce-scatter.27
  1042.4 54.7 reduce-scatter.29
  1100.0 20.0 reduce-scatter.33
  1122.6 31.1 reduce-scatter.21
  1156.2 31.1 reduce-scatter.23
where the time goes:
time: 1200 us
  waiting for transfers between devices  908 us (76%)
  matrix products  109 us (9%)
  other arithmetic  84.8 us (7%)
  local copies, waits for them, and re-layouts  62.3 us (5%)
  between operations  14.9 us (1%)
    reduce_scatter x1, waiting for transfers between devices, on_device(): lax.psum_scatter(value_terms.reshape(positions, frames, -1).astype(jnp.bf...  146 us
    all_gather x1, waiting for transfers between devices, on_device(): lax.all_gather(key_rows[None], 'pos', axis=0, tiled=True)  118 us
    all_gather x1, waiting for transfers between devices, on_device(): lax.all_gather(value_rows[None], 'pos', axis=0, tiled=True)  102 us
    reduce_scatter x1, waiting for transfers between devices, on_device(): lax.psum_scatter(key_terms.reshape(positions, frames, -1).astype(jnp.bflo...  90.8 us
    reduce_scatter x1, waiting for transfers between devices, on_device(): lax.psum_scatter(down_grad[None].astype(jnp.bfloat16), 'fr', scatter_dime...  55 us
    reduce_scatter x1, waiting for transfers between devices, on_device(): lax.psum_scatter(up_grad[None].astype(jnp.bfloat16), 'fr', scatter_dimens...  54 us
    reduce_scatter x1, waiting for transfers between devices, on_device(): lax.psum_scatter(gate_grad[None].astype(jnp.bfloat16), 'fr', scatter_dime...  53.8 us
    dot_general x7, matrix products, product(): return jnp.dot(operand, weight, preferred_element_type=jnp.float32)  41.9 us
  transfers between devices with their start and end apart: 22, of which 18 were waited for; matrix products, arithmetic and copies ran while one was open for 17% of the time, Pallas kernels for 0%

commit v1 on v0

v1 whole, which is shorter than its diff:
```python
import functools

import jax
import jax.numpy as jnp
from jax import lax
from jax.experimental import pallas as pl
from jax.experimental.pallas import tpu as pltpu
from jax.sharding import PartitionSpec as P

HEAD = 64
LANES = 128
EPSILON = 1e-06
MESH = pl.DeviceIdType.MESH
F32 = jnp.float32
BF16 = jnp.bfloat16
ANY = pl.BlockSpec(memory_space=pl.ANY)
VMEM = pl.BlockSpec(memory_space=pltpu.VMEM)
DMA = pltpu.SemaphoreType.DMA
VMEM_BYTES = 64 * 1024 * 1024 - 65536


def greet(n_fr, n_pos):
    fr = lax.axis_index("fr")
    pos = lax.axis_index("pos")
    barrier = pltpu.get_barrier_semaphore()
    for k in range(1, n_fr):
        pl.semaphore_signal(
            barrier, inc=1, device_id={"fr": lax.rem(fr + k, n_fr)}, device_id_type=MESH
        )
    for k in range(1, n_pos):
        pl.semaphore_signal(
            barrier, inc=1, device_id={"pos": lax.rem(pos + k, n_pos)}, device_id_type=MESH
        )
    pl.semaphore_wait(barrier, n_fr + n_pos - 2)


def send(src, dst, send_sem, recv_sem, **device):
    return pltpu.make_async_remote_copy(
        src_ref=src,
        dst_ref=dst,
        send_sem=send_sem,
        recv_sem=recv_sem,
        device_id=device,
        device_id_type=MESH,
    )


def rows_of(index, rows):
    return pl.ds(pl.multiple_of(index * rows, rows), rows)


def head_sums(shape, feature_dim):
    features = lax.broadcasted_iota(jnp.int32, shape, feature_dim)
    heads = lax.broadcasted_iota(jnp.int32, shape, 1 - feature_dim)
    return (features // HEAD == heads).astype(BF16)


def sum_heads(product, sums):
    high = product.astype(BF16)
    low = (product - high.astype(F32)).astype(BF16)
    return jnp.dot(high, sums, preferred_element_type=F32) + jnp.dot(
        low, sums, preferred_element_type=F32
    )


def column_tile(columns):
    return 256 if columns % 256 == 0 else LANES


def multiply(rows_ref, weight_ref, out_ref):
    tile = column_tile(weight_ref.shape[1])

    def step(at, carry):
        columns = pl.ds(pl.multiple_of(at * tile, tile), tile)
        out_ref[:, columns] = jnp.dot(
            rows_ref[...], weight_ref[:, columns], preferred_element_type=F32
        ).astype(out_ref.dtype)
        return carry

    lax.fori_loop(0, weight_ref.shape[1] // tile, step, 0)


def peer_of(pos, k, n_pos):
    return lax.rem(pos + k, n_pos)


def forward_kernel(n_fr, n_pos, *refs):
    (
        own_rows,
        lags,
        gains,
        w0,
        w1,
        w2,
        w3,
        w4,
        w5,
        w6,
        o0,
        o1,
        o2,
        o3,
        o4,
        o5,
        o6,
        hidden_out,
        normed_out,
        attended_out,
        queries_out,
        keys_out,
        values_out,
        gains_out,
        f0,
        f1,
        f2,
        f3,
        f4,
        f5,
        f6,
        rim,
        gain_slots,
        hidden,
        normed,
        proj,
        turned,
        mixed,
        attended,
        score_slots,
        total,
        sums,
        spread,
        far_send,
        far_recv,
        near_send,
        near_recv,
        own_sem,
        out_sem,
        rim_sem,
        gain_send,
        gain_recv,
        turn_send,
        turn_recv,
        back_send,
        back_recv,
        act_sem,
    ) = refs
    shards = (w0, w1, w2, w3, w4, w5, w6)
    full_out = (o0, o1, o2, o3, o4, o5, o6)
    full = (f0, f1, f2, f3, f4, f5, f6)
    turned_out = (queries_out, keys_out, values_out)
    fr = lax.axis_index("fr")
    pos = lax.axis_index("pos")
    chips = n_fr // 2
    chip = fr // 2
    core = lax.rem(fr, 2)
    partner = chip * 2 + 1 - core
    frames, features = own_rows.shape
    part = frames // n_pos
    greet(n_fr, n_pos)

    edge = own_rows.shape[0] - rim.shape[0]
    rim_copy = send(
        own_rows.at[pl.ds(edge, rim.shape[0])],
        rim,
        rim_sem.at[0],
        rim_sem.at[1],
        fr=lax.rem(fr + 1, n_fr),
    )
    rim_copy.start()
    gain_copies = []
    for k in range(1, n_fr):
        copy = send(
            gains,
            gain_slots.at[fr],
            gain_send.at[k],
            gain_recv.at[k],
            fr=lax.rem(fr + k, n_fr),
        )
        copy.start()
        gain_copies.append(copy)
    far = {}
    near = {}
    own = {}
    for at, (shard, whole) in enumerate(zip(shards, full)):
        rows = shard.shape[0]
        for k in range(1, chips):
            there = lax.rem(chip + k, chips) * 2 + core
            far[at, k] = send(
                shard, whole.at[rows_of(fr, rows)], far_send.at[at, k], far_recv.at[at, k], fr=there
            )
            far[at, k].start()
        near[at, 0] = send(
            shard, whole.at[rows_of(fr, rows)], near_send.at[at, 0], near_recv.at[at, 0], fr=partner
        )
        near[at, 0].start()
        own[at] = pltpu.make_async_copy(shard, whole.at[rows_of(fr, rows)], own_sem.at[at])
        own[at].start()

    sums[...] = head_sums(sums.shape, 0)
    spread[...] = head_sums(spread.shape, 1)
    gain_slots[pl.ds(fr, 1)] = gains[...][None]
    for copy in gain_copies:
        copy.wait()
    gain_row = jnp.concatenate([gain_slots[at, 0:1, :] for at in range(n_fr)], 1)
    gains_out[...] = jnp.concatenate([gain_slots[at] for at in range(n_fr)], 1)
    rim_copy.wait()

    block = 64
    rim_rows = rim.shape[0]
    rim_all = jnp.where(fr == 0, 0.0, rim[...].astype(F32))[rim_rows - 8 :]

    def norm_block(at, carry):
        rows = pl.ds(pl.multiple_of(at * block, block), block)
        here = own_rows[rows, :].astype(F32)
        window = jnp.concatenate([carry, here], 0)
        once = pltpu.roll(window, 1, 0)[8:]
        twice = pltpu.roll(window, 2, 0)[8:]
        lag = lags[rows, :]
        values = jnp.where(lag == 0, here, jnp.where(lag == 1, once, twice))
        hidden[rows, :] = values.astype(BF16)
        scaling = lax.rsqrt(jnp.mean(values * values, -1, keepdims=True) + EPSILON)
        normed[rows, :] = (values * scaling * gain_row).astype(BF16)
        return here[block - 8 :]

    lax.fori_loop(0, frames // block, norm_block, rim_all)
    act_copies = [
        pltpu.make_async_copy(hidden, hidden_out, act_sem.at[0]),
        pltpu.make_async_copy(normed, normed_out, act_sem.at[1]),
    ]
    for copy in act_copies:
        copy.start()

    forwarded = {}
    outs = {}

    def pass_on(at):
        rows = shards[at].shape[0]
        for k in range(1, chips):
            far[at, k].wait_recv()
            origin = lax.rem(chip - k + chips, chips) * 2 + core
            near[at, k] = send(
                full[at].at[rows_of(origin, rows)],
                full[at].at[rows_of(origin, rows)],
                near_send.at[at, k],
                near_recv.at[at, k],
                fr=partner,
            )
            near[at, k].start()

    def complete(at):
        own[at].wait()
        for k in range(chips):
            near[at, k].wait_recv()
        outs[at] = pltpu.make_async_copy(full[at], full_out[at], out_sem.at[at])
        outs[at].start()

    def turn(which, k):
        peer = peer_of(pos, k, n_pos)
        return send(
            proj.at[which, rows_of(peer, part)],
            turned.at[which, pos],
            turn_send.at[which, k],
            turn_recv.at[which, k],
            pos=peer,
        )

    for which in range(3):
        pass_on(which)
        complete(which)
        multiply(normed, full[which], proj.at[which])

        def start_turn(k, carry):
            turn(which, k).start()
            return carry

        lax.fori_loop(1, n_pos, start_turn, 0)
        turned[which, pl.ds(pos, 1)] = proj[which, rows_of(pos, part), :][None]

    pass_on(3)
    pass_on(4)
    for which in range(3):

        def end_turn(k, carry):
            turn(which, k).wait()
            return carry

        lax.fori_loop(1, n_pos, end_turn, 0)
        copy = pltpu.make_async_copy(turned.at[which], turned_out[which], act_sem.at[2 + which])
        copy.start()
        act_copies.append(copy)

    def attend(at, carry):
        query = turned[0, at].astype(F32) * HEAD ** (-0.5)

        def score(j, highest):
            scores = sum_heads(query * turned[1, j].astype(F32), sums[...])
            score_slots[j] = scores
            return jnp.maximum(highest, scores)

        highest = lax.fori_loop(0, at + 1, score, jnp.full((part, LANES), -1e30, F32))

        def weigh(j, mass):
            return mass + jnp.exp(score_slots[j] - highest)

        mass = lax.fori_loop(0, at + 1, weigh, jnp.zeros((part, LANES), F32))
        logsum = highest + jnp.log(mass)
        total[...] = jnp.zeros_like(total)

        def mix(j, carry):
            soft_low = jnp.exp(score_slots[j] - logsum).astype(BF16)
            total[...] += jnp.dot(soft_low, spread[...], preferred_element_type=F32) * turned[
                2, j
            ].astype(F32)
            return carry

        lax.fori_loop(0, at + 1, mix, 0)
        mixed[at] = total[...].astype(BF16)

        @pl.when(at != pos)
        def _():
            send(
                mixed.at[at],
                attended.at[rows_of(pos, part)],
                back_send.at[at],
                back_recv.at[pos],
                pos=at,
            ).start()

        return carry

    lax.fori_loop(0, n_pos, attend, 0)
    attended[rows_of(pos, part), :] = mixed[pos]

    complete(3)
    complete(4)
    for at in (5, 6):
        pass_on(at)
        complete(at)

    def end_back(k, carry):
        peer = peer_of(pos, k, n_pos)
        send(
            mixed.at[peer],
            attended.at[rows_of(peer, part)],
            back_send.at[peer],
            back_recv.at[peer],
            pos=peer,
        ).wait()
        return carry

    lax.fori_loop(1, n_pos, end_back, 0)
    copy = pltpu.make_async_copy(attended, attended_out, act_sem.at[5])
    copy.start()
    act_copies.append(copy)
    for copy in far.values():
        copy.wait_send()
    for copy in near.values():
        copy.wait_send()
    for copy in outs.values():
        copy.wait()
    for copy in act_copies:
        copy.wait()


def forward_call(n_fr, n_pos, own_rows, lags, gains, shards):
    frames, features = own_rows.shape
    part = frames // n_pos
    count = len(shards)
    chips = n_fr // 2
    full = [(n_fr * shard.shape[0], shard.shape[1]) for shard in shards]
    act = jax.ShapeDtypeStruct((frames, features), BF16)
    turned = jax.ShapeDtypeStruct((n_pos, part, features), BF16)
    return pl.pallas_call(
        functools.partial(forward_kernel, n_fr, n_pos),
        name="forward",
        out_shape=[jax.ShapeDtypeStruct(shape, BF16) for shape in full]
        + [act, act, act, turned, turned, turned, jax.ShapeDtypeStruct((8, features), F32)],
        in_specs=[VMEM, VMEM, VMEM] + [ANY] * count,
        out_specs=[ANY] * (count + 6) + [VMEM],
        scratch_shapes=[pltpu.VMEM(shape, BF16) for shape in full]
        + [
            pltpu.VMEM((16, features), BF16),
            pltpu.VMEM((n_fr, *gains.shape), F32),
            pltpu.VMEM((frames, features), BF16),
            pltpu.VMEM((frames, features), BF16),
            pltpu.VMEM((3, frames, features), BF16),
            pltpu.VMEM((3, n_pos, part, features), BF16),
            pltpu.VMEM((n_pos, part, features), BF16),
            pltpu.VMEM((frames, features), BF16),
            pltpu.VMEM((n_pos, part, LANES), F32),
            pltpu.VMEM((part, features), F32),
            pltpu.VMEM((features, LANES), BF16),
            pltpu.VMEM((LANES, features), BF16),
            DMA((count, chips)),
            DMA((count, chips)),
            DMA((count, chips)),
            DMA((count, chips)),
            DMA((count,)),
            DMA((count,)),
            DMA((2,)),
            DMA((n_fr,)),
            DMA((n_fr,)),
            DMA((3, n_pos)),
            DMA((3, n_pos)),
            DMA((n_pos,)),
            DMA((n_pos,)),
            DMA((6,)),
        ],
        compiler_params=pltpu.CompilerParams(
            collective_id=0, has_side_effects=True, vmem_limit_bytes=VMEM_BYTES
        ),
    )(own_rows, lags, gains, *shards)


def rms_scaling(values):
    return lax.rsqrt(jnp.mean(values * values, -1, keepdims=True) + EPSILON)


def product(operand, weight):
    return jnp.dot(operand, weight, preferred_element_type=F32)


def outer_sum(operand, second):
    return lax.dot_general(operand, second, (((0,), (0,)), ((), ())), preferred_element_type=F32)


def back_product(grad_rows, weight):
    return lax.dot_general(grad_rows, weight, (((1,), (1,)), ((), ())), preferred_element_type=F32)


def norm_back(values, scaling, gain_row, grad_normed):
    weighted = gain_row * grad_normed
    return scaling * weighted - values * scaling**3 * jnp.mean(weighted * values, -1, keepdims=True)


def scatter_sum(grad):
    return lax.psum_scatter(
        grad[None].astype(BF16), "fr", scatter_dimension=1, tiled=True
    ).astype(F32)


def on_device(
    inputs,
    delays,
    query_weight,
    key_weight,
    value_weight,
    out_weight,
    gate_weight,
    up_weight,
    down_weight,
    attention_gain,
    feed_gain,
    cotangent,
):
    n_fr = lax.axis_size("fr")
    n_pos = lax.axis_size("pos")
    own_rows = inputs[0]
    frames, features = own_rows.shape
    part = frames // n_pos
    lags = jnp.repeat(delays[:, 0], frames // delays.shape[0])[:, None]
    gains = jnp.pad(jnp.concatenate([attention_gain, feed_gain], 0).astype(F32), ((0, 6), (0, 0)))
    shards = [
        weight[0]
        for weight in (
            query_weight,
            key_weight,
            value_weight,
            out_weight,
            gate_weight,
            up_weight,
            down_weight,
        )
    ]
    (
        query_full,
        key_full,
        value_full,
        out_full,
        gate_full,
        up_full,
        down_full,
        hidden,
        normed,
        attended,
        queries,
        keys,
        values,
        gain_rows,
    ) = forward_call(n_fr, n_pos, own_rows, lags, gains, shards)
    gain_one, gain_two = gain_rows[0:1], gain_rows[1:2]
    hidden = hidden.astype(F32)
    scaling = rms_scaling(hidden)
    branch = hidden + product(attended, out_full)
    scaling_two = rms_scaling(branch)
    normed_two = (branch * scaling_two * gain_two).astype(BF16)
    gate_act = product(normed_two, gate_full)
    up_act = product(normed_two, up_full)
    inner_act = (jax.nn.silu(gate_act) * up_act).astype(BF16)
    output = (branch + product(inner_act, down_full)).astype(BF16)
    grad_out = cotangent[0]
    grad_inner = back_product(grad_out, down_full)
    sigmoid_gate = jax.nn.sigmoid(gate_act)
    grad_gate = (
        grad_inner * up_act * sigmoid_gate * (1.0 + gate_act * (1.0 - sigmoid_gate))
    ).astype(BF16)
    grad_up = (grad_inner * jax.nn.silu(gate_act)).astype(BF16)
    down_grad = outer_sum(inner_act, grad_out)
    gate_grad = outer_sum(normed_two, grad_gate)
    up_grad = outer_sum(normed_two, grad_up)
    grad_normed_two = back_product(grad_gate, gate_full) + back_product(grad_up, up_full)
    feed_gain_grad = jnp.sum(grad_normed_two * branch * scaling_two, 0)
    grad_branch = grad_out.astype(F32) + norm_back(branch, scaling_two, gain_two, grad_normed_two)
    grad_branch_low = grad_branch.astype(BF16)
    out_grad = outer_sum(attended, grad_branch_low)
    grad_attended = back_product(grad_branch_low, out_full).astype(BF16)

    def turn(rows):
        return lax.all_to_all(rows.reshape(n_pos, part, features), "pos", 0, 0, tiled=True)

    heads = features // HEAD
    split = (n_pos, part, heads, HEAD)
    query_heads = queries.reshape(split)
    key_heads = keys.reshape(split)
    value_heads = values.reshape(split)
    grad_heads = turn(grad_attended).reshape(split)
    scores = jnp.einsum("pfhe,jfhe->pfhj", query_heads, key_heads, preferred_element_type=F32)
    scores = scores * HEAD ** (-0.5)
    index = jnp.arange(n_pos)
    allowed = (index[None, :] <= index[:, None])[:, None, None, :]
    soft = jax.nn.softmax(jnp.where(allowed, scores, -1e30), -1)
    soft_low = soft.astype(BF16)
    grad_soft = jnp.einsum("pfhe,jfhe->pfhj", grad_heads, value_heads, preferred_element_type=F32)
    centre = jnp.sum(grad_soft * soft, -1, keepdims=True)
    grad_scores = (soft * (grad_soft - centre)).astype(BF16)
    grad_queries = (
        jnp.einsum("pfhj,jfhe->pfhe", grad_scores, key_heads, preferred_element_type=F32)
        * HEAD ** (-0.5)
    )
    grad_keys = (
        jnp.einsum("pfhj,pfhe->jfhe", grad_scores, query_heads, preferred_element_type=F32)
        * HEAD ** (-0.5)
    )
    grad_values = jnp.einsum(
        "pfhj,pfhe->jfhe", soft_low, grad_heads, preferred_element_type=F32
    )
    grad_queries, grad_keys, grad_values = (
        turn(grad.astype(BF16).reshape(n_pos, part, features)).reshape(frames, features)
        for grad in (grad_queries, grad_keys, grad_values)
    )
    query_grad = outer_sum(normed, grad_queries)
    key_grad = outer_sum(normed, grad_keys)
    value_grad = outer_sum(normed, grad_values)
    grad_normed = (
        back_product(grad_queries, query_full)
        + back_product(grad_keys, key_full)
        + back_product(grad_values, value_full)
    )
    attention_gain_grad = jnp.sum(grad_normed * hidden * scaling, 0)
    grad_hidden = grad_branch + norm_back(hidden, scaling, gain_one, grad_normed)
    grad_extended = jnp.pad(jnp.where(lags == 0, grad_hidden, 0.0), ((2, 0), (0, 0)))
    grad_extended = grad_extended + jnp.pad(jnp.where(lags == 1, grad_hidden, 0.0), ((1, 1), (0, 0)))
    grad_extended = grad_extended + jnp.pad(jnp.where(lags == 2, grad_hidden, 0.0), ((0, 2), (0, 0)))
    rim_back = lax.ppermute(grad_extended[:2], "fr", [(i + 1, i) for i in range(n_fr - 1)])
    input_grad = (grad_extended[2:] + jnp.pad(rim_back, ((frames - 2, 0), (0, 0)))).astype(BF16)
    return (
        output[None],
        input_grad[None],
        scatter_sum(query_grad),
        scatter_sum(key_grad),
        scatter_sum(value_grad),
        scatter_sum(out_grad),
        scatter_sum(gate_grad),
        scatter_sum(up_grad),
        scatter_sum(down_grad),
        scatter_sum(attention_gain_grad),
        scatter_sum(feed_gain_grad),
    )


def solution(mesh):
    matrix = P("pos", "fr", None)
    vector = P("pos", "fr")
    return jax.shard_map(
        on_device,
        mesh=mesh,
        in_specs=(matrix, P("fr", "pos")) + (matrix,) * 7 + (vector, vector, matrix),
        out_specs=(matrix,) * 9 + (vector, vector),
        check_vma=False,
    )
```

time: 1200 us -> 693 us (0.58)
  waiting for transfers between devices: 908 us -> 315 us
  Pallas kernels: 0 us -> 154 us
  other arithmetic: 84.8 us -> 32.9 us
  local copies, waits for them, and re-layouts: 62.3 us -> 39.1 us
    all_gather x9 -> x0, waiting for transfers between devices: 363 us -> none  [the longest x1 118 us: on_device(): lax.all_gather(key_rows[None], 'pos', axis=0, tiled=True)]
    reduce_scatter x9 -> x7, waiting for transfers between devices: 524 us -> 252 us  [scatter_sum(): lax.psum_scatter(grad[None].astype(BF16), 'fr', scatter_dimension=1, tile...]
    pallas_call x0 -> x1, Pallas kernels: none -> 154 us  [forward_call(): pl.pallas_call(functools.partial(forward_kernel, n_fr, n_pos), name='forw...]
    all_to_all x0 -> x4, waiting for transfers between devices: none -> 62.6 us  [turn(): lax.all_to_all(rows.reshape(n_pos, part, features), 'pos', 0, 0, tiled=True)]
    unnamed x62 -> x64, local copies, waits for them, and re-layouts: 35.4 us -> 12.2 us
    all_gather x2 -> x0, local copies, waits for them, and re-layouts: 22.8 us -> none  [the longest x1 11.6 us: on_device(): lax.all_gather(value_rows[None], 'pos', axis=0, tiled=True)]
    reshape x0 -> x7, local copies, waits for them, and re-layouts: none -> 21.7 us  [the longest x3 8.64 us: on_device(): grad.astype(BF16).reshape(n_pos, part, features)]
    dot_general x2 -> x0, other arithmetic: 21.7 us -> none  [the longest x1 11.5 us: attend(): jnp.einsum('fhj,jfhe->fhe', soft_low, value_heads, preferred_element_type...]
  transfers between devices with their start and end apart: 22 -> 14, of which waited for: 18 -> 10; matrix products, arithmetic and copies ran while one was open for 17% -> 17% of each run, Pallas kernels for 0% -> 0%
where the time goes in v1:
time: 693 us; the launch traced here: 685 us
  waiting for transfers between devices  315 us (45%)
  Pallas kernels  154 us (22%)
  matrix products  111 us (16%)
  local copies, waits for them, and re-layouts  39.1 us (6%)
  other arithmetic  32.9 us (5%)
  starting transfers between devices  17.2 us (2%)
  between operations  14.6 us (2%)
    reduce_scatter x7, waiting for transfers between devices, scatter_sum(): lax.psum_scatter(grad[None].astype(BF16), 'fr', scatter_dimension=1, tile...  252 us
    pallas_call x1, Pallas kernels, forward_call(): pl.pallas_call(functools.partial(forward_kernel, n_fr, n_pos), name='forw...  154 us
    all_to_all x4, waiting for transfers between devices, turn(): lax.all_to_all(rows.reshape(n_pos, part, features), 'pos', 0, 0, tiled=True)  62.6 us
    dot_general x7, matrix products, back_product(): lax.dot_general(grad_rows, weight, (((1,), (1,)), ((), ())), preferred_el...  36.4 us
    dot_general x7, matrix products, outer_sum(): lax.dot_general(operand, second, (((0,), (0,)), ((), ())), preferred_elem...  33.4 us
    dot_general x4, matrix products, product(): return jnp.dot(operand, weight, preferred_element_type=F32)  21.2 us
    convert_element_type x9, other arithmetic, scatter_sum(): return lax.psum_scatter(grad[None].astype(BF16), 'fr', scatter_dimension=...  19.2 us
    all_to_all x4, starting transfers between devices, turn(): lax.all_to_all(rows.reshape(n_pos, part, features), 'pos', 0, 0, tiled=True)  15.3 us
  transfers between devices with their start and end apart: 14, of which 10 were waited for; matrix products, arithmetic and copies ran while one was open for 17% of the time, Pallas kernels for 0%

profile of v1, /device:TPU:0, one launch (start us, length us, event | category | flops | bytes accessed | tf_op | source)
XLA Modules:
  0.0 684.5 jit_solution(1555620786472704645)
XLA Ops:
  10.1 154.4 %forward.1 = (bf16[1024,1024]{1,0:T(8,128)(2,1)}, bf16[1024,1024]{1,0:T(8,128)(2,1)}, bf16[1024,1024]{1,0:T(8,128)(2,1)}, bf16[1024,1024]{1,0:T(8,128)(2,1)}, bf...) custom-call(bf16[512,1024]{1,0:T(8,128)(2,1)} %bitcast.134, ...), custom_call_target="tpu_custom_call" | custom-call | tf_op jit(solution)/shard_map/forward/pallas_call | solution.py:373
  169.4 4.9 fusion.57
  174.4 5.0 fusion.56
  179.4 10.0 %fusion.4 = (bf16[512,2816]{1,0:T(8,128)(2,1)S(1)}, bf16[512,2816]{1,0:T(8,128)(2,1)}, bf16[512,2816]{1,0:T(8,128)(2,1)}) fusion(f32[512,2816]{1,0:T(8,128)} %fusion.56, f32[512,2816]{1,0:T(8,128)} %fusion.57, bf16[2816,1024]{1,0:T(8,128)(2,1)S(1)} %bitcast.148, bf16[1,512,1024]{2,1,0:T(8,128)(2,1)S(1)} %copy-done.12), kind=kOutput, calls=%fused_computation.6 | convolution fusion | flops 2974416896 | bytes 27000832 | tf_op jit(solution)/shard_map/dot_general | solution.py:428
  189.4 6.0 fusion.58
  222.5 4.7 fusion.55
  227.2 7.1 %all-to-all-done = bf16[8,64,1024]{2,1,0:T(8,128)(2,1)S(1)} async-done(((bf16[8,64,1024]{2,1,0:T(8,128)(2,1)}), bf16[8,64,1024]{2,1,0:T(8,128)(2,1)S(1)}, u32[]{:S(2)}, u32[]{:S(2)}) %all-to-all-start) | async-done | bytes 1048608 | tf_op jit(solution)/shard_map/all_to_all | solution.py:519
  236.0 7.2 %fusion.6 = (f32[8,64,16]{0,2,1:T(8,128)S(1)}, f32[64,16,8,8]{3,2,1,0:T(8,128)S(1)}) fusion(f32[8,64,16,8]{0,3,2,1:T(8,128)} %get-tuple-element.63, f32[8,64,16]{0,2,1:T(8,128)} %get-tuple-element.62, bf16[8,64,16,64]{3,2,1,0:T(8,128)(2,1)S(1)} %reshape.161, bf16[8,64,16,64]{3,2,1,0:T(8,128)(2,1)} %reshape.159), kind=kOutput, calls=%fused_computation.15 | convolution fusion | flops 8577024 | bytes 2686976 | tf_op jit(solution)/shard_map/pfhe,jfhe->pfhj/dot_general | solution.py:533
  261.8 20.4 %all-to-all-done.2 = bf16[8,64,1024]{2,1,0:T(8,128)(2,1)S(1)} async-done(((bf16[8,64,1024]{2,1,0:T(8,128)(2,1)}), bf16[8,64,1024]{2,1,0:T(8,128)(2,1)S(1)}, u32[]{:S(2)}, u32[]{:S(2)}) %all-to-all-start.2) | async-done | bytes 1048608 | tf_op jit(solution)/shard_map/all_to_all | solution.py:519
  282.1 4.4 all-to-all-start.1
  293.3 18.8 %all-to-all-done.1 = bf16[8,64,1024]{2,1,0:T(8,128)(2,1)} async-done(((bf16[8,64,1024]{2,1,0:T(8,128)(2,1)}), bf16[8,64,1024]{2,1,0:T(8,128)(2,1)}, u32[]{:S(2)}, u32[]{:S(2)}) %all-to-all-start.1) | async-done | bytes 1048608 | tf_op jit(solution)/shard_map/all_to_all | solution.py:519
  317.0 4.4 fusion.60
  325.3 16.3 %all-to-all-done.3 = bf16[8,64,1024]{2,1,0:T(8,128)(2,1)S(1)} async-done(((bf16[8,64,1024]{2,1,0:T(8,128)(2,1)}), bf16[8,64,1024]{2,1,0:T(8,128)(2,1)S(1)}, u32[]{:S(2)}, u32[]{:S(2)}) %all-to-all-start.3) | async-done | bytes 1048608 | tf_op jit(solution)/shard_map/all_to_all | solution.py:519
  342.5 6.3 fusion.16
  366.9 6.8 convert_bitcast_fusion.2
  373.7 6.8 convert_bitcast_fusion.1
  381.8 6.9 %convert_bitcast_fusion = bf16[1,2816,1024]{2,1,0:T(8,128)(2,1)} fusion(bf16[512,2816]{1,0:T(8,128)(2,1)} %get-tuple-element.47, bf16[1,512,1024]{2,1,0:T(8,128)(2,1)S(1)} %copy-done.13), kind=kOutput, calls=%fused_computation.7 | convolution fusion | flops 2955673600 | bytes 9699328 | tf_op jit(solution)/shard_map/dot_general | solution.py:424
  390.3 7.6 %fusion.40 = bf16[1,512,1024]{2,1,0:T(8,128)(2,1)} fusion(f32[512,1024]{1,0:T(8,128)S(1)} %copy-done.4, bf16[512,2816]{1,0:T(8,128)(2,1)} %get-tuple-element.47, bf16[2816,1024]{1,0:T(8,128)(2,1)} %get-tuple-element.31), kind=kOutput, calls=%fused_computation.69 | convolution fusion | flops 2953838592 | bytes 11796480 | tf_op jit(solution)/shard_map/dot_general | solution.py:420
  409.6 25.9 %reduce-scatter.16.cloned.1.call-done = bf16[1,256,1024]{2,1,0:T(8,128)(2,1)} async-done(((bf16[1,1024,1024]{2,1,0:T(8,128)(2,1)}), bf16[1,256,1024]{2,1,0:T(8,128)(2,1)}) %reduce-scatter.16.cloned.1.call-update) | async-done | bytes 524304 | tf_op jit(solution)/shard_map/reduce_scatter | solution.py:437
  437.6 31.4 %reduce-scatter.14.cloned.1.call-done = bf16[1,256,1024]{2,1,0:T(8,128)(2,1)} async-done(((bf16[1,1024,1024]{2,1,0:T(8,128)(2,1)}), bf16[1,256,1024]{2,1,0:T(8,128)(2,1)}) %reduce-scatter.14.cloned.1.call-update) | async-done | bytes 524304 | tf_op jit(solution)/shard_map/reduce_scatter | solution.py:437
  471.2 31.4 %reduce-scatter.18.cloned.1.call-done = bf16[1,256,1024]{2,1,0:T(8,128)(2,1)} async-done(((bf16[1,1024,1024]{2,1,0:T(8,128)(2,1)}), bf16[1,256,1024]{2,1,0:T(8,128)(2,1)}) %reduce-scatter.18.cloned.1.call-update) | async-done | bytes 524304 | tf_op jit(solution)/shard_map/reduce_scatter | solution.py:437
  504.8 55.1 %reduce-scatter.22.cloned.1.call-done = bf16[1,256,2816]{2,1,0:T(8,128)(2,1)} async-done(((bf16[1,1024,2816]{2,1,0:T(8,128)(2,1)}), bf16[1,256,2816]{2,1,0:T(8,128)(2,1)}) %reduce-scatter.22.cloned.1.call-update) | async-done | bytes 1441808 | tf_op jit(solution)/shard_map/reduce_scatter | solution.py:437
  563.0 54.2 %reduce-scatter.24.cloned.1.call-done = bf16[1,256,2816]{2,1,0:T(8,128)(2,1)} async-done(((bf16[1,1024,2816]{2,1,0:T(8,128)(2,1)}), bf16[1,256,2816]{2,1,0:T(8,128)(2,1)}) %reduce-scatter.24.cloned.1.call-update) | async-done | bytes 1441808 | tf_op jit(solution)/shard_map/reduce_scatter | solution.py:437
  620.3 54.2 %reduce-scatter.26.cloned.1.call-done = bf16[1,704,1024]{2,1,0:T(8,128)(2,1)} async-done(((bf16[1,2816,1024]{2,1,0:T(8,128)(2,1)}), bf16[1,704,1024]{2,1,0:T(8,128)(2,1)}) %reduce-scatter.26.cloned.1.call-update) | async-done | bytes 1441808 | tf_op jit(solution)/shard_map/reduce_scatter | solution.py:437
  (149 shorter events, 119.7 us)
Async XLA Ops:
  168.2 30.8 %copy-start.3 = (f32[512,1024]{1,0:T(8,128)}, f32[512,1024]{1,0:T(8,128)S(1)}, u32[]{:S(2)}) copy-start(f32[512,1024]{1,0:T(8,128)S(1)} %get-tuple-element.60) | copy-start | bytes 6291460
  169.4 10.0 %slice-start = ((s8[5767168]{0:T(1024)(128)(4,1)}), s8[4194304]{0:T(1024)(128)(4,1)S(1)}, s32[]{:S(2)}) async-start(s8[5767168]{0:T(1024)(128)(4,1)} %bitcast.147), calls=%async_computation.22 | async-start | bytes 8388608
  203.2 31.0 %all-to-all-start = ((bf16[8,64,1024]{2,1,0:T(8,128)(2,1)}), bf16[8,64,1024]{2,1,0:T(8,128)(2,1)S(1)}, u32[]{:S(2)}, u32[]{:S(2)}) async-start(bf16[8,64,1024]{2,1,0:T(8,128)(2,1)} %bitcast.15), calls=%async_computation | async-start | bytes 2097152 | tf_op jit(solution)/shard_map/all_to_all | solution.py:519
  210.0 8.4 %copy-start = (bf16[8,64,16,64]{3,2,1,0:T(8,128)(2,1)}, bf16[8,64,16,64]{3,2,1,0:T(8,128)(2,1)S(1)}, u32[]{:S(2)}) copy-start(bf16[8,64,16,64]{3,2,1,0:T(8,128)(2,1)S(1)} %reshape.157) | copy-start | bytes 3145732
  236.0 7.2 %copy-start.10 = (bf16[8,64,16,64]{3,2,1,0:T(8,128)(2,1)}, bf16[8,64,16,64]{3,2,1,0:T(8,128)(2,1)S(1)}, u32[]{:S(2)}) copy-start(bf16[8,64,16,64]{3,2,1,0:T(8,128)(2,1)S(1)} %reshape.161) | copy-start | bytes 3145732
  236.0 7.2 %copy-start.9 = (f32[8,64,16,8]{0,3,2,1:T(8,128)S(1)}, f32[8,64,16,8]{0,3,2,1:T(8,128)}, u32[]{:S(2)}) copy-start(f32[8,64,16,8]{0,3,2,1:T(8,128)} %get-tuple-element.63) | copy-start | bytes 786436
  236.0 7.2 %copy-start.18 = (f32[8,64,16]{0,2,1:T(8,128)S(1)}, f32[8,64,16]{0,2,1:T(8,128)}, u32[]{:S(2)}) copy-start(f32[8,64,16]{0,2,1:T(8,128)} %get-tuple-element.62) | copy-start | bytes 98308
  252.3 29.8 %all-to-all-start.2 = ((bf16[8,64,1024]{2,1,0:T(8,128)(2,1)}), bf16[8,64,1024]{2,1,0:T(8,128)(2,1)S(1)}, u32[]{:S(2)}, u32[]{:S(2)}) async-start(bf16[8,64,1024]{2,1,0:T(8,128)(2,1)} %reshape.164), calls=%async_computation.2 | async-start | bytes 2097152 | tf_op jit(solution)/shard_map/all_to_all | solution.py:519
  261.8 24.8 %copy-start.11 = (bf16[8,64,16,64]{3,2,1,0:T(8,128)(2,1)S(1)}, bf16[8,64,16,64]{3,2,1,0:T(8,128)(2,1)}, u32[]{:S(2)}) copy-start(bf16[8,64,16,64]{3,2,1,0:T(8,128)(2,1)} %copy-done.10) | copy-start | bytes 3145732
  282.1 34.9 %copy-start.16 = (bf16[8,64,1024]{2,1,0:T(8,128)(2,1)}, bf16[8,64,1024]{2,1,0:T(8,128)(2,1)S(1)}, u32[]{:S(2)}) copy-start(bf16[8,64,1024]{2,1,0:T(8,128)(2,1)S(1)} %all-to-all-done.2) | copy-start | bytes 3145732
  282.1 30.0 %all-to-all-start.1 = ((bf16[8,64,1024]{2,1,0:T(8,128)(2,1)}), bf16[8,64,1024]{2,1,0:T(8,128)(2,1)}, u32[]{:S(2)}, u32[]{:S(2)}) async-start(bf16[8,64,1024]{2,1,0:T(8,128)(2,1)} %reshape.162), calls=%async_computation.1 | async-start | bytes 2097152 | tf_op jit(solution)/shard_map/all_to_all | solution.py:519
  293.3 23.4 %copy-start.2 = (bf16[512,1024]{1,0:T(8,128)(2,1)S(1)}, bf16[512,1024]{1,0:T(8,128)(2,1)}, u32[]{:S(2)}) copy-start(bf16[512,1024]{1,0:T(8,128)(2,1)} %get-tuple-element.25) | copy-start | bytes 3145732
  312.1 29.4 %all-to-all-start.3 = ((bf16[8,64,1024]{2,1,0:T(8,128)(2,1)}), bf16[8,64,1024]{2,1,0:T(8,128)(2,1)S(1)}, u32[]{:S(2)}, u32[]{:S(2)}) async-start(bf16[8,64,1024]{2,1,0:T(8,128)(2,1)} %reshape.166), calls=%async_computation.3 | async-start | bytes 2097152 | tf_op jit(solution)/shard_map/all_to_all | solution.py:519
  315.7 82.2 %reduce-scatter.30.cloned.1.call-start = ((), (), s32[]{:S(2)}) async-start(), calls=%async_computation.21 | async-start | bytes 327680
  316.7 88.1 %reduce-scatter.28.cloned.1.call-start = ((), (), s32[]{:S(2)}) async-start(), calls=%async_computation.20 | async-start | bytes 327680
  342.5 7.3 %copy-start.6 = (f32[512,1024]{1,0:T(8,128)S(1)}, f32[512,1024]{1,0:T(8,128)}, u32[]{:S(2)}) copy-start(f32[512,1024]{1,0:T(8,128)} %copy-done.5) | copy-start | bytes 6291460
  349.8 57.7 %reduce-scatter.20.cloned.1.call-start = ((), (), s32[]{:S(2)}) async-start(), calls=%async_computation.16 | async-start | bytes 2621440 | tf_op jit(solution)/shard_map/reduce_scatter | solution.py:437
  353.8 81.8 %reduce-scatter.16.cloned.1.call-start = ((), (), s32[]{:S(2)}) async-start(), calls=%async_computation.14 | async-start | bytes 2621440 | tf_op jit(solution)/shard_map/reduce_scatter | solution.py:437
  357.9 111.1 %reduce-scatter.14.cloned.1.call-start = ((), (), s32[]{:S(2)}) async-start(), calls=%async_computation.13 | async-start | bytes 2621440 | tf_op jit(solution)/shard_map/reduce_scatter | solution.py:437
  361.8 140.8 %reduce-scatter.18.cloned.1.call-start = ((), (), s32[]{:S(2)}) async-start(), calls=%async_computation.15 | async-start | bytes 2621440 | tf_op jit(solution)/shard_map/reduce_scatter | solution.py:437
  365.7 194.2 %reduce-scatter.22.cloned.1.call-start = ((), (), s32[]{:S(2)}) async-start(), calls=%async_computation.17 | async-start | bytes 7208960 | tf_op jit(solution)/shard_map/reduce_scatter | solution.py:437
  373.7 243.5 %reduce-scatter.24.cloned.1.call-start = ((), (), s32[]{:S(2)}) async-start(), calls=%async_computation.18 | async-start | bytes 7208960 | tf_op jit(solution)/shard_map/reduce_scatter | solution.py:437
  380.6 293.9 %reduce-scatter.26.cloned.1.call-start = ((), (), s32[]{:S(2)}) async-start(), calls=%async_computation.19 | async-start | bytes 7208960 | tf_op jit(solution)/shard_map/reduce_scatter | solution.py:437
  402.7 3.6 collective-permute-start
  (20 other events, 60.0 us)
Sparse Core Ops, SparseCore 0:
  319.5 20.4 reduce-scatter.29
  349.9 18.1 reduce-scatter.27
  370.6 31.1 reduce-scatter.19
  404.2 31.2 reduce-scatter.15
  437.9 31.1 reduce-scatter.13
  471.4 31.1 reduce-scatter.17
  505.2 54.6 reduce-scatter.21
  562.4 54.7 reduce-scatter.23
  619.7 54.7 reduce-scatter.25

commit v2 on v1

--- a/solution.py
+++ b/solution.py
@@ -109,6 +109,7 @@
         queries_out,
         keys_out,
         values_out,
+        soft_out,
         gains_out,
         f0,
         f1,
@@ -126,6 +127,7 @@
         mixed,
         attended,
         score_slots,
+        soft_slots,
         total,
         sums,
         spread,
@@ -307,7 +309,9 @@
         total[...] = jnp.zeros_like(total)
 
         def mix(j, carry):
-            soft_low = jnp.exp(score_slots[j] - logsum).astype(BF16)
+            soft = jnp.exp(score_slots[j] - logsum)
+            soft_slots[at, j] = soft
+            soft_low = soft.astype(BF16)
             total[...] += jnp.dot(soft_low, spread[...], preferred_element_type=F32) * turned[
                 2, j
             ].astype(F32)
@@ -329,6 +333,9 @@
         return carry
 
     lax.fori_loop(0, n_pos, attend, 0)
+    copy = pltpu.make_async_copy(soft_slots, soft_out, act_sem.at[6])
+    copy.start()
+    act_copies.append(copy)
     attended[rows_of(pos, part), :] = mixed[pos]
 
     complete(3)
@@ -374,9 +381,13 @@
         functools.partial(forward_kernel, n_fr, n_pos),
         name="forward",
         out_shape=[jax.ShapeDtypeStruct(shape, BF16) for shape in full]
-        + [act, act, act, turned, turned, turned, jax.ShapeDtypeStruct((8, features), F32)],
+        + [act, act, act, turned, turned, turned]
+        + [
+            jax.ShapeDtypeStruct((n_pos, n_pos, part, LANES), F32),
+            jax.ShapeDtypeStruct((8, features), F32),
+        ],
         in_specs=[VMEM, VMEM, VMEM] + [ANY] * count,
-        out_specs=[ANY] * (count + 6) + [VMEM],
+        out_specs=[ANY] * (count + 7) + [VMEM],
         scratch_shapes=[pltpu.VMEM(shape, BF16) for shape in full]
         + [
             pltpu.VMEM((16, features), BF16),
@@ -388,6 +399,7 @@
             pltpu.VMEM((n_pos, part, features), BF16),
             pltpu.VMEM((frames, features), BF16),
             pltpu.VMEM((n_pos, part, LANES), F32),
+            pltpu.VMEM((n_pos, n_pos, part, LANES), F32),
             pltpu.VMEM((part, features), F32),
             pltpu.VMEM((features, LANES), BF16),
             pltpu.VMEM((LANES, features), BF16),
@@ -404,7 +416,7 @@
             DMA((3, n_pos)),
             DMA((n_pos,)),
             DMA((n_pos,)),
-            DMA((6,)),
+            DMA((7,)),
         ],
         compiler_params=pltpu.CompilerParams(
             collective_id=0, has_side_effects=True, vmem_limit_bytes=VMEM_BYTES
@@ -420,23 +432,566 @@
     return jnp.dot(operand, weight, preferred_element_type=F32)
 
 
-def outer_sum(operand, second):
-    return lax.dot_general(operand, second, (((0,), (0,)), ((), ())), preferred_element_type=F32)
-
-
 def back_product(grad_rows, weight):
     return lax.dot_general(grad_rows, weight, (((1,), (1,)), ((), ())), preferred_element_type=F32)
 
 
-def norm_back(values, scaling, gain_row, grad_normed):
-    weighted = gain_row * grad_normed
-    return scaling * weighted - values * scaling**3 * jnp.mean(weighted * values, -1, keepdims=True)
-
-
-def scatter_sum(grad):
-    return lax.psum_scatter(
-        grad[None].astype(BF16), "fr", scatter_dimension=1, tiled=True
-    ).astype(F32)
+def sublane_sums(values):
+    rows, features = values.shape
+    return jnp.sum(values.reshape(rows // 8, 8, features), 0)
+
+
+def backward_kernel(n_fr, n_pos, shard_rows, *refs):
+    (
+        lags,
+        gain_rows,
+        inner_t,
+        cot,
+        gate_low,
+        up_low,
+        normed_two_t,
+        attended_t,
+        normed_t,
+        branch_in,
+        hidden_in,
+        queries,
+        keys,
+        values,
+        soft_in,
+        *weights,
+    ) = refs[:22]
+    kept_out = refs[22:29]
+    come_out = refs[29:36]
+    input_grad, gains_out = refs[36:38]
+    held = refs[38:45]
+    (
+        made,
+        down_slots,
+        gate_slots,
+        up_slots,
+        small,
+        inner_v,
+        cot_v,
+        gate_v,
+        up_v,
+        normed_two_v,
+        attended_v,
+        normed_v,
+        branch,
+        hidden,
+        total,
+        low_rows,
+        grad_rows,
+        turned,
+        soft,
+        soft_grads,
+        score_slots,
+        sum_rows,
+        leaving,
+        arrived,
+        sums,
+        spread,
+        gain_split,
+        gain_in,
+        rim_out,
+        rim_in,
+        load_sem,
+        stream_sem,
+        give_send,
+        take_recv,
+        far_send,
+        far_recv,
+        kept_sem,
+        turn_send,
+        turn_recv,
+        back_send,
+        back_recv,
+        gain_send,
+        gain_recv,
+        rim_sem,
+        out_sem,
+    ) = refs[45:]
+    query_w, key_w, value_w, out_w, gate_w, up_w, down_w = weights
+    fr = lax.axis_index("fr")
+    pos = lax.axis_index("pos")
+    chips = n_fr // 2
+    chip = fr // 2
+    core = lax.rem(fr, 2)
+    partner = chip * 2 + 1 - core
+    frames, features = cot.shape
+    part = frames // n_pos
+    tile = made.shape[-1]
+    greet(n_fr, n_pos)
+
+    loads = {}
+
+    def load(name, src, dst):
+        loads[name] = pltpu.make_async_copy(src, dst, load_sem.at[len(loads)])
+        loads[name].start()
+
+    def columns_of(t):
+        return pl.ds(pl.multiple_of(t * tile, tile), tile)
+
+    def feed_copies(t):
+        slot = lax.rem(t, 2)
+        return (
+            pltpu.make_async_copy(
+                down_w.at[columns_of(t)], down_slots.at[slot], stream_sem.at[slot, 0]
+            ),
+            pltpu.make_async_copy(
+                gate_w.at[:, columns_of(t)], gate_slots.at[slot], stream_sem.at[slot, 1]
+            ),
+            pltpu.make_async_copy(
+                up_w.at[:, columns_of(t)], up_slots.at[slot], stream_sem.at[slot, 2]
+            ),
+        )
+
+    load("inner", inner_t, inner_v)
+    load("cot", cot, cot_v)
+    for copy in feed_copies(0):
+        copy.start()
+    load("gate", gate_low, gate_v)
+    load("up", up_low, up_v)
+    load("branch", branch_in, branch)
+    load("out", out_w, small.at[0])
+    load("normed_two", normed_two_t, normed_two_v)
+    load("attended", attended_t, attended_v)
+    load("queries", queries, turned.at[0])
+    load("keys", keys, turned.at[1])
+    load("values", values, turned.at[2])
+    load("soft", soft_in, soft)
+    load("normed", normed_t, normed_v)
+    load("hidden", hidden_in, hidden)
+    load("value_w", value_w, small.at[1])
+    load("key_w", key_w, small.at[2])
+    sums[...] = head_sums(sums.shape, 0)
+    spread[...] = head_sums(spread.shape, 1)
+
+    pending = []
+    done = [0]
+
+    def settle():
+        while pending:
+            pending.pop(0)()
+
+    def reduce_weight(at, left_t, right):
+        rows = shard_rows[at]
+        tiles = right.shape[1] // tile
+        base = done[0]
+        done[0] += tiles
+        group = max(1, 1024 // rows)
+
+        def outgoing(t):
+            slot = lax.rem(t + base, 2)
+            return send(
+                made.at[slot, 1 - core, :, pl.ds(0, rows)],
+                held[at].at[t],
+                give_send.at[slot],
+                take_recv.at[at, t],
+                fr=partner,
+            )
+
+        def consume(t):
+            slot = lax.rem(t + base, 2)
+            outgoing(t).wait_recv()
+            for there in range(chips):
+                held[at][t, there] = (
+                    held[at][t, there].astype(F32) + made[slot, core, there, 0:rows].astype(F32)
+                ).astype(BF16)
+            pltpu.make_async_copy(
+                held[at].at[t, chip], kept_out[at].at[:, columns_of(t)], kept_sem.at[at]
+            ).start()
+            for k in range(1, chips):
+                there = lax.rem(chip + k, chips)
+                send(
+                    held[at].at[t, there],
+                    come_out[at].at[k - 1, :, columns_of(t)],
+                    far_send.at[at, k],
+                    far_recv.at[at, k],
+                    fr=there * 2 + core,
+                ).start()
+
+        def step(t, carry):
+            slot = lax.rem(t + base, 2)
+
+            @pl.when(t >= 2)
+            def _():
+                outgoing(t - 2).wait_send()
+
+            for first in range(0, n_fr, group):
+                last = min(first + group, n_fr)
+                grads = product(left_t[first * rows : last * rows], right[:, columns_of(t)])
+                for b in range(first, last):
+                    made[slot, b % 2, b // 2, 0:rows] = grads[
+                        (b - first) * rows : (b - first + 1) * rows
+                    ].astype(BF16)
+            outgoing(t).start()
+
+            @pl.when(t >= 1)
+            def _():
+                consume(t - 1)
+
+            return carry
+
+        settle()
+        lax.fori_loop(0, tiles, step, 0)
+
+        def finish():
+            consume(tiles - 1)
+            outgoing(tiles - 2).wait_send()
+            outgoing(tiles - 1).wait_send()
+
+        pending.append(finish)
+
+    loads["inner"].wait()
+    loads["cot"].wait()
+    reduce_weight(6, inner_v, cot_v)
+
+    loads["gate"].wait()
+    loads["up"].wait()
+    feed_tiles = gate_v.shape[1] // tile
+    total[...] = jnp.zeros_like(total)
+
+    def feed(t, carry):
+        slot = lax.rem(t, 2)
+
+        @pl.when(t + 1 < feed_tiles)
+        def _():
+            for copy in feed_copies(t + 1):
+                copy.start()
+
+        for copy in feed_copies(t):
+            copy.wait()
+        columns = columns_of(t)
+        grad_inner = back_product(cot_v[...], down_slots[slot])
+        gate = gate_v[:, columns].astype(F32)
+        sigmoid = jax.nn.sigmoid(gate)
+        scaled = grad_inner * sigmoid
+        gate_v[:, columns] = (
+            scaled * up_v[:, columns].astype(F32) * (1.0 + gate * (1.0 - sigmoid))
+        ).astype(BF16)
+        up_v[:, columns] = (scaled * gate).astype(BF16)
+        for at in range(features // tile):
+            rows = slice(at * tile, (at + 1) * tile)
+            total[:, rows] += back_product(
+                gate_v[:, columns], gate_slots[slot, rows, :]
+            ) + back_product(up_v[:, columns], up_slots[slot, rows, :])
+        return carry
+
+    lax.fori_loop(0, feed_tiles, feed, 0)
+    settle()
+
+    block = 64
+    blocks = frames // block
+    loads["branch"].wait()
+
+    def block_rows(at):
+        return pl.ds(pl.multiple_of(at * block, block), block)
+
+    def feed_norm(at, carry):
+        rows = block_rows(at)
+        here = branch[rows, :]
+        grads = total[rows, :]
+        scaling = rms_scaling(here)
+        weighted = gain_rows[1:2, :] * grads
+        back = scaling * weighted - here * scaling**3 * jnp.mean(weighted * here, -1, keepdims=True)
+        back = cot_v[rows, :].astype(F32) + back
+        branch[rows, :] = back
+        low_rows[rows, :] = back.astype(BF16)
+        return carry + sublane_sums(grads * here * scaling)
+
+    feed_gain = lax.fori_loop(0, blocks, feed_norm, jnp.zeros((8, features), F32))
+    feed_gain = jnp.sum(feed_gain, 0, keepdims=True)
+
+    loads["out"].wait()
+
+    def turn_back(t, carry):
+        columns = columns_of(t)
+        grad_rows[:, columns] = back_product(low_rows[...], small[0, columns, :]).astype(BF16)
+        return carry
+
+    lax.fori_loop(0, features // tile, turn_back, 0)
+
+    def turn(k):
+        peer = peer_of(pos, k, n_pos)
+        return send(
+            grad_rows.at[rows_of(peer, part)],
+            turned.at[3, pos],
+            turn_send.at[k],
+            turn_recv.at[k],
+            pos=peer,
+        )
+
+    def start_turn(k, carry):
+        turn(k).start()
+        return carry
+
+    lax.fori_loop(1, n_pos, start_turn, 0)
+    turned[3, pl.ds(pos, 1)] = grad_rows[rows_of(pos, part), :][None]
+    load("query_w", query_w, small.at[0])
+
+    loads["normed_two"].wait()
+    reduce_weight(4, normed_two_v, gate_v)
+    reduce_weight(5, normed_two_v, up_v)
+    loads["attended"].wait()
+    reduce_weight(3, attended_v, low_rows)
+
+    for name in ("queries", "keys", "values", "soft"):
+        loads[name].wait()
+
+    def end_turn(k, carry):
+        turn(k).wait()
+        return carry
+
+    lax.fori_loop(1, n_pos, end_turn, 0)
+    settle()
+
+    def give_back(which, j):
+        return send(
+            leaving.at[which, j],
+            arrived.at[which, rows_of(pos, part)],
+            back_send.at[which, j],
+            back_recv.at[which, pos],
+            pos=j,
+        )
+
+    def part_sum(which, j, low, high, weight_of, other, scale):
+        sum_rows[...] = jnp.zeros_like(sum_rows)
+
+        def add(at, carry):
+            sum_rows[...] += product(weight_of(at), spread[...]) * turned[other, at].astype(F32)
+            return carry
+
+        lax.fori_loop(low, high, add, 0)
+        leaving[which, j] = (sum_rows[...] * scale).astype(BF16)
+
+        @pl.when(j != pos)
+        def _():
+            give_back(which, j).start()
+
+        @pl.when(j == pos)
+        def _():
+            arrived[which, rows_of(pos, part), :] = leaving[which, j]
+
+    def value_part(k, carry):
+        j = peer_of(pos, k, n_pos)
+        part_sum(2, j, j, n_pos, lambda p: soft[p, j].astype(BF16), 3, 1.0)
+        return carry
+
+    lax.fori_loop(1, n_pos + 1, value_part, 0)
+
+    def score_part(p, carry):
+        grads = turned[3, p].astype(F32)
+
+        def score(j, centre):
+            scores = sum_heads(grads * turned[2, j].astype(F32), sums[...])
+            score_slots[j] = scores
+            return centre + scores * soft[p, j]
+
+        centre = lax.fori_loop(0, p + 1, score, jnp.zeros((part, LANES), F32))
+
+        def level(j, carry):
+            soft_grads[p, j] = (soft[p, j] * (score_slots[j] - centre)).astype(BF16)
+            return carry
+
+        return lax.fori_loop(0, p + 1, level, carry)
+
+    lax.fori_loop(0, n_pos, score_part, 0)
+
+    def key_part(k, carry):
+        j = peer_of(pos, k, n_pos)
+        part_sum(1, j, j, n_pos, lambda p: soft_grads[p, j], 0, HEAD ** (-0.5))
+        return carry
+
+    lax.fori_loop(1, n_pos + 1, key_part, 0)
+
+    def query_part(k, carry):
+        p = peer_of(pos, k, n_pos)
+        part_sum(0, p, 0, p + 1, lambda j: soft_grads[p, j], 1, HEAD ** (-0.5))
+        return carry
+
+    lax.fori_loop(1, n_pos + 1, query_part, 0)
+
+    loads["normed"].wait()
+    for which, slot, name in ((2, 1, "value_w"), (1, 2, "key_w"), (0, 0, "query_w")):
+
+        def end_back(k, carry):
+            peer = peer_of(pos, k, n_pos)
+            send(
+                leaving.at[which, peer],
+                arrived.at[which, rows_of(peer, part)],
+                back_send.at[which, peer],
+                back_recv.at[which, peer],
+                pos=peer,
+            ).wait()
+            return carry
+
+        lax.fori_loop(1, n_pos, end_back, 0)
+        reduce_weight(which, normed_v, arrived.at[which])
+        loads[name].wait()
+
+        def add_normed(t, carry):
+            columns = columns_of(t)
+            grads = back_product(arrived[which], small[slot, columns, :])
+            total[:, columns] = grads if which == 2 else total[:, columns] + grads
+            return carry
+
+        lax.fori_loop(0, features // tile, add_normed, 0)
+
+    loads["hidden"].wait()
+
+    def attention_norm(at, carry):
+        rows = block_rows(at)
+        here = hidden[rows, :].astype(F32)
+        grads = total[rows, :]
+        scaling = rms_scaling(here)
+        weighted = gain_rows[0:1, :] * grads
+        back = scaling * weighted - here * scaling**3 * jnp.mean(weighted * here, -1, keepdims=True)
+        branch[rows, :] = branch[rows, :] + back
+        return carry + sublane_sums(grads * here * scaling)
+
+    gain = lax.fori_loop(0, blocks, attention_norm, jnp.zeros((8, features), F32))
+    gain = jnp.sum(gain, 0, keepdims=True)
+
+    first_lags = lags[0:8, :]
+    once = jnp.where(first_lags == 1, branch[0:8, :], 0.0)
+    once = jnp.where(
+        lax.broadcasted_iota(jnp.int32, once.shape, 0) == 0, 0.0, pltpu.roll(once, 1, 0)
+    )
+    rim_out[...] = once + jnp.where(first_lags == 2, branch[0:8, :], 0.0)
+    rim_copy = send(
+        rim_out, rim_in, rim_sem.at[0], rim_sem.at[1], fr=lax.rem(fr + n_fr - 1, n_fr)
+    )
+    rim_copy.start()
+    gain_pair = jnp.concatenate([gain, feed_gain, jnp.zeros((6, features), F32)], 0)
+    width = features // n_fr
+    for b in range(n_fr):
+        gain_split[b] = gain_pair[:, b * width : (b + 1) * width]
+    gain_copies = []
+    for k in range(1, n_fr):
+        there = lax.rem(fr + k, n_fr)
+        copy = send(
+            gain_split.at[there], gain_in.at[fr], gain_send.at[k], gain_recv.at[k], fr=there
+        )
+        copy.start()
+        gain_copies.append(copy)
+    gain_in[pl.ds(fr, 1)] = gain_split[pl.ds(fr, 1)]
+    settle()
+
+    rim_copy.wait()
+    rim = jnp.where(fr == n_fr - 1, 0.0, rim_in[...])
+
+    def shift(at, carry):
+        after_one, after_two = carry
+        rows = block_rows(blocks - 1 - at)
+        grads = branch[rows, :]
+        lag = lags[rows, :]
+        one = jnp.where(lag == 1, grads, 0.0)
+        two = jnp.where(lag == 2, grads, 0.0)
+        moved = pltpu.roll(jnp.concatenate([one, after_one], 0), block + 7, 0)[:block]
+        moved = moved + pltpu.roll(jnp.concatenate([two, after_two], 0), block + 6, 0)[:block]
+        low_rows[rows, :] = (jnp.where(lag == 0, grads, 0.0) + moved).astype(BF16)
+        return one[:8], two[:8]
+
+    lax.fori_loop(0, blocks, shift, (jnp.zeros_like(rim), rim))
+    out_copy = pltpu.make_async_copy(low_rows, input_grad, out_sem.at[0])
+    out_copy.start()
+    for copy in gain_copies:
+        copy.wait()
+    gain_sum = gain_in[0]
+    for b in range(1, n_fr):
+        gain_sum = gain_sum + gain_in[b]
+    gains_out[...] = gain_sum
+
+    for at in range(7):
+        pltpu.make_async_copy(kept_out[at], kept_out[at], kept_sem.at[at]).wait()
+        for k in range(1, chips):
+            there = lax.rem(chip + k, chips)
+            send(
+                come_out[at].at[k - 1],
+                come_out[at].at[k - 1],
+                far_send.at[at, k],
+                far_recv.at[at, k],
+                fr=there * 2 + core,
+            ).wait()
+    out_copy.wait()
+
+
+def backward_call(n_fr, n_pos, shard_shapes, *operands):
+    cot = operands[3]
+    frames, features = cot.shape
+    part = frames // n_pos
+    chips = n_fr // 2
+    tile = column_tile(features)
+    count = len(shard_shapes)
+    shard_rows = [rows for rows, _ in shard_shapes]
+    hidden_units = operands[4].shape[1]
+    most = max(shard_rows)
+    return pl.pallas_call(
+        functools.partial(backward_kernel, n_fr, n_pos, shard_rows),
+        name="backward",
+        out_shape=[jax.ShapeDtypeStruct(shape, BF16) for shape in shard_shapes]
+        + [jax.ShapeDtypeStruct((chips - 1, *shape), BF16) for shape in shard_shapes]
+        + [
+            jax.ShapeDtypeStruct((frames, features), BF16),
+            jax.ShapeDtypeStruct((8, features // n_fr), F32),
+        ],
+        in_specs=[VMEM, VMEM] + [ANY] * (len(operands) - 2),
+        out_specs=[ANY] * (2 * count + 1) + [VMEM],
+        scratch_shapes=[
+            pltpu.VMEM((columns // tile, chips, rows, tile), BF16) for rows, columns in shard_shapes
+        ]
+        + [
+            pltpu.VMEM((2, 2, chips, most, tile), BF16),
+            pltpu.VMEM((2, tile, features), BF16),
+            pltpu.VMEM((2, features, tile), BF16),
+            pltpu.VMEM((2, features, tile), BF16),
+            pltpu.VMEM((3, features, features), BF16),
+            pltpu.VMEM((hidden_units, frames), BF16),
+            pltpu.VMEM((frames, features), BF16),
+            pltpu.VMEM((frames, hidden_units), BF16),
+            pltpu.VMEM((frames, hidden_units), BF16),
+            pltpu.VMEM((features, frames), BF16),
+            pltpu.VMEM((features, frames), BF16),
+            pltpu.VMEM((features, frames), BF16),
+            pltpu.VMEM((frames, features), F32),
+            pltpu.VMEM((frames, features), BF16),
+            pltpu.VMEM((frames, features), F32),
+            pltpu.VMEM((frames, features), BF16),
+            pltpu.VMEM((frames, features), BF16),
+            pltpu.VMEM((4, n_pos, part, features), BF16),
+            pltpu.VMEM((n_pos, n_pos, part, LANES), F32),
+            pltpu.VMEM((n_pos, n_pos, part, LANES), BF16),
+            pltpu.VMEM((n_pos, part, LANES), F32),
+            pltpu.VMEM((part, features), F32),
+            pltpu.VMEM((3, n_pos, part, features), BF16),
+            pltpu.VMEM((3, frames, features), BF16),
+            pltpu.VMEM((features, LANES), BF16),
+            pltpu.VMEM((LANES, features), BF16),
+            pltpu.VMEM((n_fr, 8, features // n_fr), F32),
+            pltpu.VMEM((n_fr, 8, features // n_fr), F32),
+            pltpu.VMEM((8, features), F32),
+            pltpu.VMEM((8, features), F32),
+            DMA((17,)),
+            DMA((2, 3)),
+            DMA((2,)),
+            DMA((count, max(columns for _, columns in shard_shapes) // tile)),
+            DMA((count, chips)),
+            DMA((count, chips)),
+            DMA((count,)),
+            DMA((n_pos,)),
+            DMA((n_pos,)),
+            DMA((3, n_pos)),
+            DMA((3, n_pos)),
+            DMA((n_fr,)),
+            DMA((n_fr,)),
+            DMA((2,)),
+            DMA((1,)),
+        ],
+        compiler_params=pltpu.CompilerParams(
+            collective_id=1, has_side_effects=True, vmem_limit_bytes=VMEM_BYTES
+        ),
+    )(*operands)
 
 
 def on_device(
@@ -457,7 +1012,6 @@
     n_pos = lax.axis_size("pos")
     own_rows = inputs[0]
     frames, features = own_rows.shape
-    part = frames // n_pos
     lags = jnp.repeat(delays[:, 0], frames // delays.shape[0])[:, None]
     gains = jnp.pad(jnp.concatenate([attention_gain, feed_gain], 0).astype(F32), ((0, 6), (0, 0)))
     shards = [
@@ -472,109 +1026,47 @@
             down_weight,
         )
     ]
-    (
-        query_full,
-        key_full,
-        value_full,
-        out_full,
-        gate_full,
-        up_full,
-        down_full,
-        hidden,
-        normed,
-        attended,
-        queries,
-        keys,
-        values,
-        gain_rows,
-    ) = forward_call(n_fr, n_pos, own_rows, lags, gains, shards)
-    gain_one, gain_two = gain_rows[0:1], gain_rows[1:2]
-    hidden = hidden.astype(F32)
-    scaling = rms_scaling(hidden)
-    branch = hidden + product(attended, out_full)
-    scaling_two = rms_scaling(branch)
-    normed_two = (branch * scaling_two * gain_two).astype(BF16)
+    *full, hidden, normed, attended, queries, keys, values, soft, gain_rows = forward_call(
+        n_fr, n_pos, own_rows, lags, gains, shards
+    )
+    out_full, gate_full, up_full, down_full = full[3:]
+    branch = hidden.astype(F32) + product(attended, out_full)
+    normed_two = (branch * rms_scaling(branch) * gain_rows[1:2]).astype(BF16)
     gate_act = product(normed_two, gate_full)
     up_act = product(normed_two, up_full)
     inner_act = (jax.nn.silu(gate_act) * up_act).astype(BF16)
     output = (branch + product(inner_act, down_full)).astype(BF16)
-    grad_out = cotangent[0]
-    grad_inner = back_product(grad_out, down_full)
-    sigmoid_gate = jax.nn.sigmoid(gate_act)
-    grad_gate = (
-        grad_inner * up_act * sigmoid_gate * (1.0 + gate_act * (1.0 - sigmoid_gate))
-    ).astype(BF16)
-    grad_up = (grad_inner * jax.nn.silu(gate_act)).astype(BF16)
-    down_grad = outer_sum(inner_act, grad_out)
-    gate_grad = outer_sum(normed_two, grad_gate)
-    up_grad = outer_sum(normed_two, grad_up)
-    grad_normed_two = back_product(grad_gate, gate_full) + back_product(grad_up, up_full)
-    feed_gain_grad = jnp.sum(grad_normed_two * branch * scaling_two, 0)
-    grad_branch = grad_out.astype(F32) + norm_back(branch, scaling_two, gain_two, grad_normed_two)
-    grad_branch_low = grad_branch.astype(BF16)
-    out_grad = outer_sum(attended, grad_branch_low)
-    grad_attended = back_product(grad_branch_low, out_full).astype(BF16)
-
-    def turn(rows):
-        return lax.all_to_all(rows.reshape(n_pos, part, features), "pos", 0, 0, tiled=True)
-
-    heads = features // HEAD
-    split = (n_pos, part, heads, HEAD)
-    query_heads = queries.reshape(split)
-    key_heads = keys.reshape(split)
-    value_heads = values.reshape(split)
-    grad_heads = turn(grad_attended).reshape(split)
-    scores = jnp.einsum("pfhe,jfhe->pfhj", query_heads, key_heads, preferred_element_type=F32)
-    scores = scores * HEAD ** (-0.5)
-    index = jnp.arange(n_pos)
-    allowed = (index[None, :] <= index[:, None])[:, None, None, :]
-    soft = jax.nn.softmax(jnp.where(allowed, scores, -1e30), -1)
-    soft_low = soft.astype(BF16)
-    grad_soft = jnp.einsum("pfhe,jfhe->pfhj", grad_heads, value_heads, preferred_element_type=F32)
-    centre = jnp.sum(grad_soft * soft, -1, keepdims=True)
-    grad_scores = (soft * (grad_soft - centre)).astype(BF16)
-    grad_queries = (
-        jnp.einsum("pfhj,jfhe->pfhe", grad_scores, key_heads, preferred_element_type=F32)
-        * HEAD ** (-0.5)
+    grads = backward_call(
+        n_fr,
+        n_pos,
+        [shard.shape for shard in shards],
+        lags,
+        gain_rows,
+        inner_act.T,
+        cotangent[0],
+        gate_act.astype(BF16),
+        up_act.astype(BF16),
+        normed_two.T,
+        attended.T,
+        normed.T,
+        branch,
+        hidden,
+        queries,
+        keys,
+        values,
+        soft,
+        *full,
     )
-    grad_keys = (
-        jnp.einsum("pfhj,pfhe->jfhe", grad_scores, query_heads, preferred_element_type=F32)
-        * HEAD ** (-0.5)
-    )
-    grad_values = jnp.einsum(
-        "pfhj,pfhe->jfhe", soft_low, grad_heads, preferred_element_type=F32
-    )
-    grad_queries, grad_keys, grad_values = (
-        turn(grad.astype(BF16).reshape(n_pos, part, features)).reshape(frames, features)
-        for grad in (grad_queries, grad_keys, grad_values)
-    )
-    query_grad = outer_sum(normed, grad_queries)
-    key_grad = outer_sum(normed, grad_keys)
-    value_grad = outer_sum(normed, grad_values)
-    grad_normed = (
-        back_product(grad_queries, query_full)
-        + back_product(grad_keys, key_full)
-        + back_product(grad_values, value_full)
-    )
-    attention_gain_grad = jnp.sum(grad_normed * hidden * scaling, 0)
-    grad_hidden = grad_branch + norm_back(hidden, scaling, gain_one, grad_normed)
-    grad_extended = jnp.pad(jnp.where(lags == 0, grad_hidden, 0.0), ((2, 0), (0, 0)))
-    grad_extended = grad_extended + jnp.pad(jnp.where(lags == 1, grad_hidden, 0.0), ((1, 1), (0, 0)))
-    grad_extended = grad_extended + jnp.pad(jnp.where(lags == 2, grad_hidden, 0.0), ((0, 2), (0, 0)))
-    rim_back = lax.ppermute(grad_extended[:2], "fr", [(i + 1, i) for i in range(n_fr - 1)])
-    input_grad = (grad_extended[2:] + jnp.pad(rim_back, ((frames - 2, 0), (0, 0)))).astype(BF16)
+    kept, come, (input_grad, gain_grads) = grads[:7], grads[7:14], grads[14:]
     return (
         output[None],
         input_grad[None],
-        scatter_sum(query_grad),
-        scatter_sum(key_grad),
-        scatter_sum(value_grad),
-        scatter_sum(out_grad),
-        scatter_sum(gate_grad),
-        scatter_sum(up_grad),
-        scatter_sum(down_grad),
-        scatter_sum(attention_gain_grad),
-        scatter_sum(feed_gain_grad),
+        *(
+            (own.astype(F32) + jnp.sum(others.astype(F32), 0))[None]
+            for own, others in zip(kept, come)
+        ),
+        gain_grads[0:1],
+        gain_grads[1:2],
     )
 
 

time: 693 us -> 373 us (0.54); the launches traced: 685 us -> 372 us
  waiting for transfers between devices: 315 us -> 0 us
  Pallas kernels: 154 us -> 306 us
  matrix products: 111 us -> 20.3 us
  starting transfers between devices: 17.2 us -> 0 us
  between operations: 14.6 us -> 0.82 us
  local copies, waits for them, and re-layouts: 39.1 us -> 25.5 us
  other arithmetic: 32.9 us -> 19.7 us
    reduce_scatter x7 -> x0, waiting for transfers between devices: 252 us -> none  [scatter_sum(): lax.psum_scatter(grad[None].astype(BF16), 'fr', scatter_dimension=1, tile...]
    pallas_call x0 -> x1, Pallas kernels: none -> 151 us  [backward_call(): pl.pallas_call(functools.partial(backward_kernel, n_fr, n_pos, shard_rows...]
    dot_general x19 -> x0, matrix products: 90.2 us -> none  [the longest x7 36.4 us: back_product(): lax.dot_general(grad_rows, weight, (((1,), (1,)), ((), ())), preferred_el...]
    all_to_all x4 -> x0, waiting for transfers between devices: 62.6 us -> none  [turn(): lax.all_to_all(rows.reshape(n_pos, part, features), 'pos', 0, 0, tiled=True)]
    reshape x7 -> x0, local copies, waits for them, and re-layouts: 21.7 us -> none  [the longest x3 8.64 us: on_device(): grad.astype(BF16).reshape(n_pos, part, features)]
    all_to_all x4 -> x0, starting transfers between devices: 15.3 us -> none  [turn(): lax.all_to_all(rows.reshape(n_pos, part, features), 'pos', 0, 0, tiled=True)]
    convert_element_type x11 -> x1, other arithmetic: 20.7 us -> 7.81 us  [on_device(): inner_act = (jax.nn.silu(gate_act) * up_act).astype(BF16)]
    dot_general x0 -> x2, local copies, waits for them, and re-layouts: none -> 12.6 us  [product(): return jnp.dot(operand, weight, preferred_element_type=F32)]
  transfers between devices with their start and end apart: 14 -> 0, of which waited for: 10 -> 0; matrix products, arithmetic and copies ran while one was open for 17% -> 0% of each run, Pallas kernels for 0% -> 0%
where the time goes in v2:
time: 373 us; the launch traced here: 372 us
  Pallas kernels  306 us (82%)
  local copies, waits for them, and re-layouts  25.5 us (7%)
  matrix products  20.3 us (5%)
  other arithmetic  19.7 us (5%)
    pallas_call x1, Pallas kernels, forward_call(): pl.pallas_call(functools.partial(forward_kernel, n_fr, n_pos), name='forw...  154 us
    pallas_call x1, Pallas kernels, backward_call(): pl.pallas_call(functools.partial(backward_kernel, n_fr, n_pos, shard_rows...  151 us
    dot_general x4, matrix products, product(): return jnp.dot(operand, weight, preferred_element_type=F32)  20.3 us
    dot_general x2, local copies, waits for them, and re-layouts, product(): return jnp.dot(operand, weight, preferred_element_type=F32)  12.6 us
    broadcast_in_dim x4, other arithmetic, on_device(): (own.astype(F32) + jnp.sum(others.astype(F32), 0))[None]  10.4 us
    convert_element_type x1, other arithmetic, on_device(): inner_act = (jax.nn.silu(gate_act) * up_act).astype(BF16)  7.81 us

profile of v2, /device:TPU:0, one launch (start us, length us, event | category | flops | bytes accessed | tf_op | source)
XLA Modules:
  0.0 372.0 jit_solution(16923482924495824169)
XLA Ops:
  0.6 0.7 broadcast_in_dim.31
  1.4 0.9 broadcast_in_dim_reshape.4.refs_1_.refs_0_
  2.3 1.3 fusion.16.refs_2_
  3.6 154.3 %forward.1 = (bf16[1024,1024]{1,0:T(8,128)(2,1)}, bf16[1024,1024]{1,0:T(8,128)(2,1)}, bf16[1024,1024]{1,0:T(8,128)(2,1)}, bf16[1024,1024]{1,0:T(8,128)(2,1)}, bf...) custom-call(bf16[512,1024]{1,0:T(8,128)(2,1)} %bitcast.88, ...), custom_call_target="tpu_custom_call" | custom-call | tf_op jit(solution)/shard_map/forward/pallas_call | solution.py:380
  157.9 3.7 multiply_reduce_fusion
  161.6 0.8 slice.9
  162.4 7.6 %fusion.20 = (bf16[512,2816]{1,0:T(8,128)(2,1)}, f32[512,2816]{1,0:T(8,128)S(1)}) fusion(bf16[1024,2816]{1,0:T(8,128)(2,1)} %get-tuple-element.47.refs_20_, f32[512,1024]{1,0:T(8,128)S(1)} %get-tuple-element.76.refs_9_, f32[1024]{0:T(1024)S(1)} %bitcast.93, f32[512]{0:T(512)S(1)} %add_rsqrt_fusion), kind=kOutput, calls=%fused_computation.37 | convolution fusion | flops 2955804672 | bytes 16521216 | tf_op jit(solution)/shard_map/dot_general | solution.py:432
  170.0 4.8 %fusion.19 = (bf16[512,2816]{1,0:T(8,128)(2,1)}, f32[512,2816]{1,0:T(8,128)S(1)}) fusion(bf16[1024,2816]{1,0:T(8,128)(2,1)S(1)} %bitcast.78, f32[512,1024]{1,0:T(8,128)S(1)} %get-tuple-element.76.refs_9_, f32[1024]{0:T(1024)S(1)} %bitcast.94, f32[512]{0:T(512)S(1)} %add_rsqrt_fusion), kind=kOutput, calls=%fused_computation.36 | convolution fusion | flops 2955804672 | bytes 16521216 | tf_op jit(solution)/shard_map/dot_general | solution.py:432
  174.8 2.4 copy-done.2
  177.3 4.2 %fusion.8 = bf16[1,512,1024]{2,1,0:T(8,128)(2,1)} fusion(f32[512,1024]{1,0:T(8,128)S(1)} %get-tuple-element.76.refs_9_, bf16[2816,1024]{1,0:T(8,128)(2,1)S(1)} %bitcast.80, f32[512,2816]{1,0:T(8,128)S(1)} %get-tuple-element.80, f32[512,2816]{1,0:T(8,128)S(1)} %get-tuple-element.78), kind=kOutput, calls=%fused_computation.19 | convolution fusion | flops 2962489344 | bytes 20447232 | tf_op jit(solution)/shard_map/dot_general | solution.py:432
  181.5 6.3 %copy.30 = f32[512,2816]{0,1:T(8,128)} copy(f32[512,2816]{1,0:T(8,128)} %copy-done.1) | data formatting | bytes 11534336 | tf_op jit(solution)/shard_map/dot_general | solution.py:432
  187.8 6.3 %copy.29 = f32[512,2816]{0,1:T(8,128)} copy(f32[512,2816]{1,0:T(8,128)} %copy-done.2) | data formatting | bytes 11534336 | tf_op jit(solution)/shard_map/dot_general | solution.py:432
  194.1 7.8 %fusion.refs_2_ = bf16[2816,512]{1,0:T(8,128)(2,1)} fusion(f32[512,2816]{0,1:T(8,128)} %copy.30, f32[512,2816]{0,1:T(8,128)} %copy.29), kind=kLoop, calls=%fused_computation.1 | loop fusion | flops 8650752 | bytes 14417920 | tf_op jit(solution)/shard_map/convert_element_type | solution.py:1037
  202.2 1.3 copy.34.refs_6_
  203.5 2.3 copy.31
  205.8 1.3 copy.32
  207.1 151.3 %backward.1 = (bf16[256,1024]{1,0:T(8,128)(2,1)}, bf16[256,1024]{1,0:T(8,128)(2,1)}, bf16[256,1024]{1,0:T(8,128)(2,1)}, bf16[256,1024]{1,0:T(8,128)(2,1)}, bf16[...) custom-call(s32[512,1]{1,0:T(8,128)} %broadcast_in_dim_reshape.4.ref, ...), custom_call_target="tpu_custom_call" | custom-call | tf_op jit(solution)/shard_map/backward/pallas_call | solution.py:930
  358.5 3.4 fusion.11
  361.9 1.7 fusion.9
  363.6 0.8 copy-done.6
  364.4 3.1 fusion.5
  367.5 2.2 fusion.4
  369.7 1.3 fusion.18
  371.0 1.0 copy.36
  (40 shorter events, 0.3 us)
Async XLA Ops:
  157.9 12.1 %slice-start = ((s8[5767168]{0:T(1024)(128)(4,1)}), s8[4194304]{0:T(1024)(128)(4,1)S(1)}, s32[]{:S(2)}) async-start(s8[5767168]{0:T(1024)(128)(4,1)} %bitcast.77), calls=%async_computation | async-start | bytes 8388608
  161.6 40.3 %copy-start = (f32[512,1024]{1,0:T(8,128)}, f32[512,1024]{1,0:T(8,128)S(1)}, u32[]{:S(2)}) copy-start(f32[512,1024]{1,0:T(8,128)S(1)} %get-tuple-element.76.refs_9_) | copy-start | bytes 6291460
  162.4 7.6 %slice-start.1 = ((s8[5767168]{0:T(1024)(128)(4,1)}), s8[1572864]{0:T(1024)(128)(4,1)S(1)}, s32[]{:S(2)}) async-start(s8[5767168]{0:T(1024)(128)(4,1)} %bitcast.77), calls=%async_computation.1 | async-start | bytes 3145728
  162.4 14.9 %slice-start.2 = ((s8[5767168]{0:T(1024)(128)(4,1)}), s8[4194304]{0:T(1024)(128)(4,1)S(1)}, s32[]{:S(2)}) async-start(s8[5767168]{0:T(1024)(128)(4,1)} %bitcast.79), calls=%async_computation.2 | async-start | bytes 8388608
  170.0 4.8 %copy-start.1 = (f32[512,2816]{1,0:T(8,128)}, f32[512,2816]{1,0:T(8,128)S(1)}, u32[]{:S(2)}) copy-start(f32[512,2816]{1,0:T(8,128)S(1)} %get-tuple-element.80) | copy-start | bytes 17301508
  170.0 7.3 %slice-start.3 = ((s8[5767168]{0:T(1024)(128)(4,1)}), s8[1572864]{0:T(1024)(128)(4,1)S(1)}, s32[]{:S(2)}) async-start(s8[5767168]{0:T(1024)(128)(4,1)} %bitcast.79), calls=%async_computation.3 | async-start | bytes 3145728
  174.8 2.5 copy-start.2
  202.2 3.6 copy-start.10
  358.4 3.4 copy-start.11
  358.4 3.4 copy-start.12
  358.4 3.4 copy-start.13
  358.4 3.4 copy-start.14
  358.4 5.2 %copy-start.7 = (bf16[1,256,2816]{2,1,0:T(8,128)(2,1)S(1)}, bf16[1,256,2816]{2,1,0:T(8,128)(2,1)}, u32[]{:S(2)}) copy-start(bf16[1,256,2816]{2,1,0:T(8,128)(2,1)} %get-tuple-element.67) | copy-start | bytes 4325380
  358.4 5.1 %copy-start.8 = (bf16[1,256,2816]{2,1,0:T(8,128)(2,1)S(1)}, bf16[1,256,2816]{2,1,0:T(8,128)(2,1)}, u32[]{:S(2)}) copy-start(bf16[1,256,2816]{2,1,0:T(8,128)(2,1)} %get-tuple-element.69) | copy-start | bytes 4325380
  361.8 1.8 copy-start.5
  361.8 2.6 copy-start.6
  364.4 3.1 copy-start.3
  364.4 3.1 copy-start.4
  367.5 3.5 copy-start.9

commit v3 on v2

--- a/solution.py
+++ b/solution.py
@@ -61,6 +61,14 @@
     return jnp.dot(high, sums, preferred_element_type=F32) + jnp.dot(
         low, sums, preferred_element_type=F32
     )
+
+
+def rms_scaling(values):
+    return lax.rsqrt(jnp.mean(values * values, -1, keepdims=True) + EPSILON)
+
+
+def product(operand, weight):
+    return jnp.dot(operand, weight, preferred_element_type=F32)
 
 
 def column_tile(columns):
@@ -103,9 +111,15 @@
         o4,
         o5,
         o6,
+        output_out,
+        inner_out,
+        gate_out,
+        up_out,
+        normed_two_out,
+        attended_out,
+        normed_out,
+        branch_out,
         hidden_out,
-        normed_out,
-        attended_out,
         queries_out,
         keys_out,
         values_out,
@@ -126,6 +140,16 @@
         turned,
         mixed,
         attended,
+        normed_t,
+        attended_t,
+        normed_two_t,
+        normed_two,
+        inner,
+        inner_t,
+        gate_low,
+        up_low,
+        branch,
+        output,
         score_slots,
         soft_slots,
         total,
@@ -225,14 +249,14 @@
         return here[block - 8 :]
 
     lax.fori_loop(0, frames // block, norm_block, rim_all)
-    act_copies = [
-        pltpu.make_async_copy(hidden, hidden_out, act_sem.at[0]),
-        pltpu.make_async_copy(normed, normed_out, act_sem.at[1]),
-    ]
-    for copy in act_copies:
-        copy.start()
-
-    forwarded = {}
+    act_copies = []
+
+    def put(src, dst):
+        act_copies.append(pltpu.make_async_copy(src, dst, act_sem.at[len(act_copies)]))
+        act_copies[-1].start()
+
+    put(hidden, hidden_out)
+
     outs = {}
 
     def pass_on(at):
@@ -278,71 +302,94 @@
         lax.fori_loop(1, n_pos, start_turn, 0)
         turned[which, pl.ds(pos, 1)] = proj[which, rows_of(pos, part), :][None]
 
+    def transpose(src, dst):
+        tile = column_tile(src.shape[1])
+
+        def step(t, carry):
+            at = pl.ds(pl.multiple_of(t * tile, tile), tile)
+            dst[at, :] = src[:, at].T
+            return carry
+
+        lax.fori_loop(0, src.shape[1] // tile, step, 0)
+
+    transpose(normed, normed_t)
+    put(normed_t, normed_out)
     pass_on(3)
-    pass_on(4)
-    for which in range(3):
-
+
+    def end_turns(which):
         def end_turn(k, carry):
             turn(which, k).wait()
             return carry
 
         lax.fori_loop(1, n_pos, end_turn, 0)
-        copy = pltpu.make_async_copy(turned.at[which], turned_out[which], act_sem.at[2 + which])
-        copy.start()
-        act_copies.append(copy)
-
-    def attend(at, carry):
-        query = turned[0, at].astype(F32) * HEAD ** (-0.5)
+        put(turned.at[which], turned_out[which])
+
+    end_turns(0)
+    end_turns(1)
+
+    def score_rows(p, carry):
+        query = turned[0, p].astype(F32) * HEAD ** (-0.5)
 
         def score(j, highest):
             scores = sum_heads(query * turned[1, j].astype(F32), sums[...])
             score_slots[j] = scores
             return jnp.maximum(highest, scores)
 
-        highest = lax.fori_loop(0, at + 1, score, jnp.full((part, LANES), -1e30, F32))
+        highest = lax.fori_loop(0, p + 1, score, jnp.full((part, LANES), -1e30, F32))
 
         def weigh(j, mass):
             return mass + jnp.exp(score_slots[j] - highest)
 
-        mass = lax.fori_loop(0, at + 1, weigh, jnp.zeros((part, LANES), F32))
+        mass = lax.fori_loop(0, p + 1, weigh, jnp.zeros((part, LANES), F32))
         logsum = highest + jnp.log(mass)
+
+        def level(j, carry):
+            soft_slots[p, j] = jnp.exp(score_slots[j] - logsum)
+            return carry
+
+        return lax.fori_loop(0, p + 1, level, carry)
+
+    lax.fori_loop(0, n_pos, score_rows, 0)
+    put(soft_slots, soft_out)
+    pass_on(4)
+    end_turns(2)
+
+    def back(p):
+        return send(
+            mixed.at[p],
+            attended.at[rows_of(pos, part)],
+            back_send.at[p],
+            back_recv.at[pos],
+            pos=p,
+        )
+
+    def mix_rows(k, carry):
+        p = peer_of(pos, k, n_pos)
         total[...] = jnp.zeros_like(total)
 
         def mix(j, carry):
-            soft = jnp.exp(score_slots[j] - logsum)
-            soft_slots[at, j] = soft
-            soft_low = soft.astype(BF16)
-            total[...] += jnp.dot(soft_low, spread[...], preferred_element_type=F32) * turned[
+            total[...] += product(soft_slots[p, j].astype(BF16), spread[...]) * turned[
                 2, j
             ].astype(F32)
             return carry
 
-        lax.fori_loop(0, at + 1, mix, 0)
-        mixed[at] = total[...].astype(BF16)
-
-        @pl.when(at != pos)
+        lax.fori_loop(0, p + 1, mix, 0)
+        mixed[p] = total[...].astype(BF16)
+
+        @pl.when(p != pos)
         def _():
-            send(
-                mixed.at[at],
-                attended.at[rows_of(pos, part)],
-                back_send.at[at],
-                back_recv.at[pos],
-                pos=at,
-            ).start()
-
-        return carry
-
-    lax.fori_loop(0, n_pos, attend, 0)
-    copy = pltpu.make_async_copy(soft_slots, soft_out, act_sem.at[6])
-    copy.start()
-    act_copies.append(copy)
-    attended[rows_of(pos, part), :] = mixed[pos]
-
+            back(p).start()
+
+        @pl.when(p == pos)
+        def _():
+            attended[rows_of(pos, part), :] = mixed[p]
+
+        return carry
+
+    lax.fori_loop(1, n_pos + 1, mix_rows, 0)
     complete(3)
     complete(4)
-    for at in (5, 6):
-        pass_on(at)
-        complete(at)
+    pass_on(5)
 
     def end_back(k, carry):
         peer = peer_of(pos, k, n_pos)
@@ -356,9 +403,62 @@
         return carry
 
     lax.fori_loop(1, n_pos, end_back, 0)
-    copy = pltpu.make_async_copy(attended, attended_out, act_sem.at[5])
-    copy.start()
-    act_copies.append(copy)
+    complete(5)
+    tile = column_tile(features)
+
+    def columns_of(t):
+        return pl.ds(pl.multiple_of(t * tile, tile), tile)
+
+    def leave(t, carry):
+        columns = columns_of(t)
+        branch[:, columns] = hidden[:, columns].astype(F32) + product(
+            attended[...], full[3][:, columns]
+        )
+        return carry
+
+    lax.fori_loop(0, features // tile, leave, 0)
+    put(branch, branch_out)
+    gain_two = gains_out[1:2, :]
+
+    def norm_two(at, carry):
+        rows = pl.ds(pl.multiple_of(at * block, block), block)
+        here = branch[rows, :]
+        normed_two[rows, :] = (here * rms_scaling(here) * gain_two).astype(BF16)
+        return carry
+
+    lax.fori_loop(0, frames // block, norm_two, 0)
+
+    def feed(t, carry):
+        columns = columns_of(t)
+        gate = product(normed_two[...], full[4][:, columns])
+        up = product(normed_two[...], full[5][:, columns])
+        gate_low[:, columns] = gate.astype(BF16)
+        up_low[:, columns] = up.astype(BF16)
+        low = (gate * jax.nn.sigmoid(gate) * up).astype(BF16)
+        inner[:, columns] = low
+        inner_t[columns, :] = low.T
+        return carry
+
+    lax.fori_loop(0, inner.shape[1] // tile, feed, 0)
+    put(gate_low, gate_out)
+    put(up_low, up_out)
+    put(inner_t, inner_out)
+    transpose(attended, attended_t)
+    put(attended_t, attended_out)
+    transpose(normed_two, normed_two_t)
+    put(normed_two_t, normed_two_out)
+    pass_on(6)
+    complete(6)
+
+    def close(t, carry):
+        columns = columns_of(t)
+        output[:, columns] = (
+            branch[:, columns] + product(inner[...], full[6][:, columns])
+        ).astype(BF16)
+        return carry
+
+    lax.fori_loop(0, features // tile, close, 0)
+    put(output, output_out)
     for copy in far.values():
         copy.wait_send()
     for copy in near.values():
@@ -375,19 +475,24 @@
     count = len(shards)
     chips = n_fr // 2
     full = [(n_fr * shard.shape[0], shard.shape[1]) for shard in shards]
+    hidden_units = shards[4].shape[1]
     act = jax.ShapeDtypeStruct((frames, features), BF16)
+    act_t = jax.ShapeDtypeStruct((features, frames), BF16)
+    wide = jax.ShapeDtypeStruct((frames, hidden_units), BF16)
+    wide_t = jax.ShapeDtypeStruct((hidden_units, frames), BF16)
     turned = jax.ShapeDtypeStruct((n_pos, part, features), BF16)
     return pl.pallas_call(
         functools.partial(forward_kernel, n_fr, n_pos),
         name="forward",
         out_shape=[jax.ShapeDtypeStruct(shape, BF16) for shape in full]
-        + [act, act, act, turned, turned, turned]
+        + [act, wide_t, wide, wide, act_t, act_t, act_t]
+        + [jax.ShapeDtypeStruct((frames, features), F32), act, turned, turned, turned]
         + [
             jax.ShapeDtypeStruct((n_pos, n_pos, part, LANES), F32),
             jax.ShapeDtypeStruct((8, features), F32),
         ],
         in_specs=[VMEM, VMEM, VMEM] + [ANY] * count,
-        out_specs=[ANY] * (count + 7) + [VMEM],
+        out_specs=[ANY] * (count + 13) + [VMEM],
         scratch_shapes=[pltpu.VMEM(shape, BF16) for shape in full]
         + [
             pltpu.VMEM((16, features), BF16),
@@ -397,6 +502,16 @@
             pltpu.VMEM((3, frames, features), BF16),
             pltpu.VMEM((3, n_pos, part, features), BF16),
             pltpu.VMEM((n_pos, part, features), BF16),
+            pltpu.VMEM((frames, features), BF16),
+            pltpu.VMEM((features, frames), BF16),
+            pltpu.VMEM((features, frames), BF16),
+            pltpu.VMEM((features, frames), BF16),
+            pltpu.VMEM((frames, features), BF16),
+            pltpu.VMEM((frames, hidden_units), BF16),
+            pltpu.VMEM((hidden_units, frames), BF16),
+            pltpu.VMEM((frames, hidden_units), BF16),
+            pltpu.VMEM((frames, hidden_units), BF16),
+            pltpu.VMEM((frames, features), F32),
             pltpu.VMEM((frames, features), BF16),
             pltpu.VMEM((n_pos, part, LANES), F32),
             pltpu.VMEM((n_pos, n_pos, part, LANES), F32),
@@ -416,20 +531,12 @@
             DMA((3, n_pos)),
             DMA((n_pos,)),
             DMA((n_pos,)),
-            DMA((7,)),
+            DMA((14,)),
         ],
         compiler_params=pltpu.CompilerParams(
             collective_id=0, has_side_effects=True, vmem_limit_bytes=VMEM_BYTES
         ),
     )(own_rows, lags, gains, *shards)
-
-
-def rms_scaling(values):
-    return lax.rsqrt(jnp.mean(values * values, -1, keepdims=True) + EPSILON)
-
-
-def product(operand, weight):
-    return jnp.dot(operand, weight, preferred_element_type=F32)
 
 
 def back_product(grad_rows, weight):
@@ -1026,35 +1133,18 @@
             down_weight,
         )
     ]
-    *full, hidden, normed, attended, queries, keys, values, soft, gain_rows = forward_call(
-        n_fr, n_pos, own_rows, lags, gains, shards
-    )
-    out_full, gate_full, up_full, down_full = full[3:]
-    branch = hidden.astype(F32) + product(attended, out_full)
-    normed_two = (branch * rms_scaling(branch) * gain_rows[1:2]).astype(BF16)
-    gate_act = product(normed_two, gate_full)
-    up_act = product(normed_two, up_full)
-    inner_act = (jax.nn.silu(gate_act) * up_act).astype(BF16)
-    output = (branch + product(inner_act, down_full)).astype(BF16)
+    results = forward_call(n_fr, n_pos, own_rows, lags, gains, shards)
+    full, output, saved, gain_rows = results[:7], results[7], results[8:20], results[20]
+    inner_t, *saved = saved
     grads = backward_call(
         n_fr,
         n_pos,
         [shard.shape for shard in shards],
         lags,
         gain_rows,
-        inner_act.T,
+        inner_t,
         cotangent[0],
-        gate_act.astype(BF16),
-        up_act.astype(BF16),
-        normed_two.T,
-        attended.T,
-        normed.T,
-        branch,
-        hidden,
-        queries,
-        keys,
-        values,
-        soft,
+        *saved,
         *full,
     )
     kept, come, (input_grad, gain_grads) = grads[:7], grads[7:14], grads[14:]

time: 373 us -> 328 us (0.88)
  matrix products: 20.3 us -> 0 us
  local copies, waits for them, and re-layouts: 25.5 us -> 7.93 us
  other arithmetic: 19.7 us -> 11.6 us
    dot_general x4 -> x0, matrix products: 20.3 us -> none  [product(): return jnp.dot(operand, weight, preferred_element_type=F32)]
    dot_general x2 -> x0, local copies, waits for them, and re-layouts: 12.6 us -> none  [product(): return jnp.dot(operand, weight, preferred_element_type=F32)]
    convert_element_type x1 -> x0, other arithmetic: 7.81 us -> none  [on_device(): inner_act = (jax.nn.silu(gate_act) * up_act).astype(BF16)]
where the time goes in v3:
time: 328 us
  Pallas kernels  308 us (94%)
  other arithmetic  11.6 us (4%)
  local copies, waits for them, and re-layouts  7.93 us (2%)
    pallas_call x1, Pallas kernels, forward_call(): pl.pallas_call(functools.partial(forward_kernel, n_fr, n_pos), name='forw...  156 us
    pallas_call x1, Pallas kernels, backward_call(): pl.pallas_call(functools.partial(backward_kernel, n_fr, n_pos, shard_rows...  151 us
    broadcast_in_dim x4, other arithmetic, on_device(): (own.astype(F32) + jnp.sum(others.astype(F32), 0))[None]  10.3 us

profile of v3, /device:TPU:0, one launch (start us, length us, event | category | flops | bytes accessed | tf_op | source)
XLA Modules:
  0.0 328.0 jit_solution(16990820229927547681)
XLA Ops:
  0.6 0.7 broadcast_in_dim.30
  1.4 1.3 fusion.10.refs_2_
  2.7 0.9 broadcast_in_dim_reshape.4.refs_1_.refs_0_
  3.6 156.4 %forward.1 = (bf16[1024,1024]{1,0:T(8,128)(2,1)}, bf16[1024,1024]{1,0:T(8,128)(2,1)}, bf16[1024,1024]{1,0:T(8,128)(2,1)}, bf16[1024,1024]{1,0:T(8,128)(2,1)}, bf...) custom-call(bf16[512,1024]{1,0:T(8,128)(2,1)} %bitcast.53, ...), custom_call_target="tpu_custom_call" | custom-call | tf_op jit(solution)/shard_map/forward/pallas_call | solution.py:484
  159.9 151.3 %backward.1 = (bf16[256,1024]{1,0:T(8,128)(2,1)}, bf16[256,1024]{1,0:T(8,128)(2,1)}, bf16[256,1024]{1,0:T(8,128)(2,1)}, bf16[256,1024]{1,0:T(8,128)(2,1)}, bf16[...) custom-call(s32[512,1]{1,0:T(8,128)} %broadcast_in_dim_reshape.4.ref, ...), custom_call_target="tpu_custom_call" | custom-call | tf_op jit(solution)/shard_map/backward/pallas_call | solution.py:1037
  311.3 1.3 fusion.11
  312.6 0.0 copy-start.11
  312.7 3.4 %fusion.5 = (f32[1,256,1024]{2,1,0:T(8,128)}, f32[1,256,1024]{2,1,0:T(8,128)}) fusion(bf16[256,1024]{1,0:T(8,128)(2,1)} %get-tuple-element.72, bf16[1,256,1024]{2,1,0:T(8,128)(2,1)} %get-tuple-element.73, bf16[1,256,1024]{2,1,0:T(8,128)(2,1)} %get-tuple-element.71, bf16[256,1024]{1,0:T(8,128)(2,1)} %get-tuple-element.70), kind=kLoop, calls=%fused_computation.11 | loop fusion | flops 1572864 | bytes 4194304 | tf_op jit(solution)/shard_map/broadcast_in_dim | solution.py:1155
  316.0 0.0 copy-done.8
  316.0 0.0 copy-done.10
  316.0 0.0 copy-done.11
  316.0 0.0 copy-start.4
  316.1 0.0 copy-start.5
  316.1 1.7 fusion.3
  317.8 0.8 copy-done.5
  318.6 2.2 fusion
  320.8 0.0 copy-done
  320.8 0.3 copy-done.1
  321.0 0.8 copy-done.2
  321.9 0.4 copy-done.3
  322.3 3.1 fusion.1
  325.4 1.0 copy.27
  326.4 0.6 copy-done.7
  327.0 1.0 copy.28
  (12 shorter events, 0.0 us)
Async XLA Ops:
  312.6 3.4 %copy-start.8 = (bf16[256,1024]{1,0:T(8,128)(2,1)S(1)}, bf16[256,1024]{1,0:T(8,128)(2,1)}, u32[]{:S(2)}) copy-start(bf16[256,1024]{1,0:T(8,128)(2,1)} %get-tuple-element.74) | copy-start | bytes 1572868
  312.6 3.4 %copy-start.9 = (bf16[256,1024]{1,0:T(8,128)(2,1)S(1)}, bf16[256,1024]{1,0:T(8,128)(2,1)}, u32[]{:S(2)}) copy-start(bf16[256,1024]{1,0:T(8,128)(2,1)} %get-tuple-element.76) | copy-start | bytes 1572868
  312.6 3.4 %copy-start.10 = (bf16[1,256,1024]{2,1,0:T(8,128)(2,1)S(1)}, bf16[1,256,1024]{2,1,0:T(8,128)(2,1)}, u32[]{:S(2)}) copy-start(bf16[1,256,1024]{2,1,0:T(8,128)(2,1)} %get-tuple-element.75) | copy-start | bytes 1572868
  312.6 3.4 %copy-start.11 = (bf16[1,256,1024]{2,1,0:T(8,128)(2,1)S(1)}, bf16[1,256,1024]{2,1,0:T(8,128)(2,1)}, u32[]{:S(2)}) copy-start(bf16[1,256,1024]{2,1,0:T(8,128)(2,1)} %get-tuple-element.77) | copy-start | bytes 1572868
  316.0 1.7 copy-start.4
  316.1 2.5 copy-start.5
  318.6 2.2 copy-start
  318.6 2.4 copy-start.1
  318.6 3.3 copy-start.2
  318.6 3.7 %copy-start.3 = (bf16[1,256,2816]{2,1,0:T(8,128)(2,1)S(1)}, bf16[1,256,2816]{2,1,0:T(8,128)(2,1)}, u32[]{:S(2)}) copy-start(bf16[1,256,2816]{2,1,0:T(8,128)(2,1)} %get-tuple-element.81) | copy-start | bytes 4325380
  322.3 3.1 copy-start.6
  325.4 1.6 copy-start.7

commit v4 on v3

--- a/solution.py
+++ b/solution.py
@@ -10,6 +10,8 @@
 HEAD = 64
 LANES = 128
 EPSILON = 1e-06
+LATE = 37
+TERMS_HELD = 2750000
 MESH = pl.DeviceIdType.MESH
 F32 = jnp.float32
 BF16 = jnp.bfloat16
@@ -49,6 +51,11 @@
     return pl.ds(pl.multiple_of(index * rows, rows), rows)
 
 
+def lag_of(delays, at):
+    here = lax.broadcasted_iota(jnp.int32, delays.shape, 1) == at
+    return jnp.sum(jnp.where(here, delays[...].astype(F32), 0.0), 1, keepdims=True)
+
+
 def head_sums(shape, feature_dim):
     features = lax.broadcasted_iota(jnp.int32, shape, feature_dim)
     heads = lax.broadcasted_iota(jnp.int32, shape, 1 - feature_dim)
@@ -92,11 +99,12 @@
     return lax.rem(pos + k, n_pos)
 
 
-def forward_kernel(n_fr, n_pos, *refs):
+def forward_kernel(n_fr, n_pos, pieces, late, steps, *refs):
     (
         own_rows,
-        lags,
-        gains,
+        delays,
+        gain_one,
+        gain_two,
         w0,
         w1,
         w2,
@@ -111,8 +119,8 @@
         o4,
         o5,
         o6,
-        output_out,
         inner_out,
+        inner_rows_out,
         gate_out,
         up_out,
         normed_two_out,
@@ -133,6 +141,7 @@
         f5,
         f6,
         rim,
+        gains,
         gain_slots,
         hidden,
         normed,
@@ -149,7 +158,6 @@
         gate_low,
         up_low,
         branch,
-        output,
         score_slots,
         soft_slots,
         total,
@@ -193,6 +201,14 @@
         fr=lax.rem(fr + 1, n_fr),
     )
     rim_copy.start()
+    gains[...] = jnp.concatenate(
+        [
+            gain_one[...].astype(F32),
+            gain_two[...].astype(F32),
+            jnp.zeros((6, gains.shape[1]), F32),
+        ],
+        0,
+    )
     gain_copies = []
     for k in range(1, n_fr):
         copy = send(
@@ -207,19 +223,75 @@
     far = {}
     near = {}
     own = {}
+    def piece_rows(at, origin, piece):
+        rows = shards[at].shape[0]
+        size = rows // pieces[at]
+        return pl.ds(pl.multiple_of(origin * rows + piece * size, size), size)
+
+    tile = column_tile(features)
+    tiles = features // tile
+    spare = sum(steps) * (chips - 1)
+
+    def slot(at, k, piece):
+        return (sum(steps[:at]) + piece) * (chips - 1) + k - 1
+
+
+    def columns_of(t):
+        return pl.ds(pl.multiple_of(t * tile, tile), tile)
+
+    for t in range(tiles):
+        for k in range(1, chips):
+            far[0, k, t] = send(
+                w0.at[:, columns_of(t)],
+                f0.at[rows_of(fr, w0.shape[0]), columns_of(t)],
+                far_send.at[slot(0, k, t)],
+                far_recv.at[slot(0, k, t)],
+                fr=lax.rem(chip + k, chips) * 2 + core,
+            )
+            far[0, k, t].start()
+    up_tiles = w5.shape[1] // tile
+
+    def up_far(t, k):
+        return send(
+            w5.at[:, columns_of(t)],
+            f5.at[rows_of(fr, w5.shape[0]), columns_of(t)],
+            far_send.at[slot(5, k, t)],
+            far_recv.at[slot(5, k, t)],
+            fr=lax.rem(chip + k, chips) * 2 + core,
+        )
+
+    def up_near(t, k):
+        there = f5.at[
+            rows_of(lax.rem(chip - k + chips, chips) * 2 + core, w5.shape[0]), columns_of(t)
+        ]
+        return send(there, there, near_send.at[slot(5, k, t)], near_recv.at[slot(5, k, t)], fr=partner)
+
+    def up_start(t, carry):
+        for k in range(1, chips):
+            up_far(t, k).start()
+        return carry
+
     for at, (shard, whole) in enumerate(zip(shards, full)):
-        rows = shard.shape[0]
-        for k in range(1, chips):
-            there = lax.rem(chip + k, chips) * 2 + core
-            far[at, k] = send(
-                shard, whole.at[rows_of(fr, rows)], far_send.at[at, k], far_recv.at[at, k], fr=there
-            )
-            far[at, k].start()
-        near[at, 0] = send(
-            shard, whole.at[rows_of(fr, rows)], near_send.at[at, 0], near_recv.at[at, 0], fr=partner
-        )
-        near[at, 0].start()
-        own[at] = pltpu.make_async_copy(shard, whole.at[rows_of(fr, rows)], own_sem.at[at])
+        if at == 5:
+            lax.fori_loop(0, up_tiles, up_start, 0)
+        mine = rows_of(fr, shard.shape[0])
+        size = shard.shape[0] // pieces[at]
+        for piece in range(0 if at in (0, 5) else pieces[at] - late[at]):
+            for k in range(1, chips):
+                far[at, k, piece] = send(
+                    shard.at[piece * size : (piece + 1) * size],
+                    whole.at[piece_rows(at, fr, piece)],
+                    far_send.at[slot(at, k, piece)],
+                    far_recv.at[slot(at, k, piece)],
+                    fr=lax.rem(chip + k, chips) * 2 + core,
+                )
+                far[at, k, piece].start()
+        near[at, 0, 0] = send(
+            shard, whole.at[mine], near_send.at[spare + at], near_recv.at[spare + at], fr=partner
+        )
+        if at < 3:
+            near[at, 0, 0].start()
+        own[at] = pltpu.make_async_copy(shard, whole.at[mine], own_sem.at[at])
         own[at].start()
 
     sums[...] = head_sums(sums.shape, 0)
@@ -231,7 +303,7 @@
     gains_out[...] = jnp.concatenate([gain_slots[at] for at in range(n_fr)], 1)
     rim_copy.wait()
 
-    block = 64
+    block = frames // delays.shape[1]
     rim_rows = rim.shape[0]
     rim_all = jnp.where(fr == 0, 0.0, rim[...].astype(F32))[rim_rows - 8 :]
 
@@ -241,7 +313,7 @@
         window = jnp.concatenate([carry, here], 0)
         once = pltpu.roll(window, 1, 0)[8:]
         twice = pltpu.roll(window, 2, 0)[8:]
-        lag = lags[rows, :]
+        lag = lag_of(delays, at)
         values = jnp.where(lag == 0, here, jnp.where(lag == 1, once, twice))
         hidden[rows, :] = values.astype(BF16)
         scaling = lax.rsqrt(jnp.mean(values * values, -1, keepdims=True) + EPSILON)
@@ -259,26 +331,51 @@
 
     outs = {}
 
-    def pass_on(at):
-        rows = shards[at].shape[0]
+    def pass_on(at, piece=0):
         for k in range(1, chips):
-            far[at, k].wait_recv()
+            far[at, k, piece].wait_recv()
             origin = lax.rem(chip - k + chips, chips) * 2 + core
-            near[at, k] = send(
-                full[at].at[rows_of(origin, rows)],
-                full[at].at[rows_of(origin, rows)],
-                near_send.at[at, k],
-                near_recv.at[at, k],
+            rows = piece_rows(at, origin, piece)
+            near[at, k, piece] = send(
+                full[at].at[rows],
+                full[at].at[rows],
+                near_send.at[slot(at, k, piece)],
+                near_recv.at[slot(at, k, piece)],
                 fr=partner,
             )
-            near[at, k].start()
+            near[at, k, piece].start()
 
     def complete(at):
         own[at].wait()
         for k in range(chips):
-            near[at, k].wait_recv()
+            near[at, k, 0].wait_recv()
         outs[at] = pltpu.make_async_copy(full[at], full_out[at], out_sem.at[at])
         outs[at].start()
+
+    def finish_pieces(at):
+        early = range(pieces[at] - late[at])
+        rows = shards[at].shape[0]
+        size = rows // pieces[at]
+
+        def put_rows(where):
+            pltpu.make_async_copy(
+                full[at].at[where], full_out[at].at[where], out_sem.at[at]
+            ).start()
+
+        own[at].wait()
+        put_rows(rows_of(fr, rows))
+        near[at, 0, 0].wait_recv()
+        put_rows(rows_of(partner, rows))
+        for piece in early:
+            pass_on(at, piece)
+            for k in range(1, chips):
+                put_rows(piece_rows(at, lax.rem(chip - k + chips, chips) * 2 + core, piece))
+        for piece in early:
+            for k in range(1, chips):
+                near[at, k, piece].wait_recv()
+                put_rows(piece_rows(at, lax.rem(chip - k + chips, chips) * 2 + 1 - core, piece))
+        written = full_out[at].at[0 : n_fr * rows - 2 * (chips - 1) * late[at] * size]
+        outs[at] = pltpu.make_async_copy(written, written, out_sem.at[at])
 
     def turn(which, k):
         peer = peer_of(pos, k, n_pos)
@@ -290,7 +387,37 @@
             pos=peer,
         )
 
-    for which in range(3):
+    own[0].wait()
+    near[0, 0, 0].wait_recv()
+    for t in range(tiles):
+        for k in range(1, chips):
+            far[0, k, t].wait_recv()
+            origin = lax.rem(chip - k + chips, chips) * 2 + core
+            there = f0.at[rows_of(origin, w0.shape[0]), columns_of(t)]
+            near[0, k, t] = send(
+                there, there, near_send.at[slot(0, k, t)], near_recv.at[slot(0, k, t)], fr=partner
+            )
+            near[0, k, t].start()
+        for k in range(1, chips):
+            near[0, k, t].wait_recv()
+        proj[0, :, columns_of(t)] = product(normed[...], f0[:, columns_of(t)]).astype(BF16)
+
+        def start_tile(k, carry):
+            peer = peer_of(pos, k, n_pos)
+            send(
+                proj.at[0, rows_of(peer, part), columns_of(t)],
+                turned.at[0, pos, :, columns_of(t)],
+                turn_send.at[0, k],
+                turn_recv.at[0, k],
+                pos=peer,
+            ).start()
+            return carry
+
+        lax.fori_loop(1, n_pos, start_tile, 0)
+    turned[0, pl.ds(pos, 1)] = proj[0, rows_of(pos, part), :][None]
+    outs[0] = pltpu.make_async_copy(f0, o0, out_sem.at[0])
+    outs[0].start()
+    for which in (1, 2):
         pass_on(which)
         complete(which)
         multiply(normed, full[which], proj.at[which])
@@ -301,6 +428,9 @@
 
         lax.fori_loop(1, n_pos, start_turn, 0)
         turned[which, pl.ds(pos, 1)] = proj[which, rows_of(pos, part), :][None]
+
+    for at in range(3, 7):
+        near[at, 0, 0].start()
 
     def transpose(src, dst):
         tile = column_tile(src.shape[1])
@@ -389,7 +519,6 @@
     lax.fori_loop(1, n_pos + 1, mix_rows, 0)
     complete(3)
     complete(4)
-    pass_on(5)
 
     def end_back(k, carry):
         peer = peer_of(pos, k, n_pos)
@@ -403,12 +532,6 @@
         return carry
 
     lax.fori_loop(1, n_pos, end_back, 0)
-    complete(5)
-    tile = column_tile(features)
-
-    def columns_of(t):
-        return pl.ds(pl.multiple_of(t * tile, tile), tile)
-
     def leave(t, carry):
         columns = columns_of(t)
         branch[:, columns] = hidden[:, columns].astype(F32) + product(
@@ -418,18 +541,45 @@
 
     lax.fori_loop(0, features // tile, leave, 0)
     put(branch, branch_out)
-    gain_two = gains_out[1:2, :]
+    feed_gain = gains_out[1:2, :]
 
     def norm_two(at, carry):
         rows = pl.ds(pl.multiple_of(at * block, block), block)
         here = branch[rows, :]
-        normed_two[rows, :] = (here * rms_scaling(here) * gain_two).astype(BF16)
+        normed_two[rows, :] = (here * rms_scaling(here) * feed_gain).astype(BF16)
         return carry
 
     lax.fori_loop(0, frames // block, norm_two, 0)
+
+    transpose(attended, attended_t)
+    put(attended_t, attended_out)
+    transpose(normed_two, normed_two_t)
+    put(normed_two_t, normed_two_out)
+
+    def up_pass(t):
+        for k in range(1, chips):
+            up_far(t, k).wait_recv()
+            up_near(t, k).start()
+
+    def up_put(t):
+        return pltpu.make_async_copy(
+            f5.at[:, columns_of(t)], o5.at[:, columns_of(t)], out_sem.at[5]
+        )
+
+    own[5].wait()
+    near[5, 0, 0].wait_recv()
+    up_pass(0)
 
     def feed(t, carry):
         columns = columns_of(t)
+
+        @pl.when(t + 1 < up_tiles)
+        def _():
+            up_pass(t + 1)
+
+        for k in range(1, chips):
+            up_near(t, k).wait_recv()
+        up_put(t).start()
         gate = product(normed_two[...], full[4][:, columns])
         up = product(normed_two[...], full[5][:, columns])
         gate_low[:, columns] = gate.astype(BF16)
@@ -443,22 +593,17 @@
     put(gate_low, gate_out)
     put(up_low, up_out)
     put(inner_t, inner_out)
-    transpose(attended, attended_t)
-    put(attended_t, attended_out)
-    transpose(normed_two, normed_two_t)
-    put(normed_two_t, normed_two_out)
-    pass_on(6)
-    complete(6)
-
-    def close(t, carry):
-        columns = columns_of(t)
-        output[:, columns] = (
-            branch[:, columns] + product(inner[...], full[6][:, columns])
-        ).astype(BF16)
+    put(inner, inner_rows_out)
+    finish_pieces(6)
+
+    def up_sent(t, carry):
+        for k in range(1, chips):
+            up_far(t, k).wait_send()
+            up_near(t, k).wait_send()
         return carry
 
-    lax.fori_loop(0, features // tile, close, 0)
-    put(output, output_out)
+    lax.fori_loop(0, up_tiles, up_sent, 0)
+    pltpu.make_async_copy(o5, o5, out_sem.at[5]).wait()
     for copy in far.values():
         copy.wait_send()
     for copy in near.values():
@@ -469,11 +614,24 @@
         copy.wait()
 
 
-def forward_call(n_fr, n_pos, own_rows, lags, gains, shards):
+def down_pieces(rows):
+    return next(cuts for cuts in (11, 8, 4, 2, 1) if rows % (16 * cuts) == 0)
+
+
+def forward_call(n_fr, n_pos, own_rows, delays, gain_one, gain_two, shards):
     frames, features = own_rows.shape
     part = frames // n_pos
     count = len(shards)
     chips = n_fr // 2
+    width = gain_one.shape[1]
+    last = down_pieces(shards[-1].shape[0])
+    pieces = [1] * (count - 1) + [last]
+    late = [0] * (count - 1) + [last * LATE // 100]
+    tile = column_tile(features)
+    steps = [1] * (count - 1) + [last - late[-1]]
+    steps[0] = features // tile
+    steps[5] = shards[5].shape[1] // tile
+    copies = sum(steps) * (chips - 1)
     full = [(n_fr * shard.shape[0], shard.shape[1]) for shard in shards]
     hidden_units = shards[4].shape[1]
     act = jax.ShapeDtypeStruct((frames, features), BF16)
@@ -482,21 +640,22 @@
     wide_t = jax.ShapeDtypeStruct((hidden_units, frames), BF16)
     turned = jax.ShapeDtypeStruct((n_pos, part, features), BF16)
     return pl.pallas_call(
-        functools.partial(forward_kernel, n_fr, n_pos),
+        functools.partial(forward_kernel, n_fr, n_pos, pieces, late, steps),
         name="forward",
         out_shape=[jax.ShapeDtypeStruct(shape, BF16) for shape in full]
-        + [act, wide_t, wide, wide, act_t, act_t, act_t]
+        + [wide_t, wide, wide, wide, act_t, act_t, act_t]
         + [jax.ShapeDtypeStruct((frames, features), F32), act, turned, turned, turned]
         + [
             jax.ShapeDtypeStruct((n_pos, n_pos, part, LANES), F32),
             jax.ShapeDtypeStruct((8, features), F32),
         ],
-        in_specs=[VMEM, VMEM, VMEM] + [ANY] * count,
+        in_specs=[VMEM] * 4 + [ANY] * count,
         out_specs=[ANY] * (count + 13) + [VMEM],
         scratch_shapes=[pltpu.VMEM(shape, BF16) for shape in full]
         + [
             pltpu.VMEM((16, features), BF16),
-            pltpu.VMEM((n_fr, *gains.shape), F32),
+            pltpu.VMEM((8, width), F32),
+            pltpu.VMEM((n_fr, 8, width), F32),
             pltpu.VMEM((frames, features), BF16),
             pltpu.VMEM((frames, features), BF16),
             pltpu.VMEM((3, frames, features), BF16),
@@ -512,16 +671,15 @@
             pltpu.VMEM((frames, hidden_units), BF16),
             pltpu.VMEM((frames, hidden_units), BF16),
             pltpu.VMEM((frames, features), F32),
-            pltpu.VMEM((frames, features), BF16),
             pltpu.VMEM((n_pos, part, LANES), F32),
             pltpu.VMEM((n_pos, n_pos, part, LANES), F32),
             pltpu.VMEM((part, features), F32),
             pltpu.VMEM((features, LANES), BF16),
             pltpu.VMEM((LANES, features), BF16),
-            DMA((count, chips)),
-            DMA((count, chips)),
-            DMA((count, chips)),
-            DMA((count, chips)),
+            DMA((copies,)),
+            DMA((copies,)),
+            DMA((copies + count,)),
+            DMA((copies + count,)),
             DMA((count,)),
             DMA((count,)),
             DMA((2,)),
@@ -536,7 +694,7 @@
         compiler_params=pltpu.CompilerParams(
             collective_id=0, has_side_effects=True, vmem_limit_bytes=VMEM_BYTES
         ),
-    )(own_rows, lags, gains, *shards)
+    )(own_rows, delays, gain_one, gain_two, *shards)
 
 
 def back_product(grad_rows, weight):
@@ -548,12 +706,24 @@
     return jnp.sum(values.reshape(rows // 8, 8, features), 0)
 
 
-def backward_kernel(n_fr, n_pos, shard_rows, *refs):
+def split_terms(chips, spread_rows, shapes):
+    early = []
+    room = TERMS_HELD + 3 * LANES * (4096 - spread_rows)
+    for at in (6, 4, 5, 3, 2):
+        room -= (chips - 1) * shapes[at][0] * shapes[at][1]
+        if room < 0:
+            break
+        early.append(at)
+    return early, [at for at in range(len(shapes)) if at not in early]
+
+
+def backward_kernel(n_fr, n_pos, shard_rows, early, late, *refs):
     (
-        lags,
+        delays,
         gain_rows,
         inner_t,
         cot,
+        inner_rows,
         gate_low,
         up_low,
         normed_two_t,
@@ -566,11 +736,14 @@
         values,
         soft_in,
         *weights,
-    ) = refs[:22]
-    kept_out = refs[22:29]
-    come_out = refs[29:36]
-    input_grad, gains_out = refs[36:38]
-    held = refs[38:45]
+    ) = refs[:24]
+    kept_out = refs[24:31]
+    refs = refs[31:]
+    come_out, refs = dict(zip(late, refs)), refs[len(late) :]
+    output, input_grad, down_w, gains_out, *refs = refs
+    held, refs = refs[:7], refs[7:]
+    come, refs = dict(zip(early, refs)), refs[len(early) :]
+    come.update(come_out)
     (
         made,
         down_slots,
@@ -583,9 +756,7 @@
         up_v,
         normed_two_v,
         attended_v,
-        normed_v,
         branch,
-        hidden,
         total,
         low_rows,
         grad_rows,
@@ -617,8 +788,12 @@
         gain_recv,
         rim_sem,
         out_sem,
-    ) = refs[45:]
-    query_w, key_w, value_w, out_w, gate_w, up_w, down_w = weights
+        late_far_send,
+        late_far_recv,
+        late_near_send,
+        late_near_recv,
+    ) = refs
+    query_w, key_w, value_w, out_w, gate_w, up_w, _, down_shard = weights
     fr = lax.axis_index("fr")
     pos = lax.axis_index("pos")
     chips = n_fr // 2
@@ -629,6 +804,28 @@
     part = frames // n_pos
     tile = made.shape[-1]
     greet(n_fr, n_pos)
+
+    down_rows = down_shard.shape[0]
+    cuts = down_pieces(down_rows)
+    size = down_rows // cuts
+    late_count = cuts * LATE // 100
+    late_far = {}
+    late_near = {}
+
+    def late_rows(origin, piece):
+        start = origin * down_rows + (cuts - late_count + piece) * size
+        return pl.ds(pl.multiple_of(start, size), size)
+
+    for piece in range(late_count):
+        for k in range(1, chips):
+            late_far[piece, k] = send(
+                down_shard.at[pl.ds((cuts - late_count + piece) * size, size)],
+                down_w.at[late_rows(fr, piece)],
+                late_far_send.at[piece * (chips - 1) + k - 1],
+                late_far_recv.at[piece * (chips - 1) + k - 1],
+                fr=lax.rem(chip + k, chips) * 2 + core,
+            )
+            late_far[piece, k].start()
 
     loads = {}
 
@@ -655,8 +852,6 @@
 
     load("inner", inner_t, inner_v)
     load("cot", cot, cot_v)
-    for copy in feed_copies(0):
-        copy.start()
     load("gate", gate_low, gate_v)
     load("up", up_low, up_v)
     load("branch", branch_in, branch)
@@ -667,8 +862,6 @@
     load("keys", keys, turned.at[1])
     load("values", values, turned.at[2])
     load("soft", soft_in, soft)
-    load("normed", normed_t, normed_v)
-    load("hidden", hidden_in, hidden)
     load("value_w", value_w, small.at[1])
     load("key_w", key_w, small.at[2])
     sums[...] = head_sums(sums.shape, 0)
@@ -680,6 +873,34 @@
     def settle():
         while pending:
             pending.pop(0)()
+
+    def keep(at, t):
+        pltpu.make_async_copy(
+            held[at].at[t, chip], kept_out[at].at[:, columns_of(t)], kept_sem.at[at]
+        ).start()
+
+    def arrivals(at, k):
+        return send(
+            come[at].at[k - 1],
+            come[at].at[k - 1],
+            far_send.at[at * (chips - 1) + k - 1],
+            far_recv.at[at * (chips - 1) + k - 1],
+            fr=lax.rem(chip + k, chips) * 2 + core,
+        )
+
+    def gather_terms(at):
+        for k in range(1, chips):
+            arrivals(at, k).wait_recv()
+
+        def add(t, carry):
+            value = held[at][t, chip].astype(F32)
+            for k in range(1, chips):
+                value = value + come[at][k - 1, :, columns_of(t)].astype(F32)
+            held[at][t, chip] = value.astype(BF16)
+            keep(at, t)
+            return carry
+
+        lax.fori_loop(0, held[at].shape[0], add, 0)
 
     def reduce_weight(at, left_t, right):
         rows = shard_rows[at]
@@ -694,7 +915,7 @@
                 made.at[slot, 1 - core, :, pl.ds(0, rows)],
                 held[at].at[t],
                 give_send.at[slot],
-                take_recv.at[at, t],
+                take_recv.at[sum(held[w].shape[0] for w in range(at)) + t],
                 fr=partner,
             )
 
@@ -705,16 +926,15 @@
                 held[at][t, there] = (
                     held[at][t, there].astype(F32) + made[slot, core, there, 0:rows].astype(F32)
                 ).astype(BF16)
-            pltpu.make_async_copy(
-                held[at].at[t, chip], kept_out[at].at[:, columns_of(t)], kept_sem.at[at]
-            ).start()
+            if at in come_out:
+                keep(at, t)
             for k in range(1, chips):
                 there = lax.rem(chip + k, chips)
                 send(
                     held[at].at[t, there],
-                    come_out[at].at[k - 1, :, columns_of(t)],
-                    far_send.at[at, k],
-                    far_recv.at[at, k],
+                    come[at].at[k - 1, :, columns_of(t)],
+                    far_send.at[at * (chips - 1) + k - 1],
+                    far_recv.at[at * (chips - 1) + k - 1],
                     fr=there * 2 + core,
                 ).start()
 
@@ -754,6 +974,22 @@
     loads["cot"].wait()
     reduce_weight(6, inner_v, cot_v)
 
+    for piece in range(late_count):
+        for k in range(1, chips):
+            late_far[piece, k].wait_recv()
+            rows = late_rows(lax.rem(chip - k + chips, chips) * 2 + core, piece)
+            late_near[piece, k] = send(
+                down_w.at[rows],
+                down_w.at[rows],
+                late_near_send.at[piece * (chips - 1) + k - 1],
+                late_near_recv.at[piece * (chips - 1) + k - 1],
+                fr=partner,
+            )
+            late_near[piece, k].start()
+    for copy in late_near.values():
+        copy.wait_recv()
+    for copy in feed_copies(0):
+        copy.start()
     loads["gate"].wait()
     loads["up"].wait()
     feed_tiles = gate_v.shape[1] // tile
@@ -788,8 +1024,8 @@
     lax.fori_loop(0, feed_tiles, feed, 0)
     settle()
 
-    block = 64
-    blocks = frames // block
+    blocks = delays.shape[1]
+    block = frames // blocks
     loads["branch"].wait()
 
     def block_rows(at):
@@ -836,10 +1072,14 @@
     lax.fori_loop(1, n_pos, start_turn, 0)
     turned[3, pl.ds(pos, 1)] = grad_rows[rows_of(pos, part), :][None]
     load("query_w", query_w, small.at[0])
+    load("branch_again", branch_in, total)
+    load("hidden", hidden_in, cot_v)
 
     loads["normed_two"].wait()
     reduce_weight(4, normed_two_v, gate_v)
+    load("inner_rows", inner_rows, gate_v)
     reduce_weight(5, normed_two_v, up_v)
+    load("normed", normed_t, normed_two_v)
     loads["attended"].wait()
     reduce_weight(3, attended_v, low_rows)
 
@@ -918,6 +1158,21 @@
         return carry
 
     lax.fori_loop(1, n_pos + 1, query_part, 0)
+
+    def down_copy(t):
+        return feed_copies(t)[0]
+
+    def close(t, carry):
+        @pl.when(t + 1 < feed_tiles)
+        def _():
+            down_copy(t + 1).start()
+
+        down_copy(t).wait()
+        units = gate_v[:, columns_of(t)]
+        for at in range(features // tile):
+            columns = slice(at * tile, (at + 1) * tile)
+            total[:, columns] += product(units, down_slots[lax.rem(t, 2), :, columns])
+        return carry
 
     loads["normed"].wait()
     for which, slot, name in ((2, 1, "value_w"), (1, 2, "key_w"), (0, 0, "query_w")):
@@ -934,7 +1189,17 @@
             return carry
 
         lax.fori_loop(1, n_pos, end_back, 0)
-        reduce_weight(which, normed_v, arrived.at[which])
+        reduce_weight(which, normed_two_v, arrived.at[which])
+        if which == 2:
+            loads["inner_rows"].wait()
+            loads["branch_again"].wait()
+            down_copy(0).start()
+            lax.fori_loop(0, feed_tiles, close, 0)
+            grad_rows[...] = total[...].astype(BF16)
+            output_copy = pltpu.make_async_copy(grad_rows, output, out_sem.at[1])
+            output_copy.start()
+            if 6 in early:
+                gather_terms(6)
         loads[name].wait()
 
         def add_normed(t, carry):
@@ -944,12 +1209,14 @@
             return carry
 
         lax.fori_loop(0, features // tile, add_normed, 0)
+        if which == 1 and 4 in early:
+            gather_terms(4)
 
     loads["hidden"].wait()
 
     def attention_norm(at, carry):
         rows = block_rows(at)
-        here = hidden[rows, :].astype(F32)
+        here = cot_v[rows, :].astype(F32)
         grads = total[rows, :]
         scaling = rms_scaling(here)
         weighted = gain_rows[0:1, :] * grads
@@ -960,7 +1227,7 @@
     gain = lax.fori_loop(0, blocks, attention_norm, jnp.zeros((8, features), F32))
     gain = jnp.sum(gain, 0, keepdims=True)
 
-    first_lags = lags[0:8, :]
+    first_lags = lag_of(delays, 0)
     once = jnp.where(first_lags == 1, branch[0:8, :], 0.0)
     once = jnp.where(
         lax.broadcasted_iota(jnp.int32, once.shape, 0) == 0, 0.0, pltpu.roll(once, 1, 0)
@@ -984,6 +1251,9 @@
         gain_copies.append(copy)
     gain_in[pl.ds(fr, 1)] = gain_split[pl.ds(fr, 1)]
     settle()
+    for at in early:
+        if at not in (6, 4):
+            gather_terms(at)
 
     rim_copy.wait()
     rim = jnp.where(fr == n_fr - 1, 0.0, rim_in[...])
@@ -992,7 +1262,7 @@
         after_one, after_two = carry
         rows = block_rows(blocks - 1 - at)
         grads = branch[rows, :]
-        lag = lags[rows, :]
+        lag = lag_of(delays, blocks - 1 - at)
         one = jnp.where(lag == 1, grads, 0.0)
         two = jnp.where(lag == 2, grads, 0.0)
         moved = pltpu.roll(jnp.concatenate([one, after_one], 0), block + 7, 0)[:block]
@@ -1013,15 +1283,15 @@
     for at in range(7):
         pltpu.make_async_copy(kept_out[at], kept_out[at], kept_sem.at[at]).wait()
         for k in range(1, chips):
-            there = lax.rem(chip + k, chips)
-            send(
-                come_out[at].at[k - 1],
-                come_out[at].at[k - 1],
-                far_send.at[at, k],
-                far_recv.at[at, k],
-                fr=there * 2 + core,
-            ).wait()
+            arrivals(at, k).wait_send()
+            if at in come_out:
+                arrivals(at, k).wait_recv()
+    for copy in late_far.values():
+        copy.wait_send()
+    for copy in late_near.values():
+        copy.wait_send()
     out_copy.wait()
+    output_copy.wait()
 
 
 def backward_call(n_fr, n_pos, shard_shapes, *operands):
@@ -1033,21 +1303,26 @@
     count = len(shard_shapes)
     shard_rows = [rows for rows, _ in shard_shapes]
     hidden_units = operands[4].shape[1]
+    act = jax.ShapeDtypeStruct((frames, features), BF16)
     most = max(shard_rows)
+    down = operands[-2]
+    late_count = max(1, down_pieces(shard_rows[-1]) * LATE // 100)
+    early, late = split_terms(chips, n_pos * frames, shard_shapes)
+    come_shapes = [(chips - 1, *shape) for shape in shard_shapes]
     return pl.pallas_call(
-        functools.partial(backward_kernel, n_fr, n_pos, shard_rows),
+        functools.partial(backward_kernel, n_fr, n_pos, shard_rows, early, late),
         name="backward",
         out_shape=[jax.ShapeDtypeStruct(shape, BF16) for shape in shard_shapes]
-        + [jax.ShapeDtypeStruct((chips - 1, *shape), BF16) for shape in shard_shapes]
-        + [
-            jax.ShapeDtypeStruct((frames, features), BF16),
-            jax.ShapeDtypeStruct((8, features // n_fr), F32),
-        ],
+        + [jax.ShapeDtypeStruct(come_shapes[at], BF16) for at in late]
+        + [act, act, jax.ShapeDtypeStruct(down.shape, BF16)]
+        + [jax.ShapeDtypeStruct((8, features // n_fr), F32)],
         in_specs=[VMEM, VMEM] + [ANY] * (len(operands) - 2),
-        out_specs=[ANY] * (2 * count + 1) + [VMEM],
+        out_specs=[ANY] * (count + len(late) + 3) + [VMEM],
+        input_output_aliases={len(operands) - 2: count + len(late) + 2},
         scratch_shapes=[
             pltpu.VMEM((columns // tile, chips, rows, tile), BF16) for rows, columns in shard_shapes
         ]
+        + [pltpu.VMEM(come_shapes[at], BF16) for at in early]
         + [
             pltpu.VMEM((2, 2, chips, most, tile), BF16),
             pltpu.VMEM((2, tile, features), BF16),
@@ -1060,9 +1335,7 @@
             pltpu.VMEM((frames, hidden_units), BF16),
             pltpu.VMEM((features, frames), BF16),
             pltpu.VMEM((features, frames), BF16),
-            pltpu.VMEM((features, frames), BF16),
             pltpu.VMEM((frames, features), F32),
-            pltpu.VMEM((frames, features), BF16),
             pltpu.VMEM((frames, features), F32),
             pltpu.VMEM((frames, features), BF16),
             pltpu.VMEM((frames, features), BF16),
@@ -1079,12 +1352,12 @@
             pltpu.VMEM((n_fr, 8, features // n_fr), F32),
             pltpu.VMEM((8, features), F32),
             pltpu.VMEM((8, features), F32),
-            DMA((17,)),
+            DMA((19,)),
             DMA((2, 3)),
             DMA((2,)),
-            DMA((count, max(columns for _, columns in shard_shapes) // tile)),
-            DMA((count, chips)),
-            DMA((count, chips)),
+            DMA((sum(columns // tile for _, columns in shard_shapes),)),
+            DMA((count * (chips - 1),)),
+            DMA((count * (chips - 1),)),
             DMA((count,)),
             DMA((n_pos,)),
             DMA((n_pos,)),
@@ -1093,12 +1366,113 @@
             DMA((n_fr,)),
             DMA((n_fr,)),
             DMA((2,)),
-            DMA((1,)),
+            DMA((2,)),
+            DMA((late_count * (chips - 1),)),
+            DMA((late_count * (chips - 1),)),
+            DMA((late_count * (chips - 1),)),
+            DMA((late_count * (chips - 1),)),
         ],
         compiler_params=pltpu.CompilerParams(
             collective_id=1, has_side_effects=True, vmem_limit_bytes=VMEM_BYTES
         ),
     )(*operands)
+
+
+def finish_kernel(count, late, *refs):
+    kept, refs = refs[:count], refs[count:]
+    come, refs = dict(zip(late, refs)), refs[len(late) :]
+    output_in, input_grad_in, gains, *refs = refs
+    sums, refs = refs[:count], refs[count:]
+    output, input_grad, gain_one, gain_two, *refs = refs
+    kept_v, refs = refs[:count], refs[count:]
+    come_v, refs = dict(zip(late, refs)), refs[len(late) :]
+    sums_v, refs = refs[:count], refs[count:]
+    through, load_sem, store_sem, through_sem = refs
+    chunks = []
+    for at in range(count):
+        rows, columns = kept[at].shape
+        cuts = next(
+            cuts
+            for cuts in (4, 2, 1)
+            if rows % (16 * cuts) == 0 and (cuts == 1 or rows * columns >= cuts * 131072)
+        )
+        size = rows // cuts
+        chunks += [(at, pl.ds(piece * size, size), piece) for piece in range(cuts)]
+
+    order = {(at, piece): i for i, (at, _, piece) in enumerate(chunks)}
+
+    def loads(at, rows, piece):
+        copies = [
+            pltpu.make_async_copy(kept[at].at[rows], kept_v[at].at[rows], load_sem.at[order[at, piece]])
+        ]
+        if at in come:
+            copies.append(
+                pltpu.make_async_copy(
+                    come[at].at[:, rows], come_v[at].at[:, rows], load_sem.at[len(order) + order[at, piece]]
+                )
+            )
+        return copies
+
+    for chunk in chunks:
+        for copy in loads(*chunk):
+            copy.start()
+    acts = [
+        pltpu.make_async_copy(output_in, through.at[0], through_sem.at[0]),
+        pltpu.make_async_copy(input_grad_in, through.at[1], through_sem.at[1]),
+    ]
+    for copy in acts:
+        copy.start()
+    gain_one[...] = gains[0:1, :]
+    gain_two[...] = gains[1:2, :]
+    stores = []
+    for at, rows, piece in chunks:
+        for copy in loads(at, rows, piece):
+            copy.wait()
+        step = 16
+
+        def add(i, carry):
+            here = pl.ds(pl.multiple_of(rows.start + i * step, step), step)
+            value = kept_v[at][here, :].astype(F32)
+            for k in range(come_v[at].shape[0] if at in come else 0):
+                value = value + come_v[at][k, here, :].astype(F32)
+            sums_v[at][here, :] = value
+            return carry
+
+        lax.fori_loop(0, rows.size // step, add, 0)
+        stores.append(
+            pltpu.make_async_copy(sums_v[at].at[rows], sums[at].at[rows], store_sem.at[order[at, piece]])
+        )
+        stores[-1].start()
+    for copy, leaving, slot in zip(acts, (output, input_grad), range(2)):
+        copy.wait()
+        stores.append(pltpu.make_async_copy(through.at[slot], leaving, through_sem.at[2 + slot]))
+        stores[-1].start()
+    for copy in stores:
+        copy.wait()
+
+
+def finish_call(late, kept, come, output, input_grad, gains):
+    count = len(kept)
+    gain = jax.ShapeDtypeStruct((1, gains.shape[1]), F32)
+    return pl.pallas_call(
+        functools.partial(finish_kernel, count, late),
+        name="finish",
+        out_shape=[jax.ShapeDtypeStruct(own.shape, F32) for own in kept]
+        + [jax.ShapeDtypeStruct(output.shape, BF16)] * 2
+        + [gain, gain],
+        in_specs=[ANY] * (count + len(come) + 2) + [VMEM],
+        out_specs=[ANY] * (count + 2) + [VMEM, VMEM],
+        scratch_shapes=[pltpu.VMEM(own.shape, BF16) for own in kept]
+        + [pltpu.VMEM(others.shape, BF16) for others in come]
+        + [pltpu.VMEM(own.shape, F32) for own in kept]
+        + [
+            pltpu.VMEM((2, *output.shape), BF16),
+            DMA((2 * 3 * count,)),
+            DMA((3 * count,)),
+            DMA((4,)),
+        ],
+        compiler_params=pltpu.CompilerParams(vmem_limit_bytes=VMEM_BYTES),
+    )(*kept, *come, output, input_grad, gains)
 
 
 def on_device(
@@ -1117,10 +1491,6 @@
 ):
     n_fr = lax.axis_size("fr")
     n_pos = lax.axis_size("pos")
-    own_rows = inputs[0]
-    frames, features = own_rows.shape
-    lags = jnp.repeat(delays[:, 0], frames // delays.shape[0])[:, None]
-    gains = jnp.pad(jnp.concatenate([attention_gain, feed_gain], 0).astype(F32), ((0, 6), (0, 0)))
     shards = [
         weight[0]
         for weight in (
@@ -1133,30 +1503,36 @@
             down_weight,
         )
     ]
-    results = forward_call(n_fr, n_pos, own_rows, lags, gains, shards)
-    full, output, saved, gain_rows = results[:7], results[7], results[8:20], results[20]
+    delays = delays.T
+    results = forward_call(n_fr, n_pos, inputs[0], delays, attention_gain, feed_gain, shards)
+    full, saved, gain_rows = results[:7], results[7:20], results[20]
     inner_t, *saved = saved
     grads = backward_call(
         n_fr,
         n_pos,
         [shard.shape for shard in shards],
-        lags,
+        delays,
         gain_rows,
         inner_t,
         cotangent[0],
         *saved,
         *full,
+        shards[-1],
     )
-    kept, come, (input_grad, gain_grads) = grads[:7], grads[7:14], grads[14:]
+    late = split_terms(
+        n_fr // 2, n_pos * inputs.shape[1], [shard.shape for shard in shards]
+    )[1]
+    kept, come = grads[:7], grads[7 : 7 + len(late)]
+    output, input_grad, _, gain_grads = grads[7 + len(late) :]
+    *sums, output, input_grad, attention_gain_grad, feed_gain_grad = finish_call(
+        late, kept, come, output, input_grad, gain_grads
+    )
     return (
         output[None],
         input_grad[None],
-        *(
-            (own.astype(F32) + jnp.sum(others.astype(F32), 0))[None]
-            for own, others in zip(kept, come)
-        ),
-        gain_grads[0:1],
-        gain_grads[1:2],
+        *(total[None] for total in sums),
+        attention_gain_grad,
+        feed_gain_grad,
     )
 
 

time: 328 us -> 309 us (0.942)
  other arithmetic: 11.6 us -> 0 us
  local copies, waits for them, and re-layouts: 7.93 us -> 0 us
    broadcast_in_dim x4 -> x0, other arithmetic: 10.3 us -> none  [on_device(): (own.astype(F32) + jnp.sum(others.astype(F32), 0))[None]]
    pallas_call x1 -> x2, Pallas kernels: 156 us -> 151 us  [the longest x1 140 us: forward_call(): pl.pallas_call(functools.partial(forward_kernel, n_fr, n_pos, pieces, lat...]
    pallas_call x1, Pallas kernels: 151 us -> 157 us  [backward_call(): pl.pallas_call(functools.partial(backward_kernel, n_fr, n_pos, shard_rows...]
    unnamed x26 -> x0, local copies, waits for them, and re-layouts: 4.96 us -> none
where the time goes in v4:
time: 309 us; the launch traced here: 308 us
  Pallas kernels  308 us (100%)
    pallas_call x1, Pallas kernels, backward_call(): pl.pallas_call(functools.partial(backward_kernel, n_fr, n_pos, shard_rows...  157 us
    pallas_call x1, Pallas kernels, forward_call(): pl.pallas_call(functools.partial(forward_kernel, n_fr, n_pos, pieces, lat...  140 us
    pallas_call x1, Pallas kernels, finish_call(): pl.pallas_call(functools.partial(finish_kernel, count, late), name='finis...  10.6 us

profile of v4, /device:TPU:0, one launch (start us, length us, event | category | flops | bytes accessed | tf_op | source)
XLA Modules:
  0.0 308.3 jit_solution(11454756167035355222)
XLA Ops:
  0.6 139.9 %forward.1 = (bf16[1024,1024]{1,0:T(8,128)(2,1)}, bf16[1024,1024]{1,0:T(8,128)(2,1)}, bf16[1024,1024]{1,0:T(8,128)(2,1)}, bf16[1024,1024]{1,0:T(8,128)(2,1)}, bf...) custom-call(bf16[512,1024]{1,0:T(8,128)(2,1)} %bitcast.24, ...), custom_call_target="tpu_custom_call" | custom-call | tf_op jit(solution)/shard_map/forward/pallas_call | solution.py:642
  140.6 157.2 %backward.1 = (bf16[256,1024]{1,0:T(8,128)(2,1)}, bf16[256,1024]{1,0:T(8,128)(2,1)}, bf16[256,1024]{1,0:T(8,128)(2,1)}, bf16[256,1024]{1,0:T(8,128)(2,1)}, bf16[...) custom-call(s32[1,8]{1,0:T(1,128)} %bitcast.30, ...), custom_call_target="tpu_custom_call", output_to_operand_aliasing={{11}: (22, {})} | custom-call | tf_op jit(solution)/shard_map/backward/pallas_call | solution.py:1312
  297.7 10.6 %finish.1 = (f32[256,1024]{1,0:T(8,128)}, f32[256,1024]{1,0:T(8,128)}, f32[256,1024]{1,0:T(8,128)}, f32[256,1024]{1,0:T(8,128)}, f32[256,2816]{1,0:T(8,128)}, /*...) custom-call(bf16[256,1024]{1,0:T(8,128)(2,1)} %get-tuple-element.76., ...), custom_call_target="tpu_custom_call" | custom-call | tf_op jit(solution)/shard_map/finish/pallas_call | solution.py:1457

commit v5 on v4

--- a/solution.py
+++ b/solution.py
@@ -101,7 +101,7 @@
 
 def forward_kernel(n_fr, n_pos, pieces, late, steps, *refs):
     (
-        own_rows,
+        rows_in,
         delays,
         gain_one,
         gain_two,
@@ -140,6 +140,7 @@
         f4,
         f5,
         f6,
+        own_rows,
         rim,
         gains,
         gain_slots,
@@ -191,10 +192,12 @@
     frames, features = own_rows.shape
     part = frames // n_pos
     greet(n_fr, n_pos)
+    own_load = pltpu.make_async_copy(rows_in, own_rows, own_sem.at[len(shards)])
+    own_load.start()
 
     edge = own_rows.shape[0] - rim.shape[0]
     rim_copy = send(
-        own_rows.at[pl.ds(edge, rim.shape[0])],
+        rows_in.at[pl.ds(edge, rim.shape[0])],
         rim,
         rim_sem.at[0],
         rim_sem.at[1],
@@ -244,7 +247,7 @@
             far[0, k, t] = send(
                 w0.at[:, columns_of(t)],
                 f0.at[rows_of(fr, w0.shape[0]), columns_of(t)],
-                far_send.at[slot(0, k, t)],
+                far_send.at[0],
                 far_recv.at[slot(0, k, t)],
                 fr=lax.rem(chip + k, chips) * 2 + core,
             )
@@ -255,7 +258,7 @@
         return send(
             w5.at[:, columns_of(t)],
             f5.at[rows_of(fr, w5.shape[0]), columns_of(t)],
-            far_send.at[slot(5, k, t)],
+            far_send.at[5],
             far_recv.at[slot(5, k, t)],
             fr=lax.rem(chip + k, chips) * 2 + core,
         )
@@ -264,7 +267,7 @@
         there = f5.at[
             rows_of(lax.rem(chip - k + chips, chips) * 2 + core, w5.shape[0]), columns_of(t)
         ]
-        return send(there, there, near_send.at[slot(5, k, t)], near_recv.at[slot(5, k, t)], fr=partner)
+        return send(there, there, near_send.at[5], near_recv.at[slot(5, k, t)], fr=partner)
 
     def up_start(t, carry):
         for k in range(1, chips):
@@ -281,13 +284,13 @@
                 far[at, k, piece] = send(
                     shard.at[piece * size : (piece + 1) * size],
                     whole.at[piece_rows(at, fr, piece)],
-                    far_send.at[slot(at, k, piece)],
+                    far_send.at[at],
                     far_recv.at[slot(at, k, piece)],
                     fr=lax.rem(chip + k, chips) * 2 + core,
                 )
                 far[at, k, piece].start()
         near[at, 0, 0] = send(
-            shard, whole.at[mine], near_send.at[spare + at], near_recv.at[spare + at], fr=partner
+            shard, whole.at[mine], near_send.at[at], near_recv.at[spare + at], fr=partner
         )
         if at < 3:
             near[at, 0, 0].start()
@@ -302,6 +305,7 @@
     gain_row = jnp.concatenate([gain_slots[at, 0:1, :] for at in range(n_fr)], 1)
     gains_out[...] = jnp.concatenate([gain_slots[at] for at in range(n_fr)], 1)
     rim_copy.wait()
+    own_load.wait()
 
     block = frames // delays.shape[1]
     rim_rows = rim.shape[0]
@@ -339,7 +343,7 @@
             near[at, k, piece] = send(
                 full[at].at[rows],
                 full[at].at[rows],
-                near_send.at[slot(at, k, piece)],
+                near_send.at[at],
                 near_recv.at[slot(at, k, piece)],
                 fr=partner,
             )
@@ -382,8 +386,8 @@
         return send(
             proj.at[which, rows_of(peer, part)],
             turned.at[which, pos],
-            turn_send.at[which, k],
-            turn_recv.at[which, k],
+            turn_send.at[which],
+            turn_recv.at[which],
             pos=peer,
         )
 
@@ -395,7 +399,7 @@
             origin = lax.rem(chip - k + chips, chips) * 2 + core
             there = f0.at[rows_of(origin, w0.shape[0]), columns_of(t)]
             near[0, k, t] = send(
-                there, there, near_send.at[slot(0, k, t)], near_recv.at[slot(0, k, t)], fr=partner
+                there, there, near_send.at[0], near_recv.at[slot(0, k, t)], fr=partner
             )
             near[0, k, t].start()
         for k in range(1, chips):
@@ -407,8 +411,8 @@
             send(
                 proj.at[0, rows_of(peer, part), columns_of(t)],
                 turned.at[0, pos, :, columns_of(t)],
-                turn_send.at[0, k],
-                turn_recv.at[0, k],
+                turn_send.at[0],
+                turn_recv.at[0],
                 pos=peer,
             ).start()
             return carry
@@ -447,11 +451,14 @@
     pass_on(3)
 
     def end_turns(which):
-        def end_turn(k, carry):
-            turn(which, k).wait()
-            return carry
-
-        lax.fori_loop(1, n_pos, end_turn, 0)
+        landed = turned.at[which, 0 : n_pos - 1]
+        send(
+            landed,
+            landed,
+            turn_send.at[which],
+            turn_recv.at[which],
+            pos=peer_of(pos, 1, n_pos),
+        ).wait()
         put(turned.at[which], turned_out[which])
 
     end_turns(0)
@@ -488,8 +495,8 @@
         return send(
             mixed.at[p],
             attended.at[rows_of(pos, part)],
-            back_send.at[p],
-            back_recv.at[pos],
+            back_send.at[0],
+            back_recv.at[0],
             pos=p,
         )
 
@@ -520,18 +527,10 @@
     complete(3)
     complete(4)
 
-    def end_back(k, carry):
-        peer = peer_of(pos, k, n_pos)
-        send(
-            mixed.at[peer],
-            attended.at[rows_of(peer, part)],
-            back_send.at[peer],
-            back_recv.at[peer],
-            pos=peer,
-        ).wait()
-        return carry
-
-    lax.fori_loop(1, n_pos, end_back, 0)
+    landed = mixed.at[0 : n_pos - 1]
+    send(
+        landed, landed, back_send.at[0], back_recv.at[0], pos=peer_of(pos, 1, n_pos)
+    ).wait()
     def leave(t, carry):
         columns = columns_of(t)
         branch[:, columns] = hidden[:, columns].astype(F32) + product(
@@ -595,19 +594,14 @@
     put(inner_t, inner_out)
     put(inner, inner_rows_out)
     finish_pieces(6)
-
-    def up_sent(t, carry):
-        for k in range(1, chips):
-            up_far(t, k).wait_send()
-            up_near(t, k).wait_send()
-        return carry
-
-    lax.fori_loop(0, up_tiles, up_sent, 0)
     pltpu.make_async_copy(o5, o5, out_sem.at[5]).wait()
-    for copy in far.values():
-        copy.wait_send()
-    for copy in near.values():
-        copy.wait_send()
+    for at in range(len(shards)):
+        rows = shards[at].shape[0]
+        early = (chips - 1) * (rows - late[at] * (rows // pieces[at]))
+        gone = full[at].at[0:early]
+        send(gone, gone, far_send.at[at], near_recv.at[0], fr=partner).wait_send()
+        gone = full[at].at[0 : early + rows]
+        send(gone, gone, near_send.at[at], near_recv.at[0], fr=partner).wait_send()
     for copy in outs.values():
         copy.wait()
     for copy in act_copies:
@@ -649,10 +643,11 @@
             jax.ShapeDtypeStruct((n_pos, n_pos, part, LANES), F32),
             jax.ShapeDtypeStruct((8, features), F32),
         ],
-        in_specs=[VMEM] * 4 + [ANY] * count,
+        in_specs=[ANY] + [VMEM] * 3 + [ANY] * count,
         out_specs=[ANY] * (count + 13) + [VMEM],
         scratch_shapes=[pltpu.VMEM(shape, BF16) for shape in full]
         + [
+            pltpu.VMEM((frames, features), BF16),
             pltpu.VMEM((16, features), BF16),
             pltpu.VMEM((8, width), F32),
             pltpu.VMEM((n_fr, 8, width), F32),
@@ -676,19 +671,19 @@
             pltpu.VMEM((part, features), F32),
             pltpu.VMEM((features, LANES), BF16),
             pltpu.VMEM((LANES, features), BF16),
+            DMA((count,)),
             DMA((copies,)),
-            DMA((copies,)),
+            DMA((count,)),
             DMA((copies + count,)),
-            DMA((copies + count,)),
-            DMA((count,)),
+            DMA((count + 1,)),
             DMA((count,)),
             DMA((2,)),
             DMA((n_fr,)),
             DMA((n_fr,)),
-            DMA((3, n_pos)),
-            DMA((3, n_pos)),
-            DMA((n_pos,)),
-            DMA((n_pos,)),
+            DMA((3,)),
+            DMA((3,)),
+            DMA((1,)),
+            DMA((1,)),
             DMA((14,)),
         ],
         compiler_params=pltpu.CompilerParams(
@@ -902,11 +897,11 @@
 
         lax.fori_loop(0, held[at].shape[0], add, 0)
 
-    def reduce_weight(at, left_t, right):
+    def reduce_weight(at, left_t, right, first=0, last=None):
         rows = shard_rows[at]
-        tiles = right.shape[1] // tile
-        base = done[0]
-        done[0] += tiles
+        last = last or right.shape[1] // tile
+        base = done[0] + first
+        done[0] += last - first
         group = max(1, 1024 // rows)
 
         def outgoing(t):
@@ -941,32 +936,32 @@
         def step(t, carry):
             slot = lax.rem(t + base, 2)
 
-            @pl.when(t >= 2)
+            @pl.when(t >= first + 2)
             def _():
                 outgoing(t - 2).wait_send()
 
-            for first in range(0, n_fr, group):
-                last = min(first + group, n_fr)
-                grads = product(left_t[first * rows : last * rows], right[:, columns_of(t)])
-                for b in range(first, last):
+            for low in range(0, n_fr, group):
+                high = min(low + group, n_fr)
+                grads = product(left_t[low * rows : high * rows], right[:, columns_of(t)])
+                for b in range(low, high):
                     made[slot, b % 2, b // 2, 0:rows] = grads[
-                        (b - first) * rows : (b - first + 1) * rows
+                        (b - low) * rows : (b - low + 1) * rows
                     ].astype(BF16)
             outgoing(t).start()
 
-            @pl.when(t >= 1)
+            @pl.when(t >= first + 1)
             def _():
                 consume(t - 1)
 
             return carry
 
         settle()
-        lax.fori_loop(0, tiles, step, 0)
+        lax.fori_loop(first, last, step, 0)
 
         def finish():
-            consume(tiles - 1)
-            outgoing(tiles - 2).wait_send()
-            outgoing(tiles - 1).wait_send()
+            consume(last - 1)
+            outgoing(last - 2).wait_send()
+            outgoing(last - 1).wait_send()
 
         pending.append(finish)
 
@@ -1060,8 +1055,8 @@
         return send(
             grad_rows.at[rows_of(peer, part)],
             turned.at[3, pos],
-            turn_send.at[k],
-            turn_recv.at[k],
+            turn_send.at[0],
+            turn_recv.at[0],
             pos=peer,
         )
 
@@ -1086,43 +1081,46 @@
     for name in ("queries", "keys", "values", "soft"):
         loads[name].wait()
 
-    def end_turn(k, carry):
-        turn(k).wait()
-        return carry
-
-    lax.fori_loop(1, n_pos, end_turn, 0)
+    landed = turned.at[3, 0 : n_pos - 1]
+    send(
+        landed, landed, turn_send.at[0], turn_recv.at[0], pos=peer_of(pos, 1, n_pos)
+    ).wait()
     settle()
 
-    def give_back(which, j):
-        return send(
-            leaving.at[which, j],
-            arrived.at[which, rows_of(pos, part)],
-            back_send.at[which, j],
-            back_recv.at[which, pos],
-            pos=j,
-        )
-
-    def part_sum(which, j, low, high, weight_of, other, scale):
-        sum_rows[...] = jnp.zeros_like(sum_rows)
+    half = features // 2
+    every = slice(0, features)
+    groups = ((2, every), (1, every), (0, slice(0, half)), (0, slice(half, features)))
+
+    def part_sum(group, j, low, high, weight_of, other, scale):
+        which, columns = groups[group]
+        sum_rows[:, columns] = jnp.zeros_like(sum_rows[:, columns])
 
         def add(at, carry):
-            sum_rows[...] += product(weight_of(at), spread[...]) * turned[other, at].astype(F32)
+            sum_rows[:, columns] += product(weight_of(at), spread[:, columns]) * turned[
+                other, at, :, columns
+            ].astype(F32)
             return carry
 
         lax.fori_loop(low, high, add, 0)
-        leaving[which, j] = (sum_rows[...] * scale).astype(BF16)
+        leaving[which, j, :, columns] = (sum_rows[:, columns] * scale).astype(BF16)
 
         @pl.when(j != pos)
         def _():
-            give_back(which, j).start()
+            send(
+                leaving.at[which, j, :, columns],
+                arrived.at[which, rows_of(pos, part), columns],
+                back_send.at[group],
+                back_recv.at[group],
+                pos=j,
+            ).start()
 
         @pl.when(j == pos)
         def _():
-            arrived[which, rows_of(pos, part), :] = leaving[which, j]
+            arrived[which, rows_of(pos, part), columns] = leaving[which, j, :, columns]
 
     def value_part(k, carry):
         j = peer_of(pos, k, n_pos)
-        part_sum(2, j, j, n_pos, lambda p: soft[p, j].astype(BF16), 3, 1.0)
+        part_sum(0, j, j, n_pos, lambda p: soft[p, j].astype(BF16), 3, 1.0)
         return carry
 
     lax.fori_loop(1, n_pos + 1, value_part, 0)
@@ -1152,12 +1150,14 @@
 
     lax.fori_loop(1, n_pos + 1, key_part, 0)
 
-    def query_part(k, carry):
-        p = peer_of(pos, k, n_pos)
-        part_sum(0, p, 0, p + 1, lambda j: soft_grads[p, j], 1, HEAD ** (-0.5))
-        return carry
-
-    lax.fori_loop(1, n_pos + 1, query_part, 0)
+    for group in (2, 3):
+
+        def query_part(k, carry):
+            p = peer_of(pos, k, n_pos)
+            part_sum(group, p, 0, p + 1, lambda j: soft_grads[p, j], 1, HEAD ** (-0.5))
+            return carry
+
+        lax.fori_loop(1, n_pos + 1, query_part, 0)
 
     def down_copy(t):
         return feed_copies(t)[0]
@@ -1175,21 +1175,15 @@
         return carry
 
     loads["normed"].wait()
-    for which, slot, name in ((2, 1, "value_w"), (1, 2, "key_w"), (0, 0, "query_w")):
-
-        def end_back(k, carry):
-            peer = peer_of(pos, k, n_pos)
-            send(
-                leaving.at[which, peer],
-                arrived.at[which, rows_of(peer, part)],
-                back_send.at[which, peer],
-                back_recv.at[which, peer],
-                pos=peer,
-            ).wait()
-            return carry
-
-        lax.fori_loop(1, n_pos, end_back, 0)
-        reduce_weight(which, normed_two_v, arrived.at[which])
+    for group, slot, name in ((0, 1, "value_w"), (1, 2, "key_w"), (2, 0, "query_w"), (3, 0, None)):
+        which, across = groups[group]
+        landed = arrived.at[which, 0 : (n_pos - 1) * part, across]
+        send(
+            landed, landed, back_send.at[group], back_recv.at[group], pos=peer_of(pos, 1, n_pos)
+        ).wait()
+        reduce_weight(
+            which, normed_two_v, arrived.at[which], across.start // tile, across.stop // tile
+        )
         if which == 2:
             loads["inner_rows"].wait()
             loads["branch_again"].wait()
@@ -1200,12 +1194,13 @@
             output_copy.start()
             if 6 in early:
                 gather_terms(6)
-        loads[name].wait()
+        if name:
+            loads[name].wait()
 
         def add_normed(t, carry):
             columns = columns_of(t)
-            grads = back_product(arrived[which], small[slot, columns, :])
-            total[:, columns] = grads if which == 2 else total[:, columns] + grads
+            grads = back_product(arrived[which, :, across], small[slot, columns, across])
+            total[:, columns] = grads if group == 0 else total[:, columns] + grads
             return carry
 
         lax.fori_loop(0, features // tile, add_normed, 0)
@@ -1359,10 +1354,10 @@
             DMA((count * (chips - 1),)),
             DMA((count * (chips - 1),)),
             DMA((count,)),
-            DMA((n_pos,)),
-            DMA((n_pos,)),
-            DMA((3, n_pos)),
-            DMA((3, n_pos)),
+            DMA((1,)),
+            DMA((1,)),
+            DMA((4,)),
+            DMA((4,)),
             DMA((n_fr,)),
             DMA((n_fr,)),
             DMA((2,)),
@@ -1413,18 +1408,22 @@
             )
         return copies
 
-    for chunk in chunks:
-        for copy in loads(*chunk):
-            copy.start()
     acts = [
         pltpu.make_async_copy(output_in, through.at[0], through_sem.at[0]),
         pltpu.make_async_copy(input_grad_in, through.at[1], through_sem.at[1]),
     ]
     for copy in acts:
         copy.start()
+    for chunk in chunks:
+        for copy in loads(*chunk):
+            copy.start()
     gain_one[...] = gains[0:1, :]
     gain_two[...] = gains[1:2, :]
     stores = []
+    for copy, leaving, slot in zip(acts, (output, input_grad), range(2)):
+        copy.wait()
+        stores.append(pltpu.make_async_copy(through.at[slot], leaving, through_sem.at[2 + slot]))
+        stores[-1].start()
     for at, rows, piece in chunks:
         for copy in loads(at, rows, piece):
             copy.wait()
@@ -1442,10 +1441,6 @@
         stores.append(
             pltpu.make_async_copy(sums_v[at].at[rows], sums[at].at[rows], store_sem.at[order[at, piece]])
         )
-        stores[-1].start()
-    for copy, leaving, slot in zip(acts, (output, input_grad), range(2)):
-        copy.wait()
-        stores.append(pltpu.make_async_copy(through.at[slot], leaving, through_sem.at[2 + slot]))
         stores[-1].start()
     for copy in stores:
         copy.wait()

time: 309 us -> 307 us (level)
  no operation moved by 1% of the time
where the time goes in v5:
time: 307 us
  Pallas kernels  306 us (100%)
    pallas_call x1, Pallas kernels, backward_call(): pl.pallas_call(functools.partial(backward_kernel, n_fr, n_pos, shard_rows...  157 us
    pallas_call x1, Pallas kernels, forward_call(): pl.pallas_call(functools.partial(forward_kernel, n_fr, n_pos, pieces, lat...  139 us
    pallas_call x1, Pallas kernels, finish_call(): pl.pallas_call(functools.partial(finish_kernel, count, late), name='finis...  10.4 us

profile of v5, /device:TPU:0, one launch (start us, length us, event | category | flops | bytes accessed | tf_op | source)
XLA Modules:
  0.0 306.6 jit_solution(3556368038943613548)
XLA Ops:
  0.6 138.8 %forward.1 = (bf16[1024,1024]{1,0:T(8,128)(2,1)}, bf16[1024,1024]{1,0:T(8,128)(2,1)}, bf16[1024,1024]{1,0:T(8,128)(2,1)}, bf16[1024,1024]{1,0:T(8,128)(2,1)}, bf...) custom-call(bf16[512,1024]{1,0:T(8,128)(2,1)} %bitcast.24, ...), custom_call_target="tpu_custom_call" | custom-call | tf_op jit(solution)/shard_map/forward/pallas_call | solution.py:636
  139.5 156.6 %backward.1 = (bf16[256,1024]{1,0:T(8,128)(2,1)}, bf16[256,1024]{1,0:T(8,128)(2,1)}, bf16[256,1024]{1,0:T(8,128)(2,1)}, bf16[256,1024]{1,0:T(8,128)(2,1)}, bf16[...) custom-call(s32[1,8]{1,0:T(1,128)} %bitcast.30, ...), custom_call_target="tpu_custom_call", output_to_operand_aliasing={{11}: (22, {})} | custom-call | tf_op jit(solution)/shard_map/backward/pallas_call | solution.py:1307
  296.1 10.4 %finish.1 = (f32[256,1024]{1,0:T(8,128)}, f32[256,1024]{1,0:T(8,128)}, f32[256,1024]{1,0:T(8,128)}, f32[256,1024]{1,0:T(8,128)}, f32[256,2816]{1,0:T(8,128)}, /*...) custom-call(bf16[256,1024]{1,0:T(8,128)(2,1)} %get-tuple-element.76., ...), custom_call_target="tpu_custom_call" | custom-call | tf_op jit(solution)/shard_map/finish/pallas_call | solution.py:1452

commit v6 on v5

--- a/solution.py
+++ b/solution.py
@@ -102,9 +102,9 @@
 def forward_kernel(n_fr, n_pos, pieces, late, steps, *refs):
     (
         rows_in,
-        delays,
-        gain_one,
-        gain_two,
+        delays_in,
+        gain_one_in,
+        gain_two_in,
         w0,
         w1,
         w2,
@@ -132,7 +132,7 @@
         keys_out,
         values_out,
         soft_out,
-        gains_out,
+        gains_sent,
         f0,
         f1,
         f2,
@@ -178,6 +178,11 @@
         back_send,
         back_recv,
         act_sem,
+        delays,
+        gain_one,
+        gain_two,
+        gains_out,
+        small_sem,
     ) = refs
     shards = (w0, w1, w2, w3, w4, w5, w6)
     full_out = (o0, o1, o2, o3, o4, o5, o6)
@@ -191,6 +196,13 @@
     partner = chip * 2 + 1 - core
     frames, features = own_rows.shape
     part = frames // n_pos
+    smalls = [
+        pltpu.make_async_copy(delays_in, delays, small_sem.at[0]),
+        pltpu.make_async_copy(gain_one_in, gain_one, small_sem.at[1]),
+        pltpu.make_async_copy(gain_two_in, gain_two, small_sem.at[2]),
+    ]
+    for copy in smalls:
+        copy.start()
     greet(n_fr, n_pos)
     own_load = pltpu.make_async_copy(rows_in, own_rows, own_sem.at[len(shards)])
     own_load.start()
@@ -204,6 +216,8 @@
         fr=lax.rem(fr + 1, n_fr),
     )
     rim_copy.start()
+    for copy in smalls:
+        copy.wait()
     gains[...] = jnp.concatenate(
         [
             gain_one[...].astype(F32),
@@ -332,6 +346,7 @@
         act_copies[-1].start()
 
     put(hidden, hidden_out)
+    put(gains_out, gains_sent)
 
     outs = {}
 
@@ -643,8 +658,8 @@
             jax.ShapeDtypeStruct((n_pos, n_pos, part, LANES), F32),
             jax.ShapeDtypeStruct((8, features), F32),
         ],
-        in_specs=[ANY] + [VMEM] * 3 + [ANY] * count,
-        out_specs=[ANY] * (count + 13) + [VMEM],
+        in_specs=[ANY] * (count + 4),
+        out_specs=[ANY] * (count + 14),
         scratch_shapes=[pltpu.VMEM(shape, BF16) for shape in full]
         + [
             pltpu.VMEM((frames, features), BF16),
@@ -684,7 +699,12 @@
             DMA((3,)),
             DMA((1,)),
             DMA((1,)),
-            DMA((14,)),
+            DMA((15,)),
+            pltpu.VMEM(delays.shape, jnp.int32),
+            pltpu.VMEM(gain_one.shape, BF16),
+            pltpu.VMEM(gain_two.shape, BF16),
+            pltpu.VMEM((8, features), F32),
+            DMA((3,)),
         ],
         compiler_params=pltpu.CompilerParams(
             collective_id=0, has_side_effects=True, vmem_limit_bytes=VMEM_BYTES
@@ -714,8 +734,8 @@
 
 def backward_kernel(n_fr, n_pos, shard_rows, early, late, *refs):
     (
-        delays,
-        gain_rows,
+        delays_in,
+        gain_rows_in,
         inner_t,
         cot,
         inner_rows,
@@ -735,7 +755,7 @@
     kept_out = refs[24:31]
     refs = refs[31:]
     come_out, refs = dict(zip(late, refs)), refs[len(late) :]
-    output, input_grad, down_w, gains_out, *refs = refs
+    output, input_grad, down_w, gains_sent, *refs = refs
     held, refs = refs[:7], refs[7:]
     come, refs = dict(zip(early, refs)), refs[len(early) :]
     come.update(come_out)
@@ -787,6 +807,9 @@
         late_far_recv,
         late_near_send,
         late_near_recv,
+        delays,
+        gain_rows,
+        gains_out,
     ) = refs
     query_w, key_w, value_w, out_w, gate_w, up_w, _, down_shard = weights
     fr = lax.axis_index("fr")
@@ -845,6 +868,8 @@
             ),
         )
 
+    load("delays", delays_in, delays)
+    load("gain_rows", gain_rows_in, gain_rows)
     load("inner", inner_t, inner_v)
     load("cot", cot, cot_v)
     load("gate", gate_low, gate_v)
@@ -965,6 +990,8 @@
 
         pending.append(finish)
 
+    loads["delays"].wait()
+    loads["gain_rows"].wait()
     loads["inner"].wait()
     loads["cot"].wait()
     reduce_weight(6, inner_v, cot_v)
@@ -1274,6 +1301,8 @@
     for b in range(1, n_fr):
         gain_sum = gain_sum + gain_in[b]
     gains_out[...] = gain_sum
+    gains_copy = pltpu.make_async_copy(gains_out, gains_sent, out_sem.at[2])
+    gains_copy.start()
 
     for at in range(7):
         pltpu.make_async_copy(kept_out[at], kept_out[at], kept_sem.at[at]).wait()
@@ -1287,6 +1316,7 @@
         copy.wait_send()
     out_copy.wait()
     output_copy.wait()
+    gains_copy.wait()
 
 
 def backward_call(n_fr, n_pos, shard_shapes, *operands):
@@ -1311,8 +1341,8 @@
         + [jax.ShapeDtypeStruct(come_shapes[at], BF16) for at in late]
         + [act, act, jax.ShapeDtypeStruct(down.shape, BF16)]
         + [jax.ShapeDtypeStruct((8, features // n_fr), F32)],
-        in_specs=[VMEM, VMEM] + [ANY] * (len(operands) - 2),
-        out_specs=[ANY] * (count + len(late) + 3) + [VMEM],
+        in_specs=[ANY] * len(operands),
+        out_specs=[ANY] * (count + len(late) + 4),
         input_output_aliases={len(operands) - 2: count + len(late) + 2},
         scratch_shapes=[
             pltpu.VMEM((columns // tile, chips, rows, tile), BF16) for rows, columns in shard_shapes
@@ -1347,7 +1377,7 @@
             pltpu.VMEM((n_fr, 8, features // n_fr), F32),
             pltpu.VMEM((8, features), F32),
             pltpu.VMEM((8, features), F32),
-            DMA((19,)),
+            DMA((21,)),
             DMA((2, 3)),
             DMA((2,)),
             DMA((sum(columns // tile for _, columns in shard_shapes),)),
@@ -1361,11 +1391,14 @@
             DMA((n_fr,)),
             DMA((n_fr,)),
             DMA((2,)),
-            DMA((2,)),
+            DMA((3,)),
             DMA((late_count * (chips - 1),)),
             DMA((late_count * (chips - 1),)),
             DMA((late_count * (chips - 1),)),
             DMA((late_count * (chips - 1),)),
+            pltpu.VMEM(operands[0].shape, jnp.int32),
+            pltpu.VMEM((8, features), F32),
+            pltpu.VMEM((8, features // n_fr), F32),
         ],
         compiler_params=pltpu.CompilerParams(
             collective_id=1, has_side_effects=True, vmem_limit_bytes=VMEM_BYTES
@@ -1382,7 +1415,7 @@
     kept_v, refs = refs[:count], refs[count:]
     come_v, refs = dict(zip(late, refs)), refs[len(late) :]
     sums_v, refs = refs[:count], refs[count:]
-    through, load_sem, store_sem, through_sem = refs
+    through, gains_v, load_sem, store_sem, through_sem = refs
     chunks = []
     for at in range(count):
         rows, columns = kept[at].shape
@@ -1408,6 +1441,8 @@
             )
         return copies
 
+    gains_copy = pltpu.make_async_copy(gains, gains_v, through_sem.at[4])
+    gains_copy.start()
     acts = [
         pltpu.make_async_copy(output_in, through.at[0], through_sem.at[0]),
         pltpu.make_async_copy(input_grad_in, through.at[1], through_sem.at[1]),
@@ -1417,8 +1452,6 @@
     for chunk in chunks:
         for copy in loads(*chunk):
             copy.start()
-    gain_one[...] = gains[0:1, :]
-    gain_two[...] = gains[1:2, :]
     stores = []
     for copy, leaving, slot in zip(acts, (output, input_grad), range(2)):
         copy.wait()
@@ -1442,6 +1475,12 @@
             pltpu.make_async_copy(sums_v[at].at[rows], sums[at].at[rows], store_sem.at[order[at, piece]])
         )
         stores[-1].start()
+    gains_copy.wait()
+    for row, gain in enumerate((gain_one, gain_two)):
+        stores.append(
+            pltpu.make_async_copy(gains_v.at[row : row + 1], gain, through_sem.at[5 + row])
+        )
+        stores[-1].start()
     for copy in stores:
         copy.wait()
 
@@ -1455,16 +1494,17 @@
         out_shape=[jax.ShapeDtypeStruct(own.shape, F32) for own in kept]
         + [jax.ShapeDtypeStruct(output.shape, BF16)] * 2
         + [gain, gain],
-        in_specs=[ANY] * (count + len(come) + 2) + [VMEM],
-        out_specs=[ANY] * (count + 2) + [VMEM, VMEM],
+        in_specs=[ANY] * (count + len(come) + 3),
+        out_specs=[ANY] * (count + 4),
         scratch_shapes=[pltpu.VMEM(own.shape, BF16) for own in kept]
         + [pltpu.VMEM(others.shape, BF16) for others in come]
         + [pltpu.VMEM(own.shape, F32) for own in kept]
         + [
             pltpu.VMEM((2, *output.shape), BF16),
+            pltpu.VMEM(gains.shape, F32),
             DMA((2 * 3 * count,)),
             DMA((3 * count,)),
-            DMA((4,)),
+            DMA((7,)),
         ],
         compiler_params=pltpu.CompilerParams(vmem_limit_bytes=VMEM_BYTES),
     )(*kept, *come, output, input_grad, gains)

time: 307 us -> 303 us (0.987)
  Pallas kernels: 306 us -> 302 us
where the time goes in v6:
time: 303 us
  Pallas kernels  302 us (100%)
    pallas_call x1, Pallas kernels, backward_call(): pl.pallas_call(functools.partial(backward_kernel, n_fr, n_pos, shard_rows...  155 us
    pallas_call x1, Pallas kernels, forward_call(): pl.pallas_call(functools.partial(forward_kernel, n_fr, n_pos, pieces, lat...  138 us
    pallas_call x1, Pallas kernels, finish_call(): pl.pallas_call(functools.partial(finish_kernel, count, late), name='finis...  9.19 us

profile of v6, /device:TPU:0, one launch (start us, length us, event | category | flops | bytes accessed | tf_op | source)
XLA Modules:
  0.0 302.9 jit_solution(3616091074993196003)
XLA Ops:
  0.6 137.6 %forward.1 = (bf16[1024,1024]{1,0:T(8,128)(2,1)}, bf16[1024,1024]{1,0:T(8,128)(2,1)}, bf16[1024,1024]{1,0:T(8,128)(2,1)}, bf16[1024,1024]{1,0:T(8,128)(2,1)}, bf...) custom-call(bf16[512,1024]{1,0:T(8,128)(2,1)} %bitcast.24, ...), custom_call_target="tpu_custom_call" | custom-call | tf_op jit(solution)/shard_map/forward/pallas_call | solution.py:651
  138.2 155.3 %backward.1 = (bf16[256,1024]{1,0:T(8,128)(2,1)}, bf16[256,1024]{1,0:T(8,128)(2,1)}, bf16[256,1024]{1,0:T(8,128)(2,1)}, bf16[256,1024]{1,0:T(8,128)(2,1)}, bf16[...) custom-call(s32[1,8]{1,0:T(1,128)} %bitcast.30, ...), custom_call_target="tpu_custom_call", output_to_operand_aliasing={{11}: (22, {})} | custom-call | tf_op jit(solution)/shard_map/backward/pallas_call | solution.py:1337
  293.5 9.2 %finish.1 = (f32[256,1024]{1,0:T(8,128)}, f32[256,1024]{1,0:T(8,128)}, f32[256,1024]{1,0:T(8,128)}, f32[256,1024]{1,0:T(8,128)}, f32[256,2816]{1,0:T(8,128)}, /*...) custom-call(bf16[256,1024]{1,0:T(8,128)(2,1)} %get-tuple-element.76., ...), custom_call_target="tpu_custom_call" | custom-call | tf_op jit(solution)/shard_map/finish/pallas_call | solution.py:1491
